TPU v7x, 32 devices: a whole 2x2x4 slice. The times are simulated.
32 devices in a mesh: dp: 16 (over z, y, x), tensor: 2 (over core).
Axes of the slice: x: 2, y: 2, z: 4, core: 2. Of those that a mesh axis runs over, the one named last changes fastest.
Arguments:
- tokens: bfloat16 [16384, 1536], P(('dp', 'tensor')), may hold values from -6 to 6
- segment_ids: int32 [16, 1024], P('dp'), may hold values from 0 to 7, never falling along the last dimension, each value on 1 to 512 neighbouring positions
- first_gain: float32 [1536], replicated, may hold values from 0.25 to 1.75
- query_weight: bfloat16 [1536, 1536], P(None, 'tensor'), may hold values from -0.15625 to 0.15625
- key_weight: bfloat16 [1536, 1536], P(None, 'tensor'), may hold values from -0.15625 to 0.15625
- value_weight: bfloat16 [1536, 1536], P(None, 'tensor'), may hold values from -0.15625 to 0.15625
- outgate_weight: bfloat16 [1536, 1536], P(None, 'tensor'), may hold values from -0.15625 to 0.15625
- forget_weight: bfloat16 [1536, 24], P(None, 'tensor'), may hold values from -0.15625 to 0.15625
- forget_bias: float32 [24], P('tensor'), may hold values from 1 to 12
- output_weight: bfloat16 [1536, 1536], P('tensor'), may hold values from -0.875 to 0.875
- second_gain: float32 [1536], replicated, may hold values from 0.25 to 1.75
- gate_weight: bfloat16 [1536, 4096], P(None, 'tensor'), may hold values from -0.15625 to 0.15625
- up_weight: bfloat16 [1536, 4096], P(None, 'tensor'), may hold values from -0.15625 to 0.15625
- down_weight: bfloat16 [4096, 1536], P('tensor'), may hold values from -0.09375 to 0.09375
- cotangent: bfloat16 [16384, 1536], P(('dp', 'tensor')), may hold values from -6 to 6
Outputs:
- result: bfloat16 [16384, 1536], P(('dp', 'tensor'))
- grad_tokens: float32 [16384, 1536], P(('dp', 'tensor'))
- grad_first: float32 [1536], replicated
- grad_query: float32 [1536, 1536], P('dp', 'tensor')
- grad_key: float32 [1536, 1536], P('dp', 'tensor')
- grad_value: float32 [1536, 1536], P('dp', 'tensor')
- grad_outgate: float32 [1536, 1536], P('dp', 'tensor')
- grad_forget: float32 [1536, 24], P('dp', 'tensor')
- grad_bias: float32 [24], replicated
- grad_output: float32 [1536, 1536], P('tensor', 'dp')
- grad_second: float32 [1536], replicated
- grad_gate: float32 [1536, 4096], P('dp', 'tensor')
- grad_up: float32 [1536, 4096], P('dp', 'tensor')
- grad_down: float32 [4096, 1536], P('tensor', 'dp')
Inputs may be any that keep to these rules, and one draw needn't show every extreme that they name: `segment_ids`: ids never fall along a sequence; each document has 1 to 512 tokens and one of each sequence has exactly 512.
All inputs are finite; a program needn't handle non-finite values.
Results may differ from a plain program's by a relative error of at most 0.022.
Values may be sent and summed in bfloat16 or wider, within the bound.
A program may use at most 320 MiB of HBM per device.

v0:
```python
from functools import partial

import jax
import jax.numpy as jnp
from jax import lax
from jax.sharding import PartitionSpec as P

epsilon = 1e-06
masked_value = -1e30


def matmul(former, latter):
    return jnp.dot(former, latter, preferred_element_type=jnp.float32)


def inner_rows(former, latter):
    return lax.dot_general(
        former, latter, (((0,), (0,)), ((), ())), preferred_element_type=jnp.float32
    )


def against(former, latter):
    return lax.dot_general(
        former, latter, (((1,), (1,)), ((), ())), preferred_element_type=jnp.float32
    )


def norm_scale(matrix):
    return lax.rsqrt(jnp.mean(matrix * matrix, axis=1, keepdims=True) + epsilon)


def norm_back(upstream, normed, scaling, gain_vec):
    weighted = upstream * gain_vec
    return scaling * (weighted - normed * jnp.mean(weighted * normed, axis=1, keepdims=True))


def raw_scores(query_rows, key_rows, decays, segment, head_dim):
    length = query_rows.shape[0]
    head_count = decays.shape[1]
    query_heads = query_rows.reshape(length, head_count, head_dim)
    key_heads = key_rows.reshape(length, head_count, head_dim)
    scores = jnp.einsum("qhd,khd->hqk", query_heads, key_heads, preferred_element_type=jnp.float32)
    scores = scores * float(head_dim) ** (-0.5)
    decay_t = decays.T
    scores = scores + decay_t[:, :, None] - decay_t[:, None, :]
    places = lax.iota(jnp.int32, length)
    allowed = (places[None, :] <= places[:, None]) & (segment[:, None] == segment[None, :])
    return (jnp.where(allowed[None], scores, masked_value), query_heads, key_heads)


def attend_forward(pieces, head_dim):
    query_rows, key_rows, value_rows, decays, segment = pieces
    length = query_rows.shape[0]
    head_count = decays.shape[1]
    scores, query_heads, key_heads = raw_scores(query_rows, key_rows, decays, segment, head_dim)
    row_peak = jnp.max(scores, axis=2, keepdims=True)
    exp_scores = jnp.exp(scores - row_peak)
    row_total = jnp.sum(exp_scores, axis=2, keepdims=True)
    probs_low = (exp_scores / row_total).astype(jnp.bfloat16)
    value_heads = value_rows.reshape(length, head_count, head_dim)
    mixed_out = jnp.einsum(
        "hqk,khd->qhd", probs_low, value_heads, preferred_element_type=jnp.float32
    )
    logsum = row_peak[:, :, 0] + jnp.log(row_total[:, :, 0])
    return (mixed_out.reshape(length, head_count * head_dim), logsum)


def attend_backward(pieces, head_dim):
    query_rows, key_rows, value_rows, decays, segment, logsum, mixed_grad = pieces
    length = query_rows.shape[0]
    head_count = decays.shape[1]
    scaling = float(head_dim) ** (-0.5)
    scores, query_heads, key_heads = raw_scores(query_rows, key_rows, decays, segment, head_dim)
    probs = jnp.exp(scores - logsum[:, :, None])
    probs_low = probs.astype(jnp.bfloat16)
    value_heads = value_rows.reshape(length, head_count, head_dim)
    grad_heads = mixed_grad.reshape(length, head_count, head_dim)
    value_grad = jnp.einsum(
        "hqk,qhd->khd", probs_low, grad_heads, preferred_element_type=jnp.float32
    )
    prob_grad = jnp.einsum(
        "qhd,khd->hqk", grad_heads, value_heads, preferred_element_type=jnp.float32
    )
    row_delta = jnp.sum(probs * prob_grad, axis=2, keepdims=True)
    score_grad = (probs * (prob_grad - row_delta)).astype(jnp.bfloat16)
    query_grad = (
        jnp.einsum("hqk,khd->qhd", score_grad, key_heads, preferred_element_type=jnp.float32)
        * scaling
    )
    key_grad = (
        jnp.einsum("hqk,qhd->khd", score_grad, query_heads, preferred_element_type=jnp.float32)
        * scaling
    )
    grad_wide = score_grad.astype(jnp.float32)
    decay_grad = (jnp.sum(grad_wide, axis=2) - jnp.sum(grad_wide, axis=1)).T
    full_width = head_count * head_dim
    return (
        query_grad.reshape(length, full_width).astype(jnp.bfloat16),
        key_grad.reshape(length, full_width).astype(jnp.bfloat16),
        value_grad.reshape(length, full_width).astype(jnp.bfloat16),
        decay_grad,
    )


def local(
    tokens,
    segment_ids,
    first_gain,
    query_weight,
    key_weight,
    value_weight,
    outgate_weight,
    forget_weight,
    forget_bias,
    output_weight,
    second_gain,
    gate_weight,
    up_weight,
    down_weight,
    cotangent,
):
    local_heads = forget_weight.shape[1]
    head_dim = query_weight.shape[1] // local_heads
    sequences = segment_ids.shape[0]
    length = segment_ids.shape[1]

    def by_sequence(stacked):
        return stacked.reshape(sequences, length, stacked.shape[1])

    inputs = tokens.astype(jnp.float32)
    scale_one = norm_scale(inputs)
    normed_one = inputs * scale_one
    first_rows = (normed_one * first_gain).astype(jnp.bfloat16)
    first_all = lax.all_gather(first_rows, "tensor", axis=0, tiled=True)
    query_rows = matmul(first_all, query_weight).astype(jnp.bfloat16)
    key_rows = matmul(first_all, key_weight).astype(jnp.bfloat16)
    value_rows = matmul(first_all, value_weight).astype(jnp.bfloat16)
    outgate = jax.nn.sigmoid(matmul(first_all, outgate_weight))
    forget_logit = matmul(first_all, forget_weight) + forget_bias
    decays = jnp.cumsum(
        jax.nn.log_sigmoid(forget_logit).reshape(sequences, length, local_heads), axis=1
    )
    mixed_seq, logsum = lax.map(
        partial(attend_forward, head_dim=head_dim),
        (
            by_sequence(query_rows),
            by_sequence(key_rows),
            by_sequence(value_rows),
            decays,
            segment_ids,
        ),
    )
    head_width = query_rows.shape[1]
    mixed_out = mixed_seq.reshape(sequences * length, head_width)
    gated_out = (mixed_out * outgate).astype(jnp.bfloat16)
    attn_rows = lax.psum_scatter(
        matmul(gated_out, output_weight), "tensor", scatter_dimension=0, tiled=True
    )
    middle = inputs + attn_rows
    scale_two = norm_scale(middle)
    normed_two = middle * scale_two
    second_rows = (normed_two * second_gain).astype(jnp.bfloat16)
    second_all = lax.all_gather(second_rows, "tensor", axis=0, tiled=True)
    gate_pre = matmul(second_all, gate_weight)
    up_pre = matmul(second_all, up_weight)
    sigmoid_gate = jax.nn.sigmoid(gate_pre)
    swish_out = gate_pre * sigmoid_gate
    hidden = (swish_out * up_pre).astype(jnp.bfloat16)
    mlp_rows = lax.psum_scatter(
        matmul(hidden, down_weight).astype(jnp.bfloat16), "tensor", scatter_dimension=0, tiled=True
    ).astype(jnp.float32)
    result = (middle + mlp_rows).astype(jnp.bfloat16)
    upstream = lax.all_gather(cotangent, "tensor", axis=0, tiled=True)
    grad_down = inner_rows(hidden, upstream)
    hidden_grad = against(upstream, down_weight)
    gate_grad = (
        hidden_grad * up_pre * sigmoid_gate * (1.0 + gate_pre * (1.0 - sigmoid_gate))
    ).astype(jnp.bfloat16)
    up_grad = (hidden_grad * swish_out).astype(jnp.bfloat16)
    grad_gate = inner_rows(second_all, gate_grad)
    grad_up = inner_rows(second_all, up_grad)
    second_grad = lax.psum_scatter(
        against(gate_grad, gate_weight) + against(up_grad, up_weight),
        "tensor",
        scatter_dimension=0,
        tiled=True,
    )
    middle_grad = cotangent.astype(jnp.float32) + norm_back(
        second_grad, normed_two, scale_two, second_gain
    )
    gain_two_part = jnp.sum(second_grad * normed_two, axis=0)
    middle_low = middle_grad.astype(jnp.bfloat16)
    middle_all = lax.all_gather(middle_low, "tensor", axis=0, tiled=True)
    grad_output = inner_rows(gated_out, middle_all)
    gated_grad = against(middle_all, output_weight)
    mixed_grad = (gated_grad * outgate).astype(jnp.bfloat16)
    outgate_grad = (gated_grad * mixed_out * outgate * (1.0 - outgate)).astype(jnp.bfloat16)
    grad_outgate = inner_rows(first_all, outgate_grad)
    query_seq, key_seq, value_seq, decay_grad = lax.map(
        partial(attend_backward, head_dim=head_dim),
        (
            by_sequence(query_rows),
            by_sequence(key_rows),
            by_sequence(value_rows),
            decays,
            segment_ids,
            logsum,
            by_sequence(mixed_grad),
        ),
    )
    query_grad = query_seq.reshape(sequences * length, head_width)
    key_grad = key_seq.reshape(sequences * length, head_width)
    value_grad = value_seq.reshape(sequences * length, head_width)
    log_grad = jnp.flip(jnp.cumsum(jnp.flip(decay_grad, 1), axis=1), 1).reshape(
        sequences * length, local_heads
    )
    forget_grad = (log_grad * jax.nn.sigmoid(-forget_logit)).astype(jnp.bfloat16)
    grad_query = inner_rows(first_all, query_grad)
    grad_key = inner_rows(first_all, key_grad)
    grad_value = inner_rows(first_all, value_grad)
    grad_forget = inner_rows(first_all, forget_grad)
    bias_part = jnp.sum(forget_grad.astype(jnp.float32), axis=0)
    total = against(query_grad, query_weight)
    total = total + against(key_grad, key_weight)
    total = total + against(value_grad, value_weight)
    total = total + against(outgate_grad, outgate_weight)
    first_grad = lax.psum_scatter(
        (total + against(forget_grad, forget_weight)).astype(jnp.bfloat16),
        "tensor",
        scatter_dimension=0,
        tiled=True,
    ).astype(jnp.float32)
    tokens_grad = middle_grad + norm_back(first_grad, normed_one, scale_one, first_gain)
    gain_one_part = jnp.sum(first_grad * normed_one, axis=0)
    placed = lax.dynamic_update_slice(
        jnp.zeros((local_heads * lax.axis_size("tensor"),), jnp.float32),
        bias_part,
        (lax.axis_index("tensor") * local_heads,),
    )
    gain_one, gain_two, bias_total = lax.psum(
        (gain_one_part, gain_two_part, placed), ("dp", "tensor")
    )
    summed = tuple(
        (
            lax.psum_scatter(
                grad_query.astype(jnp.bfloat16), "dp", scatter_dimension=0, tiled=True
            ).astype(jnp.float32),
            lax.psum_scatter(
                grad_key.astype(jnp.bfloat16), "dp", scatter_dimension=0, tiled=True
            ).astype(jnp.float32),
            lax.psum_scatter(
                grad_value.astype(jnp.bfloat16), "dp", scatter_dimension=0, tiled=True
            ).astype(jnp.float32),
            lax.psum_scatter(
                grad_outgate.astype(jnp.bfloat16), "dp", scatter_dimension=0, tiled=True
            ).astype(jnp.float32),
            lax.psum_scatter(
                grad_forget.astype(jnp.bfloat16), "dp", scatter_dimension=0, tiled=True
            ).astype(jnp.float32),
            lax.psum_scatter(
                grad_output.astype(jnp.bfloat16), "dp", scatter_dimension=1, tiled=True
            ).astype(jnp.float32),
            lax.psum_scatter(
                grad_gate.astype(jnp.bfloat16), "dp", scatter_dimension=0, tiled=True
            ).astype(jnp.float32),
            lax.psum_scatter(
                grad_up.astype(jnp.bfloat16), "dp", scatter_dimension=0, tiled=True
            ).astype(jnp.float32),
            lax.psum_scatter(
                grad_down.astype(jnp.bfloat16), "dp", scatter_dimension=1, tiled=True
            ).astype(jnp.float32),
        )
    )
    return (
        result,
        tokens_grad,
        gain_one,
        summed[0],
        summed[1],
        summed[2],
        summed[3],
        summed[4],
        bias_total,
        summed[5],
        gain_two,
        summed[6],
        summed[7],
        summed[8],
    )


def solution(mesh):
    in_specs = (
        P(("dp", "tensor"), None),
        P("dp", None),
        P(),
        P(None, "tensor"),
        P(None, "tensor"),
        P(None, "tensor"),
        P(None, "tensor"),
        P(None, "tensor"),
        P("tensor"),
        P("tensor", None),
        P(),
        P(None, "tensor"),
        P(None, "tensor"),
        P("tensor", None),
        P(("dp", "tensor"), None),
    )
    out_specs = (
        P(("dp", "tensor"), None),
        P(("dp", "tensor"), None),
        P(),
        P("dp", "tensor"),
        P("dp", "tensor"),
        P("dp", "tensor"),
        P("dp", "tensor"),
        P("dp", "tensor"),
        P(),
        P("tensor", "dp"),
        P(),
        P("dp", "tensor"),
        P("dp", "tensor"),
        P("tensor", "dp"),
    )
    return jax.shard_map(local, mesh=mesh, in_specs=in_specs, out_specs=out_specs, check_vma=False)
```

profile of v0, /device:TPU:0, one launch (start us, length us, event | category | flops | bytes accessed | tf_op | source)
XLA Modules:
  0.0 1572.6 jit_solution(2904650248160119221)
XLA Ops:
  7.2 1.9 fusion.18
  9.8 3.0 fusion.15
  13.5 14.3 all-gather.5.cloned.1.call-done
  27.8 3.4 fusion.26
  31.3 3.4 reduce-window.14
  35.2 5.4 convolution_convert_fusion.10
  40.7 2.7 convolution_convert_fusion.11
  43.4 19.2 %fusion.31 = (f32[12,1024]{1,0:T(8,128)S(1)}, f32[12,1024,1024]{1,2,0:T(8,128)}) fusion(f32[12,1024]{1,0:T(8,128)S(1)} %bitcast.156, bf16[1024,12,64]{0,2,1:T(8,128)(2,1)S(1)} %bitcast.138, bf16[1024,12,64]{0,2,1:T(8,128)(2,1)S(1)} %bitcast.144, pred[1024,1024]{0,1:T(8,128)(4,1)S(1)} %fusion.11), kind=kOutput, calls=%fused_computation.87 | convolution fusion | flops 1673515008 | bytes 54624256 | tf_op jit(solution)/shard_map/while/body/eval_jaxpr/qhd,khd->hqk/dot_general | solution.py:42
  62.6 19.3 %fusion = f32[12,1024]{1,0:T(8,128)S(1)} fusion(f32[12,1024,1024]{1,2,0:T(8,128)} %get-tuple-element.98, f32[12,1024]{1,0:T(8,128)S(1)} %get-tuple-element.97), kind=kLoop, calls=%fused_computation.8 | loop fusion | flops 25153536 | bytes 50429952 | tf_op jit(solution)/shard_map/while/body/eval_jaxpr/reduce_sum | solution.py:58
  81.8 2.7 convolution_convert_fusion.12
  84.6 19.3 %fusion.5 = f32[12,64,1024]{2,1,0:T(8,128)S(1)} fusion(bf16[1024,12,64]{0,2,1:T(8,128)(2,1)S(1)} %bitcast.148, f32[12,1024,1024]{1,2,0:T(8,128)} %get-tuple-element.98, f32[12,1024]{1,0:T(8,128)S(1)} %fusion, f32[12,1024]{1,0:T(8,128)S(1)} %get-tuple-element.97), kind=kOutput, calls=%fused_computation.12 | convolution fusion | flops 1648361472 | bytes 55148544 | tf_op jit(solution)/shard_map/while/body/eval_jaxpr/hqk,khd->qhd/dot_general | solution.py:61
  103.9 4.9 fusion.19
  110.0 4.7 fusion.32
  114.8 15.3 reduce-scatter.16.cloned.1.call-done
  130.1 2.8 multiply_reduce_fusion.3
  136.7 13.7 all-gather.7.cloned.1.call-done
  150.4 12.6 fusion.34
  163.0 10.9 fusion.33
  173.9 19.0 %multiply_convert_fusion.1 = (bf16[1024,2048]{1,0:T(8,128)(2,1)}, bf16[1024,2048]{1,0:T(8,128)(2,1)}, bf16[1024,2048]{1,0:T(8,128)(2,1)}) fusion(f32[1024,2048]{1,0:T(8,128)} %fusion.33, f32[1024,2048]{1,0:T(8,128)} %fusion.34, bf16[1024,1536]{1,0:T(8,128)(2,1)} %all-gather.9.cloned.1.call-done, bf16[2048,1536]{1,0:T(8,128)(2,1)} %param.28), kind=kOutput, calls=%fused_computation.13 | convolution fusion | flops 6473908224 | bytes 38797312 | tf_op jit(solution)/shard_map/dot_general | solution.py:23
  192.9 10.2 fusion.35
  203.2 11.1 convolution_add_fusion
  214.3 15.3 reduce-scatter.20.cloned.1.call-done
  229.6 4.3 multiply_reduce_fusion.1
  234.3 3.5 fusion.29
  237.9 11.4 convolution_convert_fusion
  249.4 11.4 convolution_convert_fusion.1
  260.9 11.5 convolution_convert_fusion.2
  272.6 7.0 multiply_convert_fusion.6
  279.6 33.3 %multiply_reduce_fusion = (f32[12,1024]{1,0:T(8,128)S(1)}, f32[12,1024,1024]{1,2,0:T(8,128)}) fusion(f32[12,1024,1024]{1,2,0:T(8,128)} %get-tuple-element.98, f32[12,1024]{1,0:T(8,128)S(1)} %log_add_fusion, bf16[1024,12,64]{0,2,1:T(8,128)(2,1)} %bitcast.136, bf16[1024,12,64]{0,2,1:T(8,128)(2,1)} %bitcast.149), kind=kOutput, calls=%fused_computation.3 | convolution fusion | flops 1648349184 | bytes 103907328 | tf_op jit(solution)/shard_map/while/body/eval_jaxpr/qhd,khd->hqk/dot_general | solution.py:81
  312.9 41.5 %convert_reduce_fusion = (f32[12,1024]{1,0:T(8,128)S(1)}, f32[12,1024]{1,0:T(8,128)S(1)}, bf16[12,1024,1024]{1,2,0:T(8,128)(2,1)}) fusion(f32[12,1024,1024]{1,2,0:T(8,128)} %get-tuple-element.102, f32[12,1024]{1,0:T(8,128)S(1)} %get-tuple-element.101, f32[12,1024,1024]{1,2,0:T(8,128)} %get-tuple-element.98, f32[12,1024]{1,0:T(8,128)S(1)} %log_add_fusion), kind=kLoop, calls=%fused_computation | loop fusion | flops 88055808 | bytes 126025728 | tf_op jit(solution)/shard_map/while/body/eval_jaxpr/reduce_sum | solution.py:95
  355.0 3.4 reduce-window.16
  359.6 2.4 convolution_convert_fusion.9
  363.1 6.4 convolution_convert_fusion.4
  369.5 19.2 %fusion.23 = bf16[12,64,1024]{2,1,0:T(8,128)(2,1)S(1)} fusion(bf16[1024,12,64]{0,2,1:T(8,128)(2,1)} %bitcast.137, f32[12,1024,1024]{1,2,0:T(8,128)} %get-tuple-element.98, f32[12,1024]{1,0:T(8,128)S(1)} %log_add_fusion), kind=kOutput, calls=%fused_computation.63 | convolution fusion | flops 1636564992 | bytes 53526528 | tf_op jit(solution)/shard_map/while/body/eval_jaxpr/hqk,qhd->khd/dot_general | solution.py:78
  389.9 4.0 convolution_convert_fusion.6
  394.0 6.5 convolution_convert_fusion.5
  400.6 13.4 multiply_convert_fusion.5
  415.1 4.0 convolution_convert_fusion.8
  419.2 14.1 multiply_convert_fusion.4
  433.3 6.5 convolution_convert_fusion.7
  440.0 5.0 fusion.39
  445.0 2.7 fusion.38
  447.7 2.7 fusion.37
  450.4 4.7 fusion.36
  455.1 6.6 add_convert_fusion
  462.0 11.3 convolution_convert_fusion.3
  473.3 1.9 convert_element_type.214
  475.3 82.3 %reduce-scatter.36.cloned.1.call-done = bf16[96,2048]{1,0:T(8,128)(2,1)} async-done(((bf16[1536,2048]{1,0:T(8,128)(2,1)}), bf16[96,2048]{1,0:T(8,128)(2,1)}) %reduce-scatter.36.cloned.1.call-update) | async-done | bytes 393232 | tf_op jit(solution)/shard_map/reduce_scatter | solution.py:266
  557.6 1.9 convert_element_type.212
  559.5 149.2 %reduce-scatter.34.cloned.1.call-done = bf16[96,2048]{1,0:T(8,128)(2,1)} async-done(((bf16[1536,2048]{1,0:T(8,128)(2,1)}), bf16[96,2048]{1,0:T(8,128)(2,1)}) %reduce-scatter.34.cloned.1.call-update) | async-done | bytes 393232 | tf_op jit(solution)/shard_map/reduce_scatter | solution.py:263
  708.8 1.9 convert_element_type.210
  710.9 124.6 %reduce-scatter.40.cloned.1.call-done = bf16[96,12]{1,0:T(8,128)(2,1)} async-done(((bf16[1536,12]{1,0:T(8,128)(2,1)}), bf16[96,12]{1,0:T(8,128)(2,1)}) %reduce-scatter.40.cloned.1.call-update) | async-done | bytes 2320
  836.9 132.1 %reduce-scatter.32.cloned.1.call-done = bf16[768,96]{0,1:T(8,128)(2,1)} async-done(((bf16[768,1536]{0,1:T(8,128)(2,1)}), bf16[768,96]{0,1:T(8,128)(2,1)}) %reduce-scatter.32.cloned.1.call-update) | async-done | bytes 147472 | tf_op jit(solution)/shard_map/reduce_scatter | solution.py:260
  969.0 1.6 convert_element_type.208
  970.7 131.6 %reduce-scatter.28.cloned.1.call-done = bf16[96,768]{1,0:T(8,128)(2,1)} async-done(((bf16[1536,768]{1,0:T(8,128)(2,1)}), bf16[96,768]{1,0:T(8,128)(2,1)}) %reduce-scatter.28.cloned.1.call-update) | async-done | bytes 147472 | tf_op jit(solution)/shard_map/reduce_scatter | solution.py:251
  1103.9 131.5 %reduce-scatter.30.cloned.1.call-done = bf16[96,768]{1,0:T(8,128)(2,1)} async-done(((bf16[1536,768]{1,0:T(8,128)(2,1)}), bf16[96,768]{1,0:T(8,128)(2,1)}) %reduce-scatter.30.cloned.1.call-update) | async-done | bytes 147472 | tf_op jit(solution)/shard_map/reduce_scatter | solution.py:254
  1235.5 1.6 convert_element_type.203
  1237.1 131.7 %reduce-scatter.24.cloned.1.call-done = bf16[96,768]{1,0:T(8,128)(2,1)} async-done(((bf16[1536,768]{1,0:T(8,128)(2,1)}), bf16[96,768]{1,0:T(8,128)(2,1)}) %reduce-scatter.24.cloned.1.call-update) | async-done | bytes 147472 | tf_op jit(solution)/shard_map/reduce_scatter | solution.py:245
  1370.4 131.4 %reduce-scatter.26.cloned.1.call-done = bf16[96,768]{1,0:T(8,128)(2,1)} async-done(((bf16[1536,768]{1,0:T(8,128)(2,1)}), bf16[96,768]{1,0:T(8,128)(2,1)}) %reduce-scatter.26.cloned.1.call-update) | async-done | bytes 147472 | tf_op jit(solution)/shard_map/reduce_scatter | solution.py:248
  1501.9 1.6 convert_element_type.199
  1503.5 11.3 reduce-scatter.22.cloned.1.call-done
  1514.8 2.9 fusion.17
  1517.8 41.0 %all-reduce = (f32[1536]{0:T(1024)}, f32[24]{0:T(128)}, f32[1536]{0:T(1024)}) all-reduce(f32[1536]{0:T(1024)S(1)} %get-tuple-element.66, f32[24]{0:T(128)S(1)} %dynamic_update_slice.19, f32[1536]{0:T(1024)S(1)} %copy-done.23), channel_id=1, replica_groups=mesh['dp'=16,'tensor'=2] {'dp','tensor'}, use_global_device_ids=true, to_apply=%region_18.19 | all-reduce | flops 3096 | bytes 24768 | tf_op jit(solution)/shard_map/psum | solution.py:240
  1558.8 7.0 fusion.14
  (155 shorter events, 18.2 us)
Async XLA Ops:
  7.2 102.8 %copy-start = (bf16[768,1536]{1,0:T(8,128)(2,1)S(1)}, bf16[768,1536]{1,0:T(8,128)(2,1)}, u32[]{:S(2)}) copy-start(bf16[768,1536]{1,0:T(8,128)(2,1)} %param.24) | copy-start | bytes 7077892
  7.2 5.7 copy-start.28
  7.2 20.6 %all-gather.5.cloned.1.call-start = ((), (), s32[]{:S(2)}) async-start(), calls=%async_computation.13 | async-start | bytes 4718592 | tf_op jit(solution)/shard_map/all_gather | solution.py:134
  9.2 18.6 %copy-start.16 = (bf16[1536,12]{0,1:T(8,128)(2,1)S(1)}, bf16[1536,12]{0,1:T(8,128)(2,1)}, u32[]{:S(2)}) copy-start(bf16[1536,12]{0,1:T(8,128)(2,1)} %param.22) | copy-start | bytes 110596
  9.2 18.6 %copy-start.29 = (f32[12]{0:T(128)S(1)}, f32[12]{0:T(128)}, u32[]{:S(2)}) copy-start(f32[12]{0:T(128)} %param.23) | copy-start | bytes 148
  9.2 0.6 copy-start.24
  12.8 117.3 %reduce-scatter.16.cloned.1.call-start = ((), (), s32[]{:S(2)}) async-start(), calls=%async_computation.14 | async-start | bytes 9437184 | tf_op jit(solution)/shard_map/reduce_scatter | solution.py:156
  35.2 5.4 copy-start.4
  35.2 5.4 copy-start.35
  40.6 2.7 copy-start.11
  43.4 19.2 %copy-start.7 = (bf16[1024,768]{0,1:T(8,128)(2,1)}, bf16[1024,768]{0,1:T(8,128)(2,1)S(1)}, u32[]{:S(2)}) copy-start(bf16[1024,768]{0,1:T(8,128)(2,1)S(1)} %convolution_convert_fusion.11) | copy-start | bytes 4718596
  62.6 19.3 %copy-start.32 = (bf16[1536,768]{1,0:T(8,128)(2,1)S(1)}, bf16[1536,768]{1,0:T(8,128)(2,1)}, u32[]{:S(2)}) copy-start(bf16[1536,768]{1,0:T(8,128)(2,1)} %param.20) | copy-start | bytes 7077892
  84.6 19.3 %copy-start.14 = (bf16[1024,768]{0,1:T(8,128)(2,1)}, bf16[1024,768]{0,1:T(8,128)(2,1)S(1)}, u32[]{:S(2)}) copy-start(bf16[1024,768]{0,1:T(8,128)(2,1)S(1)} %convolution_convert_fusion.12) | copy-start | bytes 4718596
  84.6 19.3 %copy-start.31 = (bf16[1536,768]{1,0:T(8,128)(2,1)S(1)}, bf16[1536,768]{1,0:T(8,128)(2,1)}, u32[]{:S(2)}) copy-start(bf16[1536,768]{1,0:T(8,128)(2,1)} %param.21) | copy-start | bytes 7077892
  103.9 4.9 copy-start.37
  108.8 1.1 copy-start.38
  114.7 19.8 %copy-start.18 = (f32[1536]{0:T(1024)S(1)}, f32[1536]{0:T(1024)}, u32[]{:S(2)}) copy-start(f32[1536]{0:T(1024)} %param.25) | copy-start | bytes 18436
  114.7 35.6 %all-gather.7.cloned.1.call-start = ((), (), s32[]{:S(2)}) async-start(), calls=%async_computation.15 | async-start | bytes 4718592 | tf_op jit(solution)/shard_map/all_gather | solution.py:163
  132.9 1.6 copy-start.1
  132.9 101.0 %copy-start.21 = (f32[512]{0:T(512)}, f32[512]{0:T(512)S(1)}, u32[]{:S(2)}) copy-start(f32[512]{0:T(512)S(1)} %add_rsqrt_fusion) | copy-start | bytes 6148
  136.1 37.9 %all-gather.9.cloned.1.call-start = ((), (), s32[]{:S(2)}) async-start(), calls=%async_computation.17 | async-start | bytes 4718592 | tf_op jit(solution)/shard_map/all_gather | solution.py:173
  136.6 93.0 %reduce-scatter.20.cloned.1.call-start = ((), (), s32[]{:S(2)}) async-start(), calls=%async_computation.18 | async-start | bytes 9437184 | tf_op jit(solution)/shard_map/reduce_scatter | solution.py:182
  150.4 12.6 copy-start.30
  192.9 10.2 copy-start.39
  214.2 58.3 %all-gather.11.cloned.1.call-start = ((), (), s32[]{:S(2)}) async-start(), calls=%async_computation.19 | async-start | bytes 4718592 | tf_op jit(solution)/shard_map/all_gather | solution.py:193
  229.6 4.4 copy-start.2
  229.6 4.7 copy-start.3
  234.3 3.5 copy-start.26
  237.9 235.5 %reduce-scatter.38.cloned.1.call-start = ((), (), s32[]{:S(2)}) async-start(), calls=%async_computation.28 | async-start | bytes 6684672 | tf_op jit(solution)/shard_map/reduce_scatter | solution.py:269
  249.3 308.2 %reduce-scatter.36.cloned.1.call-start = ((), (), s32[]{:S(2)}) async-start(), calls=%async_computation.27 | async-start | bytes 6684672 | tf_op jit(solution)/shard_map/reduce_scatter | solution.py:266
  260.9 447.9 %reduce-scatter.34.cloned.1.call-start = ((), (), s32[]{:S(2)}) async-start(), calls=%async_computation.26 | async-start | bytes 6684672 | tf_op jit(solution)/shard_map/reduce_scatter | solution.py:263
  272.5 563.1 %reduce-scatter.40.cloned.1.call-start = ((), (), s32[]{:S(2)}) async-start(), calls=%async_computation.29 | async-start | bytes 417792
  312.9 46.6 %copy-start.15 = (f32[1024,12]{0,1:T(8,128)S(1)}, f32[1024,12]{0,1:T(8,128)}, u32[]{:S(2)}) copy-start(f32[1024,12]{0,1:T(8,128)} %get-tuple-element.96) | copy-start | bytes 147460
  363.0 606.0 %reduce-scatter.32.cloned.1.call-start = ((), (), s32[]{:S(2)}) async-start(), calls=%async_computation.25 | async-start | bytes 2506752 | tf_op jit(solution)/shard_map/reduce_scatter | solution.py:260
  369.5 732.8 %reduce-scatter.28.cloned.1.call-start = ((), (), s32[]{:S(2)}) async-start(), calls=%async_computation.23 | async-start | bytes 2506752 | tf_op jit(solution)/shard_map/reduce_scatter | solution.py:251
  369.5 20.4 %copy-start.5 = (bf16[1024,1536]{1,0:T(8,128)(2,1)S(1)}, bf16[1024,1536]{1,0:T(8,128)(2,1)}, u32[]{:S(2)}) copy-start(bf16[1024,1536]{1,0:T(8,128)(2,1)} %all-gather.5.cloned.1.call-done) | copy-start | bytes 9437188
  388.7 1.1 copy-start.9
  394.0 841.5 %reduce-scatter.30.cloned.1.call-start = ((), (), s32[]{:S(2)}) async-start(), calls=%async_computation.24 | async-start | bytes 2506752 | tf_op jit(solution)/shard_map/reduce_scatter | solution.py:254
  400.5 968.3 %reduce-scatter.24.cloned.1.call-start = ((), (), s32[]{:S(2)}) async-start(), calls=%async_computation.21 | async-start | bytes 2506752 | tf_op jit(solution)/shard_map/reduce_scatter | solution.py:245
  400.6 14.6 copy-start.6
  414.0 1.1 copy-start.12
  419.2 1082.7 %reduce-scatter.26.cloned.1.call-start = ((), (), s32[]{:S(2)}) async-start(), calls=%async_computation.22 | async-start | bytes 2506752 | tf_op jit(solution)/shard_map/reduce_scatter | solution.py:248
  439.9 1074.9 %reduce-scatter.22.cloned.1.call-start = ((), (), s32[]{:S(2)}) async-start(), calls=%async_computation.20 | async-start | bytes 4718592 | tf_op jit(solution)/shard_map/reduce_scatter | solution.py:227
  439.9 5.0 copy-start.10
  439.9 5.0 copy-start.33
  445.0 2.7 copy-start.8
  445.0 2.7 copy-start.34
  447.7 2.7 copy-start.13
  447.7 2.7 copy-start.36
  450.4 4.7 copy-start.17
  461.7 1097.1 %reduce-scatter.18.cloned.1.call-start = ((), (), s32[]{:S(2)}) async-start(), calls=%async_computation.16 | async-start | bytes 4718592 | tf_op jit(solution)/shard_map/reduce_scatter | solution.py:169
  473.3 1041.5 %copy-start.20 = (f32[1536]{0:T(1024)S(1)}, f32[1536]{0:T(1024)}, u32[]{:S(2)}) copy-start(f32[1536]{0:T(1024)} %param.17) | copy-start | bytes 18436
  473.3 1041.5 %copy-start.25 = (f32[512]{0:T(512)S(1)}, f32[512]{0:T(512)}, u32[]{:S(2)}) copy-start(f32[512]{0:T(512)} %copy-done.24) | copy-start | bytes 6148
  559.5 958.3 %copy-start.23 = (f32[1536]{0:T(1024)S(1)}, f32[1536]{0:T(1024)}, u32[]{:S(2)}) copy-start(f32[1536]{0:T(1024)} %get-tuple-element.64) | copy-start | bytes 18436
  559.5 999.3 %copy-start.19 = (f32[1536]{0:T(1024)S(1)}, f32[1536]{0:T(1024)}, u32[]{:S(2)}) copy-start(f32[1536]{0:T(1024)} %param.25) | copy-start | bytes 18436
  559.5 999.3 %copy-start.22 = (f32[512]{0:T(512)S(1)}, f32[512]{0:T(512)}, u32[]{:S(2)}) copy-start(f32[512]{0:T(512)} %copy-done.21) | copy-start | bytes 6148
  559.5 999.3 %copy-start.27 = (f32[512]{0:T(512)S(1)}, f32[512]{0:T(512)}, u32[]{:S(2)}) copy-start(f32[512]{0:T(512)} %copy-done.26) | copy-start | bytes 6148
Sparse Core Ops, SparseCore 0:
  12.9 14.8 all-gather.4
  114.8 15.1 reduce-scatter.15
  136.2 14.1 all-gather.6
  151.8 13.2 all-gather.8
  214.4 15.1 reduce-scatter.19
  238.0 14.1 all-gather.10
  257.4 148.9 reduce-scatter.37
  411.7 145.8 reduce-scatter.35
  562.8 145.9 reduce-scatter.33
  713.3 122.2 reduce-scatter.39
  840.4 128.5 reduce-scatter.31
  973.8 128.4 reduce-scatter.27
  1107.2 128.2 reduce-scatter.29
  1240.2 128.5 reduce-scatter.23
  1373.6 128.2 reduce-scatter.25
  1504.5 10.2 reduce-scatter.21
  1516.9 12.4 reduce-scatter.17
where the time goes:
time: 1580 us; the launch traced here: 1570 us
  waiting for transfers between devices  1090 us (69%)
  matrix products  310 us (20%)
  other arithmetic  110 us (7%)
  blocking collectives  41 us (3%)
    reduce_scatter x1, waiting for transfers between devices, local(): lax.psum_scatter(grad_gate.astype(jnp.bfloat16), 'dp', scatter_dimension=...  149 us
    reduce_scatter x1, waiting for transfers between devices, local(): lax.psum_scatter(grad_output.astype(jnp.bfloat16), 'dp', scatter_dimensio...  132 us
    reduce_scatter x1, waiting for transfers between devices, local(): lax.psum_scatter(grad_query.astype(jnp.bfloat16), 'dp', scatter_dimension...  132 us
    reduce_scatter x1, waiting for transfers between devices, local(): lax.psum_scatter(grad_value.astype(jnp.bfloat16), 'dp', scatter_dimension...  132 us
    reduce_scatter x1, waiting for transfers between devices, local(): lax.psum_scatter(grad_outgate.astype(jnp.bfloat16), 'dp', scatter_dimensi...  132 us
    reduce_scatter x1, waiting for transfers between devices, local(): lax.psum_scatter(grad_key.astype(jnp.bfloat16), 'dp', scatter_dimension=0...  131 us
    unnamed x18, waiting for transfers between devices  125 us
    reduce_scatter x1, waiting for transfers between devices, local(): lax.psum_scatter(grad_up.astype(jnp.bfloat16), 'dp', scatter_dimension=0,...  82.3 us
  transfers between devices with their start and end apart: 17, of which 13 were waited for; matrix products, arithmetic and copies ran while one was open for 17% of the time, Pallas kernels for 0%

commit v1 on v0

--- a/solution.py
+++ b/solution.py
@@ -32,6 +32,34 @@
 def norm_back(upstream, normed, scaling, gain_vec):
     weighted = upstream * gain_vec
     return scaling * (weighted - normed * jnp.mean(weighted * normed, axis=1, keepdims=True))
+
+
+def halve(stacked, bit, axis, wide):
+    mine = (lax.axis_index("dp") >> bit) & 1
+    count = lax.axis_size("dp")
+    sent = lax.ppermute(
+        lax.dynamic_index_in_dim(stacked, 1 - mine, axis, keepdims=False),
+        "dp",
+        [(place, place ^ (1 << bit)) for place in range(count)],
+    )
+    kept = lax.dynamic_index_in_dim(stacked, mine, axis, keepdims=False)
+    total = kept.astype(jnp.float32) + sent.astype(jnp.float32)
+    return total if wide else total.astype(jnp.bfloat16)
+
+
+def spread_sum(gradient, swap):
+    count = lax.axis_size("dp")
+    bits = count.bit_length() - 1
+    order = list(range(bits))
+    for front, back in swap:
+        order[front], order[back] = order[back], order[front]
+    live = list(range(bits - 1, -1, -1))
+    stacked = gradient.reshape((2,) * bits + (gradient.shape[0] // count, gradient.shape[1]))
+    for place, bit in enumerate(order):
+        axis = live.index(bit)
+        live.pop(axis)
+        stacked = halve(stacked, bit, axis, place == bits - 1)
+    return stacked
 
 
 def raw_scores(query_rows, key_rows, decays, segment, head_dim):
@@ -171,7 +199,6 @@
     ).astype(jnp.float32)
     result = (middle + mlp_rows).astype(jnp.bfloat16)
     upstream = lax.all_gather(cotangent, "tensor", axis=0, tiled=True)
-    grad_down = inner_rows(hidden, upstream)
     hidden_grad = against(upstream, down_weight)
     gate_grad = (
         hidden_grad * up_pre * sigmoid_gate * (1.0 + gate_pre * (1.0 - sigmoid_gate))
@@ -191,7 +218,7 @@
     gain_two_part = jnp.sum(second_grad * normed_two, axis=0)
     middle_low = middle_grad.astype(jnp.bfloat16)
     middle_all = lax.all_gather(middle_low, "tensor", axis=0, tiled=True)
-    grad_output = inner_rows(gated_out, middle_all)
+    grad_output = inner_rows(middle_all, gated_out)
     gated_grad = against(middle_all, output_weight)
     mixed_grad = (gated_grad * outgate).astype(jnp.bfloat16)
     outgate_grad = (gated_grad * mixed_out * outgate * (1.0 - outgate)).astype(jnp.bfloat16)
@@ -240,36 +267,23 @@
     gain_one, gain_two, bias_total = lax.psum(
         (gain_one_part, gain_two_part, placed), ("dp", "tensor")
     )
-    summed = tuple(
-        (
-            lax.psum_scatter(
-                grad_query.astype(jnp.bfloat16), "dp", scatter_dimension=0, tiled=True
-            ).astype(jnp.float32),
-            lax.psum_scatter(
-                grad_key.astype(jnp.bfloat16), "dp", scatter_dimension=0, tiled=True
-            ).astype(jnp.float32),
-            lax.psum_scatter(
-                grad_value.astype(jnp.bfloat16), "dp", scatter_dimension=0, tiled=True
-            ).astype(jnp.float32),
-            lax.psum_scatter(
-                grad_outgate.astype(jnp.bfloat16), "dp", scatter_dimension=0, tiled=True
-            ).astype(jnp.float32),
-            lax.psum_scatter(
-                grad_forget.astype(jnp.bfloat16), "dp", scatter_dimension=0, tiled=True
-            ).astype(jnp.float32),
-            lax.psum_scatter(
-                grad_output.astype(jnp.bfloat16), "dp", scatter_dimension=1, tiled=True
-            ).astype(jnp.float32),
-            lax.psum_scatter(
-                grad_gate.astype(jnp.bfloat16), "dp", scatter_dimension=0, tiled=True
-            ).astype(jnp.float32),
-            lax.psum_scatter(
-                grad_up.astype(jnp.bfloat16), "dp", scatter_dimension=0, tiled=True
-            ).astype(jnp.float32),
-            lax.psum_scatter(
-                grad_down.astype(jnp.bfloat16), "dp", scatter_dimension=1, tiled=True
-            ).astype(jnp.float32),
-        )
+    along, across, deep = (), ((0, 1),), ((0, 2),)
+    low = jnp.bfloat16
+    half = hidden.shape[1] // 2
+    down_grads = [
+        spread_sum(inner_rows(upstream, hidden[:, :half]).astype(low), along),
+        spread_sum(inner_rows(upstream, hidden[:, half:]).astype(low), across),
+    ]
+    summed = (
+        spread_sum(grad_query.astype(low), along),
+        spread_sum(grad_key.astype(low), across),
+        spread_sum(grad_value.astype(low), deep),
+        spread_sum(grad_outgate.astype(low), across),
+        spread_sum(grad_forget.astype(low), along),
+        spread_sum(grad_output.astype(low), along).T,
+        spread_sum(grad_gate.astype(low), along),
+        spread_sum(grad_up.astype(low), across),
+        jnp.concatenate(down_grads, axis=1).T,
     )
     return (
         result,

time: 1580 us -> 844 us (0.53)
  waiting for transfers between devices: 1090 us -> 249 us
  starting transfers between devices: 0.92 us -> 63.5 us
  local copies, waits for them, and re-layouts: 10.1 us -> 49.5 us
  matrix products: 310 us -> 292 us
  other arithmetic: 110 us -> 126 us
    reduce_scatter x8 -> x0, waiting for transfers between devices: 890 us -> none  [the longest x1 149 us: local(): lax.psum_scatter(grad_gate.astype(jnp.bfloat16), 'dp', scatter_dimension=...]
    ppermute x0 -> x40, waiting for transfers between devices: none -> 190 us  [halve(): lax.ppermute(lax.dynamic_index_in_dim(stacked, 1 - mine, axis, keepdims=F...]
    unnamed x18 -> x8, waiting for transfers between devices: 125 us -> 0.64 us
    ppermute x0 -> x40, starting transfers between devices: none -> 63.1 us  [halve(): lax.ppermute(lax.dynamic_index_in_dim(stacked, 1 - mine, axis, keepdims=F...]
    dynamic_slice x0 -> x16, local copies, waits for them, and re-layouts: none -> 23.2 us  [the longest x7 12.5 us: halve(): kept = lax.dynamic_index_in_dim(stacked, mine, axis, keepdims=False)]
    dot_general x9 -> x10, matrix products: 64.2 us -> 49.1 us  [inner_rows(): lax.dot_general(former, latter, (((0,), (0,)), ((), ())), preferred_eleme...]
  transfers between devices with their start and end apart: 17 -> 48, of which waited for: 13 -> 25; matrix products, arithmetic and copies ran while one was open for 17% -> 37% of each run, Pallas kernels for 0% -> 0%
where the time goes in v1:
time: 844 us; the launch traced here: 833 us
  matrix products  292 us (35%)
  waiting for transfers between devices  249 us (30%)
  other arithmetic  126 us (15%)
  starting transfers between devices  63.5 us (8%)
  local copies, waits for them, and re-layouts  49.5 us (6%)
  blocking collectives  37.8 us (4%)
  between operations  15.7 us (2%)
    ppermute x40, waiting for transfers between devices, halve(): lax.ppermute(lax.dynamic_index_in_dim(stacked, 1 - mine, axis, keepdims=F...  190 us
    dot_general x9, matrix products, against(): lax.dot_general(former, latter, (((1,), (1,)), ((), ())), preferred_eleme...  68.5 us
    ppermute x40, starting transfers between devices, halve(): lax.ppermute(lax.dynamic_index_in_dim(stacked, 1 - mine, axis, keepdims=F...  63.1 us
    dot_general x9, matrix products, matmul(): return jnp.dot(former, latter, preferred_element_type=jnp.float32)  55.7 us
    dot_general x10, matrix products, inner_rows(): lax.dot_general(former, latter, (((0,), (0,)), ((), ())), preferred_eleme...  49.1 us
    reduce_sum x1, other arithmetic, attend_backward(): decay_grad = (jnp.sum(grad_wide, axis=2) - jnp.sum(grad_wide, axis=1)).T  40.6 us
    psum x1, blocking collectives, local(): lax.psum((gain_one_part, gain_two_part, placed), ('dp', 'tensor'))  37.8 us
    dot_general x1, matrix products, attend_backward(): jnp.einsum('qhd,khd->hqk', grad_heads, value_heads, preferred_element_typ...  32.4 us
  transfers between devices with their start and end apart: 48, of which 25 were waited for; matrix products, arithmetic and copies ran while one was open for 37% of the time, Pallas kernels for 0%

profile of v1, /device:TPU:0, one launch (start us, length us, event | category | flops | bytes accessed | tf_op | source)
XLA Modules:
  0.0 833.4 jit_solution(7812901049966172741)
XLA Ops:
  9.8 3.0 fusion.19
  13.5 14.3 %all-gather.5.cloned.1.call-done = bf16[1024,1536]{1,0:T(8,128)(2,1)} async-done(((bf16[512,1536]{1,0:T(8,128)(2,1)}), bf16[1024,1536]{1,0:T(8,128)(2,1)}) %all-gather.5.cloned.1.call-update) | async-done | bytes 3145744 | tf_op jit(solution)/shard_map/all_gather | solution.py:162
  27.8 3.4 fusion.58
  31.3 3.4 reduce-window.14
  35.2 5.4 convolution_convert_fusion.12
  43.4 19.6 %fusion.72 = (f32[12,1024]{1,0:T(8,128)S(1)}, f32[12,1024,1024]{1,2,0:T(8,128)}) fusion(f32[12,1024]{1,0:T(8,128)S(1)} %bitcast.418, bf16[1024,12,64]{0,2,1:T(8,128)(2,1)S(1)} %bitcast.396, bf16[1024,12,64]{0,2,1:T(8,128)(2,1)S(1)} %bitcast.407, pred[1024,1024]{0,1:T(8,128)(4,1)S(1)} %fusion.13), kind=kOutput, calls=%fused_computation.240 | convolution fusion | flops 1673515008 | bytes 54624256 | tf_op jit(solution)/shard_map/while/body/eval_jaxpr/qhd,khd->hqk/dot_general | solution.py:70
  62.9 19.3 %fusion = f32[12,1024]{1,0:T(8,128)S(1)} fusion(f32[12,1024,1024]{1,2,0:T(8,128)} %get-tuple-element.116, f32[12,1024]{1,0:T(8,128)S(1)} %get-tuple-element.115), kind=kLoop, calls=%fused_computation.8 | loop fusion | flops 25153536 | bytes 50429952 | tf_op jit(solution)/shard_map/while/body/eval_jaxpr/reduce_sum | solution.py:86
  85.0 19.4 %fusion.5 = f32[12,64,1024]{2,1,0:T(8,128)S(1)} fusion(bf16[1024,12,64]{0,2,1:T(8,128)(2,1)S(1)} %bitcast.409, f32[12,1024,1024]{1,2,0:T(8,128)} %get-tuple-element.116, f32[12,1024]{1,0:T(8,128)S(1)} %fusion, f32[12,1024]{1,0:T(8,128)S(1)} %get-tuple-element.115), kind=kOutput, calls=%fused_computation.12 | convolution fusion | flops 1648361472 | bytes 55148544 | tf_op jit(solution)/shard_map/while/body/eval_jaxpr/hqk,khd->qhd/dot_general | solution.py:89
  104.4 4.9 fusion.27
  110.5 4.6 fusion.73
  115.2 15.3 %reduce-scatter.5.cloned.1.call-done = f32[512,1536]{1,0:T(8,128)} async-done(((f32[1024,1536]{1,0:T(8,128)}), f32[512,1536]{1,0:T(8,128)}) %reduce-scatter.5.cloned.1.call-update) | async-done | bytes 3145744 | tf_op jit(solution)/shard_map/reduce_scatter | solution.py:184
  137.1 13.7 %all-gather.7.cloned.1.call-done = bf16[1024,1536]{1,0:T(8,128)(2,1)} async-done(((bf16[512,1536]{1,0:T(8,128)(2,1)}), bf16[1024,1536]{1,0:T(8,128)(2,1)}) %all-gather.7.cloned.1.call-update) | async-done | bytes 3145744 | tf_op jit(solution)/shard_map/all_gather | solution.py:191
  150.8 12.8 %fusion.74 = f32[1024,2048]{1,0:T(8,128)} fusion(bf16[1024,1536]{1,0:T(8,128)(2,1)} %all-gather.7.cloned.1.call-done, bf16[1536,2048]{1,0:T(8,128)(2,1)} %param.26), kind=kOutput, calls=%fused_computation.242 | convolution fusion | flops 6442450944 | bytes 17825792 | tf_op jit(solution)/shard_map/dot_general | solution.py:13
  163.6 10.9 %fusion.75 = f32[1024,2048]{1,0:T(8,128)} fusion(bf16[1024,1536]{1,0:T(8,128)(2,1)S(1)} %copy-done.48, bf16[1536,2048]{1,0:T(8,128)(2,1)} %param.27), kind=kOutput, calls=%fused_computation.243 | convolution fusion | flops 6442450944 | bytes 17825792 | tf_op jit(solution)/shard_map/dot_general | solution.py:13
  174.5 19.1 %multiply_convert_fusion.1 = (bf16[1024,2048]{1,0:T(8,128)(2,1)}, bf16[1024,2048]{1,0:T(8,128)(2,1)}, bf16[1024,2048]{1,0:T(8,128)(2,1)}) fusion(f32[1024,2048]{1,0:T(8,128)} %fusion.74, f32[1024,2048]{1,0:T(8,128)} %fusion.75, bf16[1024,1536]{1,0:T(8,128)(2,1)} %all-gather.9.cloned.1.call-done, bf16[2048,1536]{1,0:T(8,128)(2,1)} %param.28), kind=kOutput, calls=%fused_computation.13 | convolution fusion | flops 6473908224 | bytes 38797312 | tf_op jit(solution)/shard_map/dot_general | solution.py:23
  193.6 10.2 %fusion.76 = f32[1024,1536]{1,0:T(8,128)S(1)} fusion(bf16[1024,2048]{1,0:T(8,128)(2,1)} %get-tuple-element.89, bf16[1536,2048]{1,0:T(8,128)(2,1)} %param.26), kind=kOutput, calls=%fused_computation.244 | convolution fusion | flops 6442450944 | bytes 16777216 | tf_op jit(solution)/shard_map/dot_general | solution.py:23
  203.9 10.7 %convolution_add_fusion = f32[1024,1536]{1,0:T(8,128)} fusion(f32[1024,1536]{1,0:T(8,128)S(1)} %fusion.76, bf16[1024,2048]{1,0:T(8,128)(2,1)S(1)} %copy-done.63, bf16[1536,2048]{1,0:T(8,128)(2,1)} %param.27), kind=kOutput, calls=%fused_computation.32 | convolution fusion | flops 6444023808 | bytes 23068672 | tf_op jit(solution)/shard_map/dot_general | solution.py:23
  214.6 15.3 %reduce-scatter.9.cloned.1.call-done = f32[512,1536]{1,0:T(8,128)} async-done(((f32[1024,1536]{1,0:T(8,128)}), f32[512,1536]{1,0:T(8,128)}) %reduce-scatter.9.cloned.1.call-update) | async-done | bytes 3145744 | tf_op jit(solution)/shard_map/reduce_scatter | solution.py:209
  229.9 4.3 multiply_reduce_fusion.1
  234.6 3.5 fusion.70
  238.3 7.7 fusion.15
  246.0 5.1 copy.85
  256.6 6.7 fusion.16
  263.3 4.7 copy.86
  267.9 3.4 constant_dynamic-slice_fusion.1
  274.1 7.0 multiply_convert_fusion.6
  281.1 32.4 %multiply_reduce_fusion = (f32[12,1024]{1,0:T(8,128)S(1)}, f32[12,1024,1024]{1,2,0:T(8,128)}) fusion(f32[12,1024,1024]{1,2,0:T(8,128)} %get-tuple-element.116, f32[12,1024]{1,0:T(8,128)S(1)} %log_add_fusion, bf16[1024,12,64]{0,2,1:T(8,128)(2,1)} %bitcast.390, bf16[1024,12,64]{0,2,1:T(8,128)(2,1)} %bitcast.410), kind=kOutput, calls=%fused_computation.3 | convolution fusion | flops 1648349184 | bytes 103907328 | tf_op jit(solution)/shard_map/while/body/eval_jaxpr/qhd,khd->hqk/dot_general | solution.py:109
  313.5 40.6 %convert_reduce_fusion = (f32[12,1024]{1,0:T(8,128)S(1)}, f32[12,1024]{1,0:T(8,128)S(1)}, bf16[12,1024,1024]{1,2,0:T(8,128)(2,1)}) fusion(f32[12,1024,1024]{1,2,0:T(8,128)} %get-tuple-element.120, f32[12,1024]{1,0:T(8,128)S(1)} %get-tuple-element.119, f32[12,1024,1024]{1,2,0:T(8,128)} %get-tuple-element.116, f32[12,1024]{1,0:T(8,128)S(1)} %log_add_fusion), kind=kLoop, calls=%fused_computation | loop fusion | flops 88055808 | bytes 126025728 | tf_op jit(solution)/shard_map/while/body/eval_jaxpr/reduce_sum | solution.py:123
  354.1 13.8 %multiply_convert_fusion.5 = bf16[12,64,1024]{2,1,0:T(8,128)(2,1)} fusion(bf16[1024,12,64]{0,2,1:T(8,128)(2,1)S(1)} %bitcast.408, bf16[12,1024,1024]{1,2,0:T(8,128)(2,1)} %get-tuple-element.85), kind=kOutput, calls=%fused_computation.73 | convolution fusion | flops 1612185600 | bytes 28311552 | tf_op jit(solution)/shard_map/while/body/eval_jaxpr/hqk,khd->qhd/dot_general | solution.py:115
  367.9 14.3 %multiply_convert_fusion.4 = bf16[12,64,1024]{2,1,0:T(8,128)(2,1)} fusion(bf16[1024,12,64]{0,2,1:T(8,128)(2,1)} %bitcast.397, bf16[12,1024,1024]{1,2,0:T(8,128)(2,1)} %get-tuple-element.85), kind=kOutput, calls=%fused_computation.72 | convolution fusion | flops 1612185600 | bytes 28311552 | tf_op jit(solution)/shard_map/while/body/eval_jaxpr/hqk,qhd->khd/dot_general | solution.py:119
  382.3 19.0 %fusion.38 = bf16[12,64,1024]{2,1,0:T(8,128)(2,1)} fusion(bf16[1024,12,64]{0,2,1:T(8,128)(2,1)S(1)} %bitcast.391, f32[12,1024,1024]{1,2,0:T(8,128)} %get-tuple-element.116, f32[12,1024]{1,0:T(8,128)S(1)} %log_add_fusion), kind=kOutput, calls=%fused_computation.94 | convolution fusion | flops 1636564992 | bytes 53526528 | tf_op jit(solution)/shard_map/while/body/eval_jaxpr/hqk,qhd->khd/dot_general | solution.py:106
  401.9 3.4 reduce-window.16
  406.4 5.0 fusion.78
  416.8 4.7 fusion.80
  422.2 6.5 add_convert_fusion
  428.7 9.8 %convolution_convert_fusion = bf16[1536,2048]{1,0:T(8,128)(2,1)S(1)} fusion(bf16[1024,1536]{1,0:T(8,128)(2,1)} %all-gather.7.cloned.1.call-done, bf16[1024,2048]{1,0:T(8,128)(2,1)} %get-tuple-element.88), kind=kOutput, calls=%fused_computation.18 | convolution fusion | flops 6445596672 | bytes 13631488 | tf_op jit(solution)/shard_map/dot_general | solution.py:17
  444.3 7.2 convolution_convert_fusion.1
  464.2 64.7 %collective-permute-done.33 = bf16[2,2,96,1024]{3,2,1,0:T(8,128)(2,1)S(1)} collective-permute-done((bf16[2,2,96,1024]{3,2,1,0:T(8,128)(2,1)S(1)}, bf16[2,2,96,1024]{3,2,1,0:T(8,128)(2,1)S(1)}, u32[]{:S(2)}, u32[]{:S(2)}) %collective-permute-start.33) | collective-permute-done | bytes 786464 | tf_op jit(solution)/shard_map/ppermute | solution.py:40
  531.5 8.2 convolution_convert_fusion.2
  539.8 4.7 collective-permute-done.37
  550.2 3.2 fusion.7
  555.4 3.2 fusion.8
  561.4 8.2 collective-permute-done.39
  569.7 17.5 %collective-permute-done.29 = bf16[2,2,96,2048]{3,2,0,1:T(8,128)(2,1)S(1)} collective-permute-done((bf16[2,2,96,2048]{3,2,0,1:T(8,128)(2,1)S(1)}, bf16[2,2,96,2048]{3,2,0,1:T(8,128)(2,1)S(1)}, u32[]{:S(2)}, u32[]{:S(2)}) %collective-permute-start.29) | collective-permute-done | bytes 1572896 | tf_op jit(solution)/shard_map/ppermute | solution.py:40
  588.2 4.1 collective-permute-done.25
  594.5 18.0 %collective-permute-done.30 = bf16[2,96,2048]{2,1,0:T(8,128)(2,1)S(1)} collective-permute-done((bf16[2,96,2048]{2,1,0:T(8,128)(2,1)S(1)}, bf16[2,96,2048]{2,1,0:T(8,128)(2,1)S(1)}, u32[]{:S(2)}, u32[]{:S(2)}) %collective-permute-start.30) | collective-permute-done | bytes 786464 | tf_op jit(solution)/shard_map/ppermute | solution.py:40
  613.0 15.6 %collective-permute-done.26 = bf16[2,96,2048]{2,1,0:T(8,128)(2,1)S(1)} collective-permute-done((bf16[2,96,2048]{2,1,0:T(8,128)(2,1)S(1)}, bf16[2,96,2048]{2,1,0:T(8,128)(2,1)S(1)}, u32[]{:S(2)}, u32[]{:S(2)}) %collective-permute-start.26) | collective-permute-done | bytes 786464 | tf_op jit(solution)/shard_map/ppermute | solution.py:40
  629.7 3.6 collective-permute-done.31
  637.2 3.3 convolution_convert_fusion.5
  646.0 5.0 convolution_convert_fusion.8
  656.6 4.5 collective-permute-start.12
  668.2 7.8 collective-permute-done.17
  691.1 5.9 collective-permute-done.19
  706.9 8.5 %collective-permute-done.4 = bf16[2,2,2,96,768]{4,3,0,1,2:T(8,128)(2,1)} collective-permute-done((bf16[2,2,2,96,768]{4,3,0,1,2:T(8,128)(2,1)}, bf16[2,2,2,96,768]{4,3,0,1,2:T(8,128)(2,1)}, u32[]{:S(2)}, u32[]{:S(2)}) %collective-permute-start.4) | collective-permute-done | bytes 1179680 | tf_op jit(solution)/shard_map/ppermute | solution.py:40
  717.5 8.6 %collective-permute-done = bf16[2,2,2,96,768]{4,3,0,1,2:T(8,128)(2,1)S(1)} collective-permute-done((bf16[2,2,2,96,768]{4,3,0,1,2:T(8,128)(2,1)}, bf16[2,2,2,96,768]{4,3,0,1,2:T(8,128)(2,1)S(1)}, u32[]{:S(2)}, u32[]{:S(2)}) %collective-permute-start) | collective-permute-done | bytes 1179680 | tf_op jit(solution)/shard_map/ppermute | solution.py:40
  728.7 5.4 collective-permute-start.22
  734.1 3.6 collective-permute-done.13
  737.9 6.8 collective-permute-start.14
  745.7 6.2 collective-permute-start.6
  752.4 4.3 collective-permute-done.14
  757.1 3.0 collective-permute-start.11
  762.2 4.7 collective-permute-done.2
  781.4 37.8 %all-reduce = (f32[1536]{0:T(1024)}, f32[24]{0:T(128)}, f32[1536]{0:T(1024)}) all-reduce(f32[1536]{0:T(1024)S(1)} %get-tuple-element.66, f32[24]{0:T(128)S(1)} %copy-done.46, f32[1536]{0:T(1024)S(1)} %copy-done.39), channel_id=1, replica_groups=mesh['dp'=16,'tensor'=2] {'dp','tensor'}, use_global_device_ids=true, to_apply=%region_18.19 | all-reduce | flops 3096 | bytes 24768 | tf_op jit(solution)/shard_map/psum | solution.py:267
  819.2 7.1 fusion.18
  (344 shorter events, 139.6 us)
Async XLA Ops:
  7.2 103.3 %copy-start = (bf16[768,1536]{1,0:T(8,128)(2,1)S(1)}, bf16[768,1536]{1,0:T(8,128)(2,1)}, u32[]{:S(2)}) copy-start(bf16[768,1536]{1,0:T(8,128)(2,1)} %param.24) | copy-start | bytes 7077892
  7.2 20.6 %all-gather.5.cloned.1.call-start = ((), (), s32[]{:S(2)}) async-start(), calls=%async_computation.4 | async-start | bytes 4718592 | tf_op jit(solution)/shard_map/all_gather | solution.py:162
  12.8 117.7 %reduce-scatter.5.cloned.1.call-start = ((), (), s32[]{:S(2)}) async-start(), calls=%async_computation.5 | async-start | bytes 9437184 | tf_op jit(solution)/shard_map/reduce_scatter | solution.py:184
  115.1 19.9 %copy-start.34 = (f32[1536]{0:T(1024)S(1)}, f32[1536]{0:T(1024)}, u32[]{:S(2)}) copy-start(f32[1536]{0:T(1024)} %param.25) | copy-start | bytes 18436
  115.1 35.7 %all-gather.7.cloned.1.call-start = ((), (), s32[]{:S(2)}) async-start(), calls=%async_computation.6 | async-start | bytes 4718592 | tf_op jit(solution)/shard_map/all_gather | solution.py:191
  133.4 100.9 %copy-start.37 = (f32[512]{0:T(512)}, f32[512]{0:T(512)S(1)}, u32[]{:S(2)}) copy-start(f32[512]{0:T(512)S(1)} %add_rsqrt_fusion) | copy-start | bytes 6148
  136.5 38.0 %all-gather.9.cloned.1.call-start = ((), (), s32[]{:S(2)}) async-start(), calls=%async_computation.8 | async-start | bytes 4718592 | tf_op jit(solution)/shard_map/all_gather | solution.py:201
  137.1 92.8 %reduce-scatter.9.cloned.1.call-start = ((), (), s32[]{:S(2)}) async-start(), calls=%async_computation.9 | async-start | bytes 9437184 | tf_op jit(solution)/shard_map/reduce_scatter | solution.py:209
  214.6 59.5 %all-gather.11.cloned.1.call-start = ((), (), s32[]{:S(2)}) async-start(), calls=%async_computation.10 | async-start | bytes 4718592 | tf_op jit(solution)/shard_map/all_gather | solution.py:220
  238.2 540.7 %reduce-scatter.11.cloned.1.call-start = ((), (), s32[]{:S(2)}) async-start(), calls=%async_computation.11 | async-start | bytes 4718592 | tf_op jit(solution)/shard_map/reduce_scatter | solution.py:254
  253.9 197.7 %collective-permute-start.32 = (bf16[2,2,2,96,1024]{4,3,2,1,0:T(8,128)(2,1)}, bf16[2,2,2,96,1024]{4,3,2,1,0:T(8,128)(2,1)}, u32[]{:S(2)}, u32[]{:S(2)}) collective-permute-start(bf16[2,2,2,96,1024]{4,3,2,1,0:T(8,128)(2,1)} %dynamic-slice_bitcast_fusion), channel_id=1, source_target_pairs={{0,2},{2,0},{4,6},{6,4},{8,10},{10,8},{12,14},{14,12},{16,18},{18,... | collective-permute-start | bytes 4718600 | tf_op jit(solution)/shard_map/ppermute | solution.py:40
  272.6 186.9 %collective-permute-start.36 = (bf16[2,2,2,96,1024]{4,3,0,1,2:T(8,128)(2,1)}, bf16[2,2,2,96,1024]{4,3,0,1,2:T(8,128)(2,1)}, u32[]{:S(2)}, u32[]{:S(2)}) collective-permute-start(bf16[2,2,2,96,1024]{4,3,0,1,2:T(8,128)(2,1)} %bitcast.379), channel_id=1, source_target_pairs={{0,4},{2,6},{4,0},{6,2},{8,12},{10,14},{12,8},{14,10},{16,20},{18,... | collective-permute-start | bytes 4718600 | tf_op jit(solution)/shard_map/ppermute | solution.py:40
  313.5 40.6 %copy-start.27 = (bf16[1024,768]{0,1:T(8,128)(2,1)S(1)}, bf16[1024,768]{0,1:T(8,128)(2,1)}, u32[]{:S(2)}) copy-start(bf16[1024,768]{0,1:T(8,128)(2,1)} %copy-done.26) | copy-start | bytes 4718596
  428.7 390.5 %reduce-scatter.7.cloned.1.call-start = ((), (), s32[]{:S(2)}) async-start(), calls=%async_computation.7 | async-start | bytes 4718592 | tf_op jit(solution)/shard_map/reduce_scatter | solution.py:197
  443.1 107.2 %collective-permute-start.28 = (bf16[2,2,2,96,2048]{4,3,0,1,2:T(8,128)(2,1)}, bf16[2,2,2,96,2048]{4,3,0,1,2:T(8,128)(2,1)}, u32[]{:S(2)}, u32[]{:S(2)}) collective-permute-start(bf16[2,2,2,96,2048]{4,3,0,1,2:T(8,128)(2,1)} %bitcast.377), channel_id=1, source_target_pairs={{0,4},{2,6},{4,0},{6,2},{8,12},{10,14},{12,8},{14,10},{16,20},{18,... | collective-permute-start | bytes 9437192 | tf_op jit(solution)/shard_map/ppermute | solution.py:40
  453.7 75.1 %collective-permute-start.33 = (bf16[2,2,96,1024]{3,2,1,0:T(8,128)(2,1)S(1)}, bf16[2,2,96,1024]{3,2,1,0:T(8,128)(2,1)S(1)}, u32[]{:S(2)}, u32[]{:S(2)}) collective-permute-start(bf16[2,2,96,1024]{3,2,1,0:T(8,128)(2,1)S(1)} %dynamic-slice_bitcast_fusion.4), channel_id=1, source_target_pairs={{0,4},{2,6},{4,0},{6,2},{8,12},{10,14},{12,8},{14,10},{16,20},{18,... | collective-permute-start | bytes 2359304 | tf_op jit(solution)/shard_map/ppermute | solution.py:40
  457.1 74.4 %slice-start = ((s8[6291456]{0:T(1024)(128)(4,1)}), s8[4194304]{0:T(1024)(128)(4,1)S(1)}, s32[]{:S(2)}) async-start(s8[6291456]{0:T(1024)(128)(4,1)} %bitcast.423), calls=%async_computation.12 | async-start | bytes 8388608
  458.9 95.4 %collective-permute-start.24 = (bf16[2,2,2,96,2048]{4,3,0,1,2:T(8,128)(2,1)}, bf16[2,2,2,96,2048]{4,3,0,1,2:T(8,128)(2,1)}, u32[]{:S(2)}, u32[]{:S(2)}) collective-permute-start(bf16[2,2,2,96,2048]{4,3,0,1,2:T(8,128)(2,1)} %bitcast.378), channel_id=1, source_target_pairs={{0,2},{2,0},{4,6},{6,4},{8,10},{10,8},{12,14},{14,12},{16,18},{18,... | collective-permute-start | bytes 9437192 | tf_op jit(solution)/shard_map/ppermute | solution.py:40
  459.5 72.0 %slice-start.1 = ((s8[6291456]{0:T(1024)(128)(4,1)}), s8[2097152]{0:T(1024)(128)(4,1)S(1)}, s32[]{:S(2)}) async-start(s8[6291456]{0:T(1024)(128)(4,1)} %bitcast.423), calls=%async_computation.13 | async-start | bytes 4194304
  462.0 67.2 %copy-start.13 = (bf16[2,2,2,96,1024]{4,3,0,1,2:T(8,128)(2,1)}, bf16[2,2,2,96,1024]{4,3,0,1,2:T(8,128)(2,1)S(1)}, u32[]{:S(2)}) copy-start(bf16[2,2,2,96,1024]{4,3,0,1,2:T(8,128)(2,1)S(1)} %fusion.23) | copy-start | bytes 4718596
  462.0 69.5 %copy-start.62 = (bf16[1024,2048]{1,0:T(8,128)(2,1)S(1)}, bf16[1024,2048]{1,0:T(8,128)(2,1)}, u32[]{:S(2)}) copy-start(bf16[1024,2048]{1,0:T(8,128)(2,1)} %get-tuple-element.90) | copy-start | bytes 12582916
  463.0 81.5 %collective-permute-start.37 = (bf16[2,2,96,1024]{3,2,0,1:T(8,128)(2,1)}, bf16[2,2,96,1024]{3,2,0,1:T(8,128)(2,1)}, u32[]{:S(2)}, u32[]{:S(2)}) collective-permute-start(bf16[2,2,96,1024]{3,2,0,1:T(8,128)(2,1)} %dynamic-slice_bitcast_fusion.3), channel_id=1, source_target_pairs={{0,2},{2,0},{4,6},{6,4},{8,10},{10,8},{12,14},{14,12},{16,18},{18,... | collective-permute-start | bytes 2359304 | tf_op jit(solution)/shard_map/ppermute | solution.py:40
  530.0 17.6 %collective-permute-start.34 = (bf16[2,96,1024]{2,1,0:T(8,128)(2,1)}, bf16[2,96,1024]{2,1,0:T(8,128)(2,1)S(1)}, u32[]{:S(2)}, u32[]{:S(2)}) collective-permute-start(bf16[2,96,1024]{2,1,0:T(8,128)(2,1)} %dynamic-slice_bitcast_fusion.13), channel_id=1, source_target_pairs={{0,8},{2,10},{4,12},{6,14},{8,0},{10,2},{12,4},{14,6},{16,24},{18,... | collective-permute-start | bytes 1179656 | tf_op jit(solution)/shard_map/ppermute | solution.py:40
  546.0 14.4 %collective-permute-start.38 = (bf16[2,96,1024]{2,1,0:T(8,128)(2,1)S(1)}, bf16[2,96,1024]{2,1,0:T(8,128)(2,1)S(1)}, u32[]{:S(2)}, u32[]{:S(2)}) collective-permute-start(bf16[2,96,1024]{2,1,0:T(8,128)(2,1)S(1)} %dynamic-slice_bitcast_fusion.12), channel_id=1, source_target_pairs={{0,8},{2,10},{4,12},{6,14},{8,0},{10,2},{12,4},{14,6},{16,24},{18,... | collective-permute-start | bytes 1179656 | tf_op jit(solution)/shard_map/ppermute | solution.py:40
  547.8 13.6 %collective-permute-start.35 = (bf16[96,1024]{1,0:T(8,128)(2,1)S(1)}, bf16[96,1024]{1,0:T(8,128)(2,1)S(1)}, u32[]{:S(2)}, u32[]{:S(2)}) collective-permute-start(bf16[96,1024]{1,0:T(8,128)(2,1)S(1)} %dynamic-slice_bitcast_fusion.22), channel_id=1, source_target_pairs={{0,16},{2,18},{4,20},{6,22},{8,24},{10,26},{12,28},{14,30},{16,0},... | collective-permute-start | bytes 589832 | tf_op jit(solution)/shard_map/ppermute | solution.py:40
  553.6 33.5 %collective-permute-start.29 = (bf16[2,2,96,2048]{3,2,0,1:T(8,128)(2,1)S(1)}, bf16[2,2,96,2048]{3,2,0,1:T(8,128)(2,1)S(1)}, u32[]{:S(2)}, u32[]{:S(2)}) collective-permute-start(bf16[2,2,96,2048]{3,2,0,1:T(8,128)(2,1)S(1)} %dynamic-slice_bitcast_fusion.1), channel_id=1, source_target_pairs={{0,2},{2,0},{4,6},{6,4},{8,10},{10,8},{12,14},{14,12},{16,18},{18,... | collective-permute-start | bytes 4718600 | tf_op jit(solution)/shard_map/ppermute | solution.py:40
  558.8 33.5 %collective-permute-start.25 = (bf16[2,2,96,2048]{3,2,0,1:T(8,128)(2,1)S(1)}, bf16[2,2,96,2048]{3,2,0,1:T(8,128)(2,1)S(1)}, u32[]{:S(2)}, u32[]{:S(2)}) collective-permute-start(bf16[2,2,96,2048]{3,2,0,1:T(8,128)(2,1)S(1)} %dynamic-slice_bitcast_fusion.2), channel_id=1, source_target_pairs={{0,4},{2,6},{4,0},{6,2},{8,12},{10,14},{12,8},{14,10},{16,20},{18,... | collective-permute-start | bytes 4718600 | tf_op jit(solution)/shard_map/ppermute | solution.py:40
  560.5 9.1 %collective-permute-start.39 = (bf16[96,1024]{1,0:T(8,128)(2,1)S(1)}, bf16[96,1024]{1,0:T(8,128)(2,1)S(1)}, u32[]{:S(2)}, u32[]{:S(2)}) collective-permute-start(bf16[96,1024]{1,0:T(8,128)(2,1)S(1)} %dynamic-slice_bitcast_fusion.21), channel_id=1, source_target_pairs={{0,16},{2,18},{4,20},{6,22},{8,24},{10,26},{12,28},{14,30},{16,0},... | collective-permute-start | bytes 589832 | tf_op jit(solution)/shard_map/ppermute | solution.py:40
  587.8 24.7 %collective-permute-start.30 = (bf16[2,96,2048]{2,1,0:T(8,128)(2,1)S(1)}, bf16[2,96,2048]{2,1,0:T(8,128)(2,1)S(1)}, u32[]{:S(2)}, u32[]{:S(2)}) collective-permute-start(bf16[2,96,2048]{2,1,0:T(8,128)(2,1)S(1)} %dynamic-slice_bitcast_fusion.5), channel_id=1, source_target_pairs={{0,8},{2,10},{4,12},{6,14},{8,0},{10,2},{12,4},{14,6},{16,24},{18,... | collective-permute-start | bytes 2359304 | tf_op jit(solution)/shard_map/ppermute | solution.py:40
  593.1 35.5 %collective-permute-start.26 = (bf16[2,96,2048]{2,1,0:T(8,128)(2,1)S(1)}, bf16[2,96,2048]{2,1,0:T(8,128)(2,1)S(1)}, u32[]{:S(2)}, u32[]{:S(2)}) collective-permute-start(bf16[2,96,2048]{2,1,0:T(8,128)(2,1)S(1)} %dynamic-slice_bitcast_fusion.6), channel_id=1, source_target_pairs={{0,8},{2,10},{4,12},{6,14},{8,0},{10,2},{12,4},{14,6},{16,24},{18,... | collective-permute-start | bytes 2359304 | tf_op jit(solution)/shard_map/ppermute | solution.py:40
  612.8 21.4 %copy-start.7 = (bf16[1024,1536]{1,0:T(8,128)(2,1)S(1)}, bf16[1024,1536]{1,0:T(8,128)(2,1)}, u32[]{:S(2)}) copy-start(bf16[1024,1536]{1,0:T(8,128)(2,1)} %all-gather.5.cloned.1.call-done) | copy-start | bytes 9437188
  612.8 21.4 %copy-start.25 = (bf16[12,64,1024]{2,1,0:T(8,128)(2,1)S(1)}, bf16[12,64,1024]{2,1,0:T(8,128)(2,1)}, u32[]{:S(2)}) copy-start(bf16[12,64,1024]{2,1,0:T(8,128)(2,1)} %multiply_convert_fusion.5) | copy-start | bytes 4718596
  612.9 20.4 %collective-permute-start.31 = (bf16[96,2048]{1,0:T(8,128)(2,1)S(1)}, bf16[96,2048]{1,0:T(8,128)(2,1)S(1)}, u32[]{:S(2)}, u32[]{:S(2)}) collective-permute-start(bf16[96,2048]{1,0:T(8,128)(2,1)S(1)} %dynamic-slice_bitcast_fusion.14), channel_id=1, source_target_pairs={{0,16},{2,18},{4,20},{6,22},{8,24},{10,26},{12,28},{14,30},{16,0},... | collective-permute-start | bytes 1179656 | tf_op jit(solution)/shard_map/ppermute | solution.py:40
  629.7 53.5 %collective-permute-start.27 = (bf16[96,2048]{1,0:T(8,128)(2,1)}, bf16[96,2048]{1,0:T(8,128)(2,1)}, u32[]{:S(2)}, u32[]{:S(2)}) collective-permute-start(bf16[96,2048]{1,0:T(8,128)(2,1)} %dynamic-slice_bitcast_fusion.15), channel_id=1, source_target_pairs={{0,16},{2,18},{4,20},{6,22},{8,24},{10,26},{12,28},{14,30},{16,0},... | collective-permute-start | bytes 1179656 | tf_op jit(solution)/shard_map/ppermute | solution.py:40
  643.1 56.4 %collective-permute-start.20 = (bf16[2,2,2,96,768]{4,3,0,1,2:T(8,128)(2,1)}, bf16[2,2,2,96,768]{4,3,0,1,2:T(8,128)(2,1)}, u32[]{:S(2)}, u32[]{:S(2)}) collective-permute-start(bf16[2,2,2,96,768]{4,3,0,1,2:T(8,128)(2,1)} %bitcast.380), channel_id=1, source_target_pairs={{0,2},{2,0},{4,6},{6,4},{8,10},{10,8},{12,14},{14,12},{16,18},{18,... | collective-permute-start | bytes 3538952 | tf_op jit(solution)/shard_map/ppermute | solution.py:40
  644.5 18.0 %collective-permute-start.16 = (bf16[2,2,2,96,12]{3,4,0,1,2:T(8,128)(2,1)S(1)}, bf16[2,2,2,96,12]{3,4,0,1,2:T(8,128)(2,1)S(1)}, u32[]{:S(2)}, u32[]{:S(2)}) collective-permute-start(bf16[2,2,2,96,12]{3,4,0,1,2:T(8,128)(2,1)S(1)} %bitcast.419), channel_id=1, source_target_pairs={{0,2},{2,0},{4,6},{6,4},{8,10},{10,8},{12,14},{14,12},{16,18},{18,... | collective-permute-start | bytes 55304 | tf_op jit(solution)/shard_map/ppermute | solution.py:40
  656.6 46.7 %collective-permute-start.12 = (bf16[2,2,2,96,768]{4,3,0,1,2:T(8,128)(2,1)}, bf16[2,2,2,96,768]{4,3,0,1,2:T(8,128)(2,1)}, u32[]{:S(2)}, u32[]{:S(2)}) collective-permute-start(bf16[2,2,2,96,768]{4,3,0,1,2:T(8,128)(2,1)} %bitcast.381), channel_id=1, source_target_pairs={{0,4},{2,6},{4,0},{6,2},{8,12},{10,14},{12,8},{14,10},{16,20},{18,... | collective-permute-start | bytes 3538952 | tf_op jit(solution)/shard_map/ppermute | solution.py:40
  662.6 13.4 %collective-permute-start.17 = (bf16[2,2,96,12]{2,3,0,1:T(8,128)(2,1)S(1)}, bf16[2,2,96,12]{2,3,0,1:T(8,128)(2,1)S(1)}, u32[]{:S(2)}, u32[]{:S(2)}) collective-permute-start(bf16[2,2,96,12]{2,3,0,1:T(8,128)(2,1)S(1)} %fusion.64), channel_id=1, source_target_pairs={{0,4},{2,6},{4,0},{6,2},{8,12},{10,14},{12,8},{14,10},{16,20},{18,... | collective-permute-start | bytes 27656 | tf_op jit(solution)/shard_map/ppermute | solution.py:40
  676.0 4.4 collective-permute-start.18
  678.8 26.3 %collective-permute-start.8 = (bf16[2,2,2,96,768]{4,3,0,2,1:T(8,128)(2,1)}, bf16[2,2,2,96,768]{4,3,0,2,1:T(8,128)(2,1)}, u32[]{:S(2)}, u32[]{:S(2)}) collective-permute-start(bf16[2,2,2,96,768]{4,3,0,2,1:T(8,128)(2,1)} %bitcast.382), channel_id=1, source_target_pairs={{0,8},{2,10},{4,12},{6,14},{8,0},{10,2},{12,4},{14,6},{16,24},{18,... | collective-permute-start | bytes 3538952 | tf_op jit(solution)/shard_map/ppermute | solution.py:40
  680.5 16.6 %collective-permute-start.19 = (bf16[96,12]{0,1:T(8,128)(2,1)S(1)}, bf16[96,12]{0,1:T(8,128)(2,1)S(1)}, u32[]{:S(2)}, u32[]{:S(2)}) collective-permute-start(bf16[96,12]{0,1:T(8,128)(2,1)S(1)} %fusion.69), channel_id=1, source_target_pairs={{0,16},{2,18},{4,20},{6,22},{8,24},{10,26},{12,28},{14,30},{16,0},... | collective-permute-start | bytes 6920 | tf_op jit(solution)/shard_map/ppermute | solution.py:40
  686.2 29.2 %collective-permute-start.4 = (bf16[2,2,2,96,768]{4,3,0,1,2:T(8,128)(2,1)}, bf16[2,2,2,96,768]{4,3,0,1,2:T(8,128)(2,1)}, u32[]{:S(2)}, u32[]{:S(2)}) collective-permute-start(bf16[2,2,2,96,768]{4,3,0,1,2:T(8,128)(2,1)} %bitcast.383), channel_id=1, source_target_pairs={{0,4},{2,6},{4,0},{6,2},{8,12},{10,14},{12,8},{14,10},{16,20},{18,... | collective-permute-start | bytes 3538952 | tf_op jit(solution)/shard_map/ppermute | solution.py:40
  697.0 29.1 %collective-permute-start = (bf16[2,2,2,96,768]{4,3,0,1,2:T(8,128)(2,1)}, bf16[2,2,2,96,768]{4,3,0,1,2:T(8,128)(2,1)S(1)}, u32[]{:S(2)}, u32[]{:S(2)}) collective-permute-start(bf16[2,2,2,96,768]{4,3,0,1,2:T(8,128)(2,1)} %bitcast.411), channel_id=1, source_target_pairs={{0,2},{2,0},{4,6},{6,4},{8,10},{10,8},{12,14},{14,12},{16,18},{18,... | collective-permute-start | bytes 3538952 | tf_op jit(solution)/shard_map/ppermute | solution.py:40
  701.1 27.4 %collective-permute-start.21 = (bf16[2,2,96,768]{3,2,0,1:T(8,128)(2,1)S(1)}, bf16[2,2,96,768]{3,2,0,1:T(8,128)(2,1)S(1)}, u32[]{:S(2)}, u32[]{:S(2)}) collective-permute-start(bf16[2,2,96,768]{3,2,0,1:T(8,128)(2,1)S(1)} %dynamic-slice_bitcast_fusion.7), channel_id=1, source_target_pairs={{0,4},{2,6},{4,0},{6,2},{8,12},{10,14},{12,8},{14,10},{16,20},{18,... | collective-permute-start | bytes 1769480 | tf_op jit(solution)/shard_map/ppermute | solution.py:40
  705.0 32.7 %collective-permute-start.13 = (bf16[2,2,96,768]{3,2,0,1:T(8,128)(2,1)S(1)}, bf16[2,2,96,768]{3,2,0,1:T(8,128)(2,1)S(1)}, u32[]{:S(2)}, u32[]{:S(2)}) collective-permute-start(bf16[2,2,96,768]{3,2,0,1:T(8,128)(2,1)S(1)} %dynamic-slice_bitcast_fusion.8), channel_id=1, source_target_pairs={{0,2},{2,0},{4,6},{6,4},{8,10},{10,8},{12,14},{14,12},{16,18},{18,... | collective-permute-start | bytes 1769480 | tf_op jit(solution)/shard_map/ppermute | solution.py:40
  706.7 38.0 %collective-permute-start.9 = (bf16[2,2,96,768]{3,2,0,1:T(8,128)(2,1)S(1)}, bf16[2,2,96,768]{3,2,0,1:T(8,128)(2,1)S(1)}, u32[]{:S(2)}, u32[]{:S(2)}) collective-permute-start(bf16[2,2,96,768]{3,2,0,1:T(8,128)(2,1)S(1)} %dynamic-slice_bitcast_fusion.9), channel_id=1, source_target_pairs={{0,4},{2,6},{4,0},{6,2},{8,12},{10,14},{12,8},{14,10},{16,20},{18,... | collective-permute-start | bytes 1769480 | tf_op jit(solution)/shard_map/ppermute | solution.py:40
  717.0 28.5 %collective-permute-start.5 = (bf16[2,2,96,768]{3,2,0,1:T(8,128)(2,1)S(1)}, bf16[2,2,96,768]{3,2,0,1:T(8,128)(2,1)S(1)}, u32[]{:S(2)}, u32[]{:S(2)}) collective-permute-start(bf16[2,2,96,768]{3,2,0,1:T(8,128)(2,1)S(1)} %dynamic-slice_bitcast_fusion.10), channel_id=1, source_target_pairs={{0,2},{2,0},{4,6},{6,4},{8,10},{10,8},{12,14},{14,12},{16,18},{18,... | collective-permute-start | bytes 1769480 | tf_op jit(solution)/shard_map/ppermute | solution.py:40
  726.5 25.5 %collective-permute-start.1 = (bf16[2,2,96,768]{3,2,0,1:T(8,128)(2,1)S(1)}, bf16[2,2,96,768]{3,2,0,1:T(8,128)(2,1)S(1)}, u32[]{:S(2)}, u32[]{:S(2)}) collective-permute-start(bf16[2,2,96,768]{3,2,0,1:T(8,128)(2,1)S(1)} %dynamic-slice_bitcast_fusion.11), channel_id=1, source_target_pairs={{0,4},{2,6},{4,0},{6,2},{8,12},{10,14},{12,8},{14,10},{16,20},{18,... | collective-permute-start | bytes 1769480 | tf_op jit(solution)/shard_map/ppermute | solution.py:40
  728.7 23.5 %collective-permute-start.22 = (bf16[2,96,768]{2,1,0:T(8,128)(2,1)S(1)}, bf16[2,96,768]{2,1,0:T(8,128)(2,1)S(1)}, u32[]{:S(2)}, u32[]{:S(2)}) collective-permute-start(bf16[2,96,768]{2,1,0:T(8,128)(2,1)S(1)} %dynamic-slice_bitcast_fusion.16), channel_id=1, source_target_pairs={{0,8},{2,10},{4,12},{6,14},{8,0},{10,2},{12,4},{14,6},{16,24},{18,... | collective-permute-start | bytes 884744 | tf_op jit(solution)/shard_map/ppermute | solution.py:40
  737.9 18.8 %collective-permute-start.14 = (bf16[2,96,768]{2,1,0:T(8,128)(2,1)S(1)}, bf16[2,96,768]{2,1,0:T(8,128)(2,1)S(1)}, u32[]{:S(2)}, u32[]{:S(2)}) collective-permute-start(bf16[2,96,768]{2,1,0:T(8,128)(2,1)S(1)} %dynamic-slice_bitcast_fusion.17), channel_id=1, source_target_pairs={{0,8},{2,10},{4,12},{6,14},{8,0},{10,2},{12,4},{14,6},{16,24},{18,... | collective-permute-start | bytes 884744 | tf_op jit(solution)/shard_map/ppermute | solution.py:40
  744.9 12.0 %collective-permute-start.10 = (bf16[2,96,768]{2,1,0:T(8,128)(2,1)S(1)}, bf16[2,96,768]{2,1,0:T(8,128)(2,1)S(1)}, u32[]{:S(2)}, u32[]{:S(2)}) collective-permute-start(bf16[2,96,768]{2,1,0:T(8,128)(2,1)S(1)} %dynamic-slice_bitcast_fusion.18), channel_id=1, source_target_pairs={{0,2},{2,0},{4,6},{6,4},{8,10},{10,8},{12,14},{14,12},{16,18},{18,... | collective-permute-start | bytes 884744 | tf_op jit(solution)/shard_map/ppermute | solution.py:40
  745.7 16.4 %collective-permute-start.6 = (bf16[2,96,768]{2,1,0:T(8,128)(2,1)S(1)}, bf16[2,96,768]{2,1,0:T(8,128)(2,1)S(1)}, u32[]{:S(2)}, u32[]{:S(2)}) collective-permute-start(bf16[2,96,768]{2,1,0:T(8,128)(2,1)S(1)} %dynamic-slice_bitcast_fusion.19), channel_id=1, source_target_pairs={{0,8},{2,10},{4,12},{6,14},{8,0},{10,2},{12,4},{14,6},{16,24},{18,... | collective-permute-start | bytes 884744 | tf_op jit(solution)/shard_map/ppermute | solution.py:40
  752.1 14.8 %collective-permute-start.2 = (bf16[2,96,768]{2,1,0:T(8,128)(2,1)S(1)}, bf16[2,96,768]{2,1,0:T(8,128)(2,1)S(1)}, u32[]{:S(2)}, u32[]{:S(2)}) collective-permute-start(bf16[2,96,768]{2,1,0:T(8,128)(2,1)S(1)} %dynamic-slice_bitcast_fusion.20), channel_id=1, source_target_pairs={{0,8},{2,10},{4,12},{6,14},{8,0},{10,2},{12,4},{14,6},{16,24},{18,... | collective-permute-start | bytes 884744 | tf_op jit(solution)/shard_map/ppermute | solution.py:40
  752.3 16.2 %collective-permute-start.23 = (bf16[96,768]{1,0:T(8,128)(2,1)S(1)}, bf16[96,768]{1,0:T(8,128)(2,1)S(1)}, u32[]{:S(2)}, u32[]{:S(2)}) collective-permute-start(bf16[96,768]{1,0:T(8,128)(2,1)S(1)} %dynamic-slice_bitcast_fusion.23), channel_id=1, source_target_pairs={{0,16},{2,18},{4,20},{6,22},{8,24},{10,26},{12,28},{14,30},{16,0},... | collective-permute-start | bytes 442376 | tf_op jit(solution)/shard_map/ppermute | solution.py:40
  756.8 22.1 %copy-start.4 = (bf16[512,1536]{1,0:T(8,128)(2,1)S(1)}, bf16[512,1536]{1,0:T(8,128)(2,1)}, u32[]{:S(2)}) copy-start(bf16[512,1536]{1,0:T(8,128)(2,1)} %param.15) | copy-start | bytes 4718596
  756.8 22.1 %copy-start.36 = (f32[1536]{0:T(1024)S(1)}, f32[1536]{0:T(1024)}, u32[]{:S(2)}) copy-start(f32[1536]{0:T(1024)} %param.17) | copy-start | bytes 18436
  756.8 22.1 %copy-start.41 = (f32[512]{0:T(512)S(1)}, f32[512]{0:T(512)}, u32[]{:S(2)}) copy-start(f32[512]{0:T(512)} %copy-done.40) | copy-start | bytes 6148
  756.8 15.0 %collective-permute-start.15 = (bf16[96,768]{1,0:T(8,128)(2,1)S(1)}, bf16[96,768]{1,0:T(8,128)(2,1)S(1)}, u32[]{:S(2)}, u32[]{:S(2)}) collective-permute-start(bf16[96,768]{1,0:T(8,128)(2,1)S(1)} %dynamic-slice_bitcast_fusion.24), channel_id=1, source_target_pairs={{0,16},{2,18},{4,20},{6,22},{8,24},{10,26},{12,28},{14,30},{16,0},... | collective-permute-start | bytes 442376 | tf_op jit(solution)/shard_map/ppermute | solution.py:40
  757.1 17.9 %collective-permute-start.11 = (bf16[96,768]{1,0:T(8,128)(2,1)S(1)}, bf16[96,768]{1,0:T(8,128)(2,1)S(1)}, u32[]{:S(2)}, u32[]{:S(2)}) collective-permute-start(bf16[96,768]{1,0:T(8,128)(2,1)S(1)} %dynamic-slice_bitcast_fusion.25), channel_id=1, source_target_pairs={{0,16},{2,18},{4,20},{6,22},{8,24},{10,26},{12,28},{14,30},{16,0},... | collective-permute-start | bytes 442376 | tf_op jit(solution)/shard_map/ppermute | solution.py:40
  762.2 14.4 %collective-permute-start.7 = (bf16[96,768]{1,0:T(8,128)(2,1)S(1)}, bf16[96,768]{1,0:T(8,128)(2,1)S(1)}, u32[]{:S(2)}, u32[]{:S(2)}) collective-permute-start(bf16[96,768]{1,0:T(8,128)(2,1)S(1)} %dynamic-slice_bitcast_fusion.26), channel_id=1, source_target_pairs={{0,16},{2,18},{4,20},{6,22},{8,24},{10,26},{12,28},{14,30},{16,0},... | collective-permute-start | bytes 442376 | tf_op jit(solution)/shard_map/ppermute | solution.py:40
  767.1 52.1 %copy-start.35 = (f32[1536]{0:T(1024)S(1)}, f32[1536]{0:T(1024)}, u32[]{:S(2)}) copy-start(f32[1536]{0:T(1024)} %param.25) | copy-start | bytes 18436
  767.1 52.1 %copy-start.38 = (f32[512]{0:T(512)S(1)}, f32[512]{0:T(512)}, u32[]{:S(2)}) copy-start(f32[512]{0:T(512)} %copy-done.37) | copy-start | bytes 6148
  767.1 52.1 %copy-start.43 = (f32[512]{0:T(512)S(1)}, f32[512]{0:T(512)}, u32[]{:S(2)}) copy-start(f32[512]{0:T(512)} %copy-done.42) | copy-start | bytes 6148
  767.1 11.0 %collective-permute-start.3 = (bf16[96,768]{1,0:T(8,128)(2,1)S(1)}, bf16[96,768]{1,0:T(8,128)(2,1)S(1)}, u32[]{:S(2)}, u32[]{:S(2)}) collective-permute-start(bf16[96,768]{1,0:T(8,128)(2,1)S(1)} %dynamic-slice_bitcast_fusion.27), channel_id=1, source_target_pairs={{0,16},{2,18},{4,20},{6,22},{8,24},{10,26},{12,28},{14,30},{16,0},... | collective-permute-start | bytes 442376 | tf_op jit(solution)/shard_map/ppermute | solution.py:40
  (51 other events, 382.5 us)
Sparse Core Ops, SparseCore 0:
  12.9 14.8 all-gather.4
  115.2 15.2 reduce-scatter.4
  136.6 14.1 all-gather.6
  152.2 13.2 all-gather.8
  214.7 15.1 reduce-scatter.8
  238.3 14.1 all-gather.10
  428.8 10.2 reduce-scatter.10
  539.9 9.3 reduce-scatter.6

commit v2 on v1

v2 whole, which is shorter than its diff:
```python
from functools import partial

import jax
import jax.numpy as jnp
from jax import lax
from jax.experimental import pallas as pl
from jax.experimental.pallas import tpu as pltpu
from jax.sharding import PartitionSpec as P

epsilon = 1e-06
masked_value = -1e30


def matmul(former, latter):
    return jnp.dot(former, latter, preferred_element_type=jnp.float32)


def inner_rows(former, latter):
    return lax.dot_general(
        former, latter, (((0,), (0,)), ((), ())), preferred_element_type=jnp.float32
    )


def against(former, latter):
    return lax.dot_general(
        former, latter, (((1,), (1,)), ((), ())), preferred_element_type=jnp.float32
    )


def norm_scale(matrix):
    return lax.rsqrt(jnp.mean(matrix * matrix, axis=1, keepdims=True) + epsilon)


def norm_back(upstream, normed, scaling, gain_vec):
    weighted = upstream * gain_vec
    return scaling * (weighted - normed * jnp.mean(weighted * normed, axis=1, keepdims=True))


def halve(stacked, bit, axis, wide):
    mine = (lax.axis_index("dp") >> bit) & 1
    count = lax.axis_size("dp")
    sent = lax.ppermute(
        lax.dynamic_index_in_dim(stacked, 1 - mine, axis, keepdims=False),
        "dp",
        [(place, place ^ (1 << bit)) for place in range(count)],
    )
    kept = lax.dynamic_index_in_dim(stacked, mine, axis, keepdims=False)
    total = kept.astype(jnp.float32) + sent.astype(jnp.float32)
    return total if wide else total.astype(jnp.bfloat16)


def spread_sum(gradient, swap):
    count = lax.axis_size("dp")
    bits = count.bit_length() - 1
    order = list(range(bits))
    for front, back in swap:
        order[front], order[back] = order[back], order[front]
    live = list(range(bits - 1, -1, -1))
    stacked = gradient.reshape((2,) * bits + (gradient.shape[0] // count, gradient.shape[1]))
    for place, bit in enumerate(order):
        axis = live.index(bit)
        live.pop(axis)
        stacked = halve(stacked, bit, axis, place == bits - 1)
    return stacked


block_rows = 256
longest_doc = 512
low = jnp.bfloat16
log2e = 1.4426950408889634


def windows(length):
    reach = -(-(longest_doc - 1) // block_rows)
    spans = []
    place = 0
    for one in range(length // block_rows):
        start = max(0, one - reach) * block_rows
        width = (one + 1) * block_rows - start
        spans.append((one * block_rows, start, width, place))
        place += width
    return spans, place


def lane_of(shape):
    return lax.broadcasted_iota(jnp.int32, shape, len(shape) - 1)


def running(rows, back):
    length = rows.shape[1]
    lanes = lane_of(rows.shape)
    step = 1
    while step < length:
        if back:
            moved = jnp.where(lanes < length - step, pltpu.roll(rows, length - step, 1), 0.0)
        else:
            moved = jnp.where(lanes >= step, pltpu.roll(rows, step, 1), 0.0)
        rows = rows + moved
        step *= 2
    return rows


def log_sigmoid(value):
    return jnp.minimum(value, 0.0) - jnp.log1p(jnp.exp(-jnp.abs(value)))


def fill_bias(seg_col, seg_row, bias, spans):
    for first, start, width, place in spans:
        rows = first + lax.broadcasted_iota(jnp.int32, (block_rows, width), 0)
        cols = start + lax.broadcasted_iota(jnp.int32, (block_rows, width), 1)
        same = seg_col[first : first + block_rows, :] == seg_row[:, start : start + width]
        bias[:, place : place + width] = jnp.where((cols <= rows) & same, 0.0, masked_value)


def head_parts(block, head_dim, head, mark):
    lanes = lane_of(block.shape)
    kept = jnp.where(lanes // head_dim == head, block, jnp.zeros_like(block))
    if mark is None:
        return kept
    return jnp.where(lanes == mark, jnp.ones_like(block), kept)


def forward_body(q_ref, k_ref, v_ref, gate_ref, logit_ref, col_ref, row_ref, mixed_ref, gated_ref, peak_ref, bias, fall, *, head_dim, spans, heads):
    pair = pl.program_id(0)

    @pl.when(pair == 0)
    def _():
        fill_bias(col_ref[...], row_ref[...], bias, spans)
        fall[...] = running(log_sigmoid(logit_ref[...]), False) * log2e

    lanes = lane_of((block_rows, q_ref.shape[1]))
    falls = [fall[pl.ds(pair * heads + head, 1), :] for head in range(heads)]
    for first, start, width, place in spans:
        query = q_ref[first : first + block_rows, :]
        key = k_ref[start : start + width, :]
        value = v_ref[start : start + width, :]
        mixed = None
        peaks = None
        for head in range(heads):
            line = falls[head]
            shift = line[:, first : first + 1] - line[:, start : start + width]
            scores = lax.dot_general(
                head_parts(query, head_dim, head, None), key, (((1,), (1,)), ((), ())),
                preferred_element_type=jnp.float32,
            )
            scores = scores * (head_dim**-0.5 * log2e) + shift + bias[:, place : place + width]
            top = jnp.max(scores, axis=1, keepdims=True)
            weight = jnp.exp2(scores - top)
            total = jnp.sum(weight, axis=1, keepdims=True)
            weight = (weight * (1.0 / total)).astype(low)
            part = jnp.dot(weight, head_parts(value, head_dim, head, None), preferred_element_type=jnp.float32)
            peak = jnp.broadcast_to(top + jnp.log2(total), lanes.shape)
            mixed = part if mixed is None else mixed + part
            peaks = peak if peaks is None else jnp.where(lanes // head_dim == head, peak, peaks)
        rows = slice(first, first + block_rows)
        mixed_ref[rows, :] = mixed
        peak_ref[rows, :] = peaks
        gated_ref[rows, :] = (mixed * gate_ref[rows, :]).astype(low)


def attention_sizes(width, head_dim):
    wide = 128 if width % 128 == 0 and 128 % head_dim == 0 else width
    return wide, wide // head_dim


def attend_forward(query, key, value, outgate, logit_t, segment, head_dim):
    length, width = query.shape
    wide, heads = attention_sizes(width, head_dim)
    spans, total = windows(length)
    whole = pl.BlockSpec(memory_space=pltpu.VMEM)
    part = pl.BlockSpec((length, wide), lambda i: (0, i))
    rows = -(-logit_t.shape[0] // 8) * 8
    area = sum(span[2] for span in spans) * block_rows
    return pl.pallas_call(
        partial(forward_body, head_dim=head_dim, spans=spans, heads=heads),
        grid=(width // wide,),
        in_specs=[part, part, part, part, whole, whole, whole],
        out_specs=[part, part, part],
        out_shape=[
            jax.ShapeDtypeStruct((length, width), jnp.float32),
            jax.ShapeDtypeStruct((length, width), low),
            jax.ShapeDtypeStruct((length, width), jnp.float32),
        ],
        scratch_shapes=[
            pltpu.VMEM((block_rows, total), jnp.float32),
            pltpu.VMEM((rows, length), jnp.float32),
        ],
        compiler_params=pltpu.CompilerParams(vmem_limit_bytes=50 * 2**20),
        cost_estimate=pl.CostEstimate(
            flops=16 * area * width, bytes_accessed=20 * length * width, transcendentals=area * width // head_dim
        ),
        name="attend_forward",
    )(query, key, value, outgate, jnp.pad(logit_t, ((0, rows - logit_t.shape[0]), (0, 0))), segment.reshape(length, 1), segment.reshape(1, length))


def backward_body(q_ref, k_ref, v_ref, grad_ref, peak_ref, logit_ref, col_ref, row_ref, dq_ref, dk_ref, dv_ref, forget_ref, bias, fall, key_sum, value_sum, slope, *, head_dim, spans, heads):
    pair = pl.program_id(0)
    wide = q_ref.shape[1]

    @pl.when(pair == 0)
    def _():
        fill_bias(col_ref[...], row_ref[...], bias, spans)
        fall[...] = running(log_sigmoid(logit_ref[...]), False) * log2e
        slope[...] = jnp.zeros_like(slope)

    falls = [fall[pl.ds(pair * heads + head, 1), :] for head in range(heads)]
    scaling = head_dim**-0.5
    value_sum[...] = jnp.zeros_like(value_sum)
    key_sum[...] = jnp.zeros_like(key_sum)
    lanes = lane_of((block_rows, wide))
    slots = lane_of((block_rows, slope.shape[1]))
    marks = [((head + 1) * head_dim) % wide for head in range(heads)]
    for first, start, width, place in spans:
        rows = slice(first, first + block_rows)
        query = q_ref[rows, :]
        key = k_ref[start : start + width, :]
        value = v_ref[start : start + width, :]
        grad = grad_ref[rows, :]
        query_grad = None
        for head in range(heads):
            line = falls[head]
            shift = line[:, first : first + 1] - line[:, start : start + width]
            scores = lax.dot_general(
                head_parts(query, head_dim, head, None), key, (((1,), (1,)), ((), ())),
                preferred_element_type=jnp.float32,
            )
            peak = peak_ref[rows, head * head_dim : head * head_dim + 1]
            scores = scores * (scaling * log2e) + shift + bias[:, place : place + width]
            weight = jnp.exp2(scores - peak)
            own_grad = head_parts(grad, head_dim, head, None)
            rise = lax.dot_general(
                own_grad, value, (((1,), (1,)), ((), ())), preferred_element_type=jnp.float32
            )
            delta = jnp.sum(weight * rise, axis=1, keepdims=True)
            change = (weight * (rise - delta)).astype(low)
            weight = weight.astype(low)
            value_sum[start : start + width, :] += lax.dot_general(
                weight, own_grad, (((0,), (0,)), ((), ())), preferred_element_type=jnp.float32
            )
            mark = marks[head]
            from_key = jnp.dot(change, head_parts(key, head_dim, head, mark), preferred_element_type=jnp.float32)
            key_sum[head, start : start + width, :] += lax.dot_general(
                change, head_parts(query, head_dim, head, mark), (((0,), (0,)), ((), ())),
                preferred_element_type=jnp.float32,
            )
            slope[rows, :] += jnp.where(slots == pair * heads + head, from_key[:, mark : mark + 1], 0.0)
            query_grad = from_key if query_grad is None else jnp.where(lanes // head_dim == head, from_key, query_grad)
        dq_ref[rows, :] = (query_grad * scaling).astype(low)
    length = q_ref.shape[0]
    lanes = lane_of((length, wide))
    slots = lane_of(slope.shape)
    total = key_sum[0]
    gone = jnp.where(slots == pair * heads, total[:, marks[0] : marks[0] + 1], 0.0)
    for head in range(1, heads):
        other = key_sum[head]
        gone += jnp.where(slots == pair * heads + head, other[:, marks[head] : marks[head] + 1], 0.0)
        total = jnp.where(lanes // head_dim == head, other, total)
    slope[...] -= gone
    dk_ref[...] = (total * scaling).astype(low)
    dv_ref[...] = value_sum[...].astype(low)

    @pl.when(pair == pl.num_programs(0) - 1)
    def _():
        count = logit_ref.shape[0]
        turned = slope[...].T[:count, :]
        forget_ref[...] = (running(turned, True) * jax.nn.sigmoid(-logit_ref[...])).astype(low)


def attend_backward(query, key, value, mixed_grad, peaks, logit_t, segment, head_dim):
    length, width = query.shape
    wide, heads = attention_sizes(width, head_dim)
    spans, total = windows(length)
    whole = pl.BlockSpec(memory_space=pltpu.VMEM)
    part = pl.BlockSpec((length, wide), lambda i: (0, i))
    rows = -(-logit_t.shape[0] // 8) * 8
    area = sum(span[2] for span in spans) * block_rows
    return pl.pallas_call(
        partial(backward_body, head_dim=head_dim, spans=spans, heads=heads),
        grid=(width // wide,),
        in_specs=[part, part, part, part, part, whole, whole, whole],
        out_specs=[part, part, part, pl.BlockSpec((rows, length), lambda i: (0, 0))],
        out_shape=[jax.ShapeDtypeStruct((length, width), low)] * 3
        + [jax.ShapeDtypeStruct((rows, length), low)],
        scratch_shapes=[
            pltpu.VMEM((block_rows, total), jnp.float32),
            pltpu.VMEM((rows, length), jnp.float32),
            pltpu.VMEM((heads, length, wide), jnp.float32),
            pltpu.VMEM((length, wide), jnp.float32),
            pltpu.VMEM((length, 128), jnp.float32),
        ],
        compiler_params=pltpu.CompilerParams(vmem_limit_bytes=50 * 2**20),
        cost_estimate=pl.CostEstimate(
            flops=40 * area * width, bytes_accessed=20 * length * width, transcendentals=area * width // head_dim
        ),
        name="attend_backward",
    )(query, key, value, mixed_grad, peaks, jnp.pad(logit_t, ((0, rows - logit_t.shape[0]), (0, 0))), segment.reshape(length, 1), segment.reshape(1, length))


MESH = pl.DeviceIdType.MESH
tile = 256
strip = 64


def greet(other):
    barrier = pltpu.get_barrier_semaphore()
    pl.semaphore_signal(barrier, inc=1, device_id={"tensor": other}, device_id_type=MESH)
    pl.semaphore_wait(barrier, 1)


def over(count, body):
    lax.fori_loop(0, count, lambda place, carry: (body(place), carry)[1], 0)


def span(place, size):
    return pl.ds(pl.multiple_of(place * size, size), size)


def to_other(source, target, sends, arrivals, place, other):
    return pltpu.make_async_remote_copy(
        src_ref=source,
        dst_ref=target,
        send_sem=sends.at[place],
        recv_sem=arrivals.at[place],
        device_id={"tensor": other},
        device_id_type=MESH,
    )


def scale_of(rows):
    return lax.rsqrt(jnp.mean(rows * rows, axis=1, keepdims=True) + epsilon)


def strip_copies(held, full, own, far, near, arrivals, place, me, other):
    half = held.shape[0]
    rows = span(place, strip)
    into = pl.ds(pl.multiple_of(me * half + place * strip, strip), strip)
    remote = to_other(held.at[rows], full.at[into], far, arrivals, place, other)
    return remote, pltpu.make_async_copy(held.at[rows], full.at[into], near.at[place])


def gather_body(token_ref, gain_ref, full_ref, held, far, near, arrivals):
    me = lax.axis_index("tensor")
    other = 1 - me
    greet(other)
    count = held.shape[0] // strip
    copies = lambda place: strip_copies(held, full_ref, me, far, near, arrivals, place, me, other)

    def step(place):
        rows = span(place, strip)
        values = token_ref[rows, :].astype(jnp.float32)
        held[rows, :] = (values * scale_of(values) * gain_ref[...]).astype(low)
        for copy in copies(place):
            copy.start()

    over(count, step)

    def finish(place):
        for copy in copies(place):
            copy.wait()

    over(count, finish)


def exchange_products(product, send, recv, total, sends, arrivals, me, other):
    half = total.shape[0]
    count = total.shape[1] // tile
    copy = lambda place: to_other(send.at[place], recv.at[place], sends, arrivals, place, other)

    def away(place):
        send[place] = product(span(other, half), place).astype(low)
        copy(place).start()

    def home(place):
        columns = span(place, tile)
        total[:, columns] = product(span(me, half), place)
        copy(place).wait()
        total[:, columns] += recv[place].astype(jnp.float32)

    over(count, away)
    over(count, home)


def project_body(gated_ref, weight_ref, token_ref, cot_ref, gain_ref, middle_ref, full_ref, up_ref, send, recv, held, sends, arrivals, far, near, landed, up_sems):
    me = lax.axis_index("tensor")
    other = 1 - me
    greet(other)
    half = token_ref.shape[0]
    up_far = pltpu.make_async_remote_copy(
        src_ref=cot_ref, dst_ref=up_ref.at[span(me, half)], send_sem=up_sems.at[0], recv_sem=up_sems.at[1],
        device_id={"tensor": other}, device_id_type=MESH,
    )
    up_near = pltpu.make_async_copy(cot_ref, up_ref.at[span(me, half)], up_sems.at[2])
    up_near.start()

    def product(rows, place):
        return jnp.dot(gated_ref[rows, :], weight_ref[:, span(place, tile)], preferred_element_type=jnp.float32)

    exchange_products(product, send, recv, middle_ref, sends, arrivals, me, other)
    up_far.start()
    count = half // strip
    copies = lambda place: strip_copies(held, full_ref, me, far, near, landed, place, me, other)

    def step(place):
        rows = span(place, strip)
        middle = token_ref[rows, :].astype(jnp.float32) + middle_ref[rows, :]
        middle_ref[rows, :] = middle
        held[rows, :] = (middle * scale_of(middle) * gain_ref[...]).astype(low)
        for copy in copies(place):
            copy.start()

    over(count, step)

    def finish(place):
        for copy in copies(place):
            copy.wait()

    over(count, finish)
    up_near.wait()
    up_far.wait()


def result_body(hidden_ref, weight_ref, middle_ref, result_ref, send, recv, total, sends, arrivals):
    me = lax.axis_index("tensor")
    other = 1 - me
    greet(other)

    def product(rows, place):
        return jnp.dot(hidden_ref[rows, :], weight_ref[:, span(place, tile)], preferred_element_type=jnp.float32)

    exchange_products(product, send, recv, total, sends, arrivals, me, other)

    def step(place):
        rows = span(place, strip)
        result_ref[rows, :] = (total[rows, :] + middle_ref[rows, :]).astype(low)

    over(total.shape[0] // strip, step)


def nt(former, latter):
    return lax.dot_general(former, latter, (((1,), (1,)), ((), ())), preferred_element_type=jnp.float32)


def back_body(gate_ref, up_ref, gate_weight_ref, up_weight_ref, middle_ref, cot_ref, gain_ref, out_ref, full_ref, part_ref, send, recv, total, held, sends, arrivals, far, near, landed):
    me = lax.axis_index("tensor")
    other = 1 - me
    greet(other)

    def product(rows, place):
        columns = span(place, tile)
        return nt(gate_ref[rows, :], gate_weight_ref[columns, :]) + nt(up_ref[rows, :], up_weight_ref[columns, :])

    exchange_products(product, send, recv, total, sends, arrivals, me, other)
    part_ref[...] = jnp.zeros_like(part_ref)
    count = total.shape[0] // strip
    copies = lambda place: strip_copies(held, full_ref, me, far, near, landed, place, me, other)

    def step(place):
        rows = span(place, strip)
        middle = middle_ref[rows, :]
        scale = scale_of(middle)
        normed = middle * scale
        upstream = total[rows, :]
        weighted = upstream * gain_ref[...]
        push = scale * (weighted - normed * jnp.mean(weighted * normed, axis=1, keepdims=True))
        grad = cot_ref[rows, :].astype(jnp.float32) + push
        out_ref[rows, :] = grad
        held[rows, :] = grad.astype(low)
        for copy in copies(place):
            copy.start()
        part_ref[...] += jnp.sum((upstream * normed).reshape(strip // 8, 8, -1), axis=0)

    over(count, step)

    def finish(place):
        for copy in copies(place):
            copy.wait()

    over(count, finish)


def first_body(query_ref, key_ref, value_ref, gate_ref, forget_ref, wq_ref, wk_ref, wv_ref, wg_ref, wf_ref, grad_ref, token_ref, gain_ref, out_ref, part_ref, send, recv, total, sends, arrivals):
    me = lax.axis_index("tensor")
    other = 1 - me
    greet(other)

    def product(rows, place):
        columns = span(place, tile)
        value = nt(query_ref[rows, :], wq_ref[columns, :]) + nt(key_ref[rows, :], wk_ref[columns, :])
        value = value + nt(value_ref[rows, :], wv_ref[columns, :]) + nt(gate_ref[rows, :], wg_ref[columns, :])
        return value + lax.dot_general(
            forget_ref[:, rows], wf_ref[:, columns], (((0,), (0,)), ((), ())), preferred_element_type=jnp.float32
        )

    exchange_products(product, send, recv, total, sends, arrivals, me, other)
    part_ref[...] = jnp.zeros_like(part_ref)

    def step(place):
        rows = span(place, strip)
        values = token_ref[rows, :].astype(jnp.float32)
        scale = scale_of(values)
        normed = values * scale
        upstream = total[rows, :]
        weighted = upstream * gain_ref[...]
        push = scale * (weighted - normed * jnp.mean(weighted * normed, axis=1, keepdims=True))
        out_ref[rows, :] = grad_ref[rows, :] + push
        part_ref[...] += jnp.sum((upstream * normed).reshape(strip // 8, 8, -1), axis=0)

    over(total.shape[0] // strip, step)


def all_sum_body(bits, part_ref, out_ref, slots, sends, arrivals):
    out_ref[...] = part_ref[...]
    places = {}
    for axis in ("dp", "tensor"):
        places[axis] = lax.axis_index(axis)
    partners = []
    for axis, bit in bits:
        here = places[axis]
        flip = here + (1 << bit) - 2 * (1 << bit) * (here // (1 << bit) % 2)
        partners.append({axis: flip})
    barrier = pltpu.get_barrier_semaphore()
    for partner in partners:
        pl.semaphore_signal(barrier, inc=1, device_id=partner, device_id_type=MESH)
    pl.semaphore_wait(barrier, len(partners))
    for place, partner in enumerate(partners):
        copy = pltpu.make_async_remote_copy(
            src_ref=slots.at[2 * place], dst_ref=slots.at[2 * place + 1], send_sem=sends.at[place],
            recv_sem=arrivals.at[place], device_id=partner, device_id_type=MESH,
        )
        slots[2 * place] = out_ref[...]
        copy.start()
        copy.wait()
        out_ref[...] += slots[2 * place + 1]


vmem = pl.BlockSpec(memory_space=pltpu.VMEM)
anywhere = pl.BlockSpec(memory_space=pl.ANY)
dma = pltpu.SemaphoreType.DMA


def comm_params(identity):
    return pltpu.CompilerParams(collective_id=identity, has_side_effects=True, vmem_limit_bytes=60 * 2**20)


def norm_gather(tokens, gain):
    half, width = tokens.shape
    count = half // strip
    return pl.pallas_call(
        gather_body,
        out_shape=jax.ShapeDtypeStruct((2 * half, width), low),
        in_specs=[vmem, vmem],
        out_specs=anywhere,
        scratch_shapes=[pltpu.VMEM((half, width), low), dma((count,)), dma((count,)), dma((count,))],
        compiler_params=comm_params(0),
        cost_estimate=pl.CostEstimate(flops=8 * half * width, bytes_accessed=12 * half * width, transcendentals=half),
        name="norm_gather",
    )(tokens, gain.reshape(1, width))


def exchange_scratch(half, width):
    count = width // tile
    return [pltpu.VMEM((count, half, tile), low), pltpu.VMEM((count, half, tile), low)], [dma((count,)), dma((count,))]


def project(gated, weight, tokens, cotangent, gain):
    half, width = tokens.shape
    count = half // strip
    buffers, sems = exchange_scratch(half, width)
    return pl.pallas_call(
        project_body,
        out_shape=[
            jax.ShapeDtypeStruct((half, width), jnp.float32),
            jax.ShapeDtypeStruct((2 * half, width), low),
            jax.ShapeDtypeStruct((2 * half, width), low),
        ],
        in_specs=[vmem] * 5,
        out_specs=[vmem, anywhere, anywhere],
        scratch_shapes=buffers + [pltpu.VMEM((half, width), low)] + sems + [dma((count,)), dma((count,)), dma((count,)), dma((3,))],
        compiler_params=comm_params(1),
        cost_estimate=pl.CostEstimate(flops=4 * half * width * weight.shape[0], bytes_accessed=24 * half * width, transcendentals=half),
        name="project",
    )(gated, weight, tokens, cotangent, gain.reshape(1, width))


def result_rows(hidden, weight, middle):
    half, width = middle.shape
    buffers, sems = exchange_scratch(half, width)
    return pl.pallas_call(
        result_body,
        out_shape=jax.ShapeDtypeStruct((half, width), low),
        in_specs=[vmem] * 3,
        out_specs=vmem,
        scratch_shapes=buffers + [pltpu.VMEM((half, width), jnp.float32)] + sems,
        compiler_params=comm_params(2),
        cost_estimate=pl.CostEstimate(flops=4 * half * width * weight.shape[0], bytes_accessed=30 * half * width, transcendentals=0),
        name="result_rows",
    )(hidden, weight, middle)


def middle_back(gate_grad, up_grad, gate_weight, up_weight, middle, cotangent, gain):
    half, width = middle.shape
    count = half // strip
    buffers, sems = exchange_scratch(half, width)
    return pl.pallas_call(
        back_body,
        out_shape=[
            jax.ShapeDtypeStruct((half, width), jnp.float32),
            jax.ShapeDtypeStruct((2 * half, width), low),
            jax.ShapeDtypeStruct((8, width), jnp.float32),
        ],
        in_specs=[vmem] * 7,
        out_specs=[vmem, anywhere, vmem],
        scratch_shapes=buffers
        + [pltpu.VMEM((half, width), jnp.float32), pltpu.VMEM((half, width), low)]
        + sems
        + [dma((count,)), dma((count,)), dma((count,))],
        compiler_params=comm_params(3),
        cost_estimate=pl.CostEstimate(flops=8 * half * width * gate_weight.shape[1], bytes_accessed=50 * half * width, transcendentals=half),
        name="middle_back",
    )(gate_grad, up_grad, gate_weight, up_weight, middle, cotangent, gain.reshape(1, width))


def first_back(query_grad, key_grad, value_grad, outgate_grad, forget_grad, weights, forget_t, middle_grad, tokens, gain):
    half, width = tokens.shape
    buffers, sems = exchange_scratch(half, width)
    return pl.pallas_call(
        first_body,
        out_shape=[
            jax.ShapeDtypeStruct((half, width), jnp.float32),
            jax.ShapeDtypeStruct((8, width), jnp.float32),
        ],
        in_specs=[vmem] * 13,
        out_specs=[vmem, vmem],
        scratch_shapes=buffers + [pltpu.VMEM((half, width), jnp.float32)] + sems,
        compiler_params=comm_params(4),
        cost_estimate=pl.CostEstimate(flops=16 * half * width * query_grad.shape[1], bytes_accessed=40 * half * width, transcendentals=half),
        name="first_back",
    )(query_grad, key_grad, value_grad, outgate_grad, forget_grad, *weights, forget_t, middle_grad, tokens, gain.reshape(1, width))


def all_sum(part):
    bits = [("tensor", bit) for bit in range(lax.axis_size("tensor").bit_length() - 1)]
    bits += [("dp", bit) for bit in range(lax.axis_size("dp").bit_length() - 1)]
    return pl.pallas_call(
        partial(all_sum_body, bits),
        out_shape=jax.ShapeDtypeStruct(part.shape, part.dtype),
        in_specs=[vmem],
        out_specs=vmem,
        scratch_shapes=[pltpu.VMEM((2 * len(bits),) + part.shape, part.dtype), dma((len(bits),)), dma((len(bits),))],
        compiler_params=comm_params(5),
        name="all_sum",
    )(part)


def local(
    tokens,
    segment_ids,
    first_gain,
    query_weight,
    key_weight,
    value_weight,
    outgate_weight,
    forget_weight,
    forget_bias,
    output_weight,
    second_gain,
    gate_weight,
    up_weight,
    down_weight,
    cotangent,
):
    local_heads = forget_weight.shape[1]
    head_dim = query_weight.shape[1] // local_heads
    paired = lax.axis_size("tensor") == 2
    segment = segment_ids[0]
    gather = partial(lax.all_gather, axis_name="tensor", axis=0, tiled=True)
    scatter = partial(lax.psum_scatter, axis_name="tensor", scatter_dimension=0, tiled=True)

    if paired:
        first_all = norm_gather(tokens, first_gain)
    else:
        inputs = tokens.astype(jnp.float32)
        scale_one = norm_scale(inputs)
        normed_one = inputs * scale_one
        first_all = gather((normed_one * first_gain).astype(low))
    query_rows = matmul(first_all, query_weight).astype(low)
    key_rows = matmul(first_all, key_weight).astype(low)
    value_rows = matmul(first_all, value_weight).astype(low)
    outgate = jax.nn.sigmoid(matmul(first_all, outgate_weight))
    logit_t = lax.dot_general(
        forget_weight, first_all, (((0,), (1,)), ((), ())), preferred_element_type=jnp.float32
    ) + forget_bias[:, None]
    mixed_out, gated_out, peaks = attend_forward(
        query_rows, key_rows, value_rows, outgate, logit_t, segment, head_dim
    )
    if paired:
        middle, second_all, upstream = project(gated_out, output_weight, tokens, cotangent, second_gain)
    else:
        middle = inputs + scatter(matmul(gated_out, output_weight))
        scale_two = norm_scale(middle)
        normed_two = middle * scale_two
        second_all = gather((normed_two * second_gain).astype(low))
        upstream = gather(cotangent)
    gate_pre = matmul(second_all, gate_weight)
    up_pre = matmul(second_all, up_weight)
    sigmoid_gate = jax.nn.sigmoid(gate_pre)
    swish_out = gate_pre * sigmoid_gate
    hidden = (swish_out * up_pre).astype(low)
    along, across, deep = (), ((0, 1),), ((0, 2),)
    half = hidden.shape[1] // 2
    down_front = inner_rows(upstream, hidden[:, :half]).astype(low)
    down_back = inner_rows(upstream, hidden[:, half:]).astype(low)
    hidden_grad = against(upstream, down_weight)
    gate_grad = (
        hidden_grad * up_pre * sigmoid_gate * (1.0 + gate_pre * (1.0 - sigmoid_gate))
    ).astype(low)
    up_grad = (hidden_grad * swish_out).astype(low)
    gate_grad, up_grad, down_front, down_back = lax.optimization_barrier(
        (gate_grad, up_grad, down_front, down_back)
    )
    grad_gate = inner_rows(second_all, gate_grad).astype(low)
    grad_up = inner_rows(second_all, up_grad).astype(low)
    gate_grad, up_grad, grad_gate, grad_up = lax.optimization_barrier(
        (gate_grad, up_grad, grad_gate, grad_up)
    )
    if paired:
        middle_grad, middle_all, gain_two_part = middle_back(
            gate_grad, up_grad, gate_weight, up_weight, middle, cotangent, second_gain
        )
    else:
        second_grad = scatter(against(gate_grad, gate_weight) + against(up_grad, up_weight))
        middle_grad = cotangent.astype(jnp.float32) + norm_back(
            second_grad, normed_two, scale_two, second_gain
        )
        gain_two_part = jnp.sum(second_grad * normed_two, axis=0, keepdims=True)
        middle_all = gather(middle_grad.astype(low))
    grad_output = inner_rows(middle_all, gated_out).astype(low)
    gated_grad = against(middle_all, output_weight)
    mixed_grad = (gated_grad * outgate).astype(low)
    outgate_grad = (gated_grad * mixed_out * outgate * (1.0 - outgate)).astype(low)
    grad_outgate = inner_rows(first_all, outgate_grad).astype(low)
    mixed_grad, grad_output, grad_outgate = lax.optimization_barrier(
        (mixed_grad, grad_output, grad_outgate)
    )
    query_grad, key_grad, value_grad, forget_rows = attend_backward(
        query_rows, key_rows, value_rows, mixed_grad, peaks, logit_t, segment, head_dim
    )
    grad_query = inner_rows(first_all, query_grad).astype(low)
    grad_key = inner_rows(first_all, key_grad).astype(low)
    grad_value = inner_rows(first_all, value_grad).astype(low)
    forget_grad = forget_rows[:local_heads]
    grad_forget = lax.dot_general(
        first_all, forget_grad, (((0,), (1,)), ((), ())), preferred_element_type=jnp.float32
    ).astype(low)
    bias_part = jnp.sum(forget_grad.astype(jnp.float32), axis=1)
    forget_t = forget_weight.T
    if paired:
        forget_t = jnp.pad(forget_t, ((0, forget_rows.shape[0] - local_heads), (0, 0)))
        weights = (query_weight, key_weight, value_weight, outgate_weight)
        tokens_grad, gain_one_part = first_back(
            query_grad, key_grad, value_grad, outgate_grad, forget_rows, weights, forget_t,
            middle_grad, tokens, first_gain,
        )
    else:
        total = against(query_grad, query_weight)
        total = total + against(key_grad, key_weight)
        total = total + against(value_grad, value_weight)
        total = total + against(outgate_grad, outgate_weight)
        total = total + inner_rows(forget_grad, forget_t)
        first_grad = scatter(total.astype(low)).astype(jnp.float32)
        tokens_grad = middle_grad + norm_back(first_grad, normed_one, scale_one, first_gain)
        gain_one_part = jnp.sum(first_grad * normed_one, axis=0, keepdims=True)
    all_heads = local_heads * lax.axis_size("tensor")
    placed = lax.dynamic_update_slice(
        jnp.zeros((1, tokens.shape[1]), jnp.float32),
        bias_part[None],
        (0, lax.axis_index("tensor") * local_heads),
    )
    shares = jnp.concatenate(
        [
            jnp.sum(gain_one_part, axis=0, keepdims=True),
            jnp.sum(gain_two_part, axis=0, keepdims=True),
            placed,
            jnp.zeros((5, tokens.shape[1]), jnp.float32),
        ]
    )
    sums = all_sum(shares)
    width = grad_query.shape[1]
    query_part = spread_sum(jnp.concatenate([grad_query, grad_forget], axis=1), along)
    return (
        result_rows(hidden, down_weight, middle)
        if paired
        else (middle + scatter(matmul(hidden, down_weight).astype(low)).astype(jnp.float32)).astype(low),
        tokens_grad,
        sums[0],
        query_part[:, :width],
        spread_sum(grad_key, across),
        spread_sum(grad_value, deep),
        spread_sum(grad_outgate, across),
        query_part[:, width:],
        sums[2, :all_heads],
        spread_sum(grad_output, along).T,
        sums[1],
        spread_sum(grad_gate, along),
        spread_sum(grad_up, across),
        jnp.concatenate([spread_sum(down_front, along), spread_sum(down_back, across)], axis=1).T,
    )


def solution(mesh):
    in_specs = (
        P(("dp", "tensor"), None),
        P("dp", None),
        P(),
        P(None, "tensor"),
        P(None, "tensor"),
        P(None, "tensor"),
        P(None, "tensor"),
        P(None, "tensor"),
        P("tensor"),
        P("tensor", None),
        P(),
        P(None, "tensor"),
        P(None, "tensor"),
        P("tensor", None),
        P(("dp", "tensor"), None),
    )
    out_specs = (
        P(("dp", "tensor"), None),
        P(("dp", "tensor"), None),
        P(),
        P("dp", "tensor"),
        P("dp", "tensor"),
        P("dp", "tensor"),
        P("dp", "tensor"),
        P("dp", "tensor"),
        P(),
        P("tensor", "dp"),
        P(),
        P("dp", "tensor"),
        P("dp", "tensor"),
        P("tensor", "dp"),
    )
    return jax.shard_map(local, mesh=mesh, in_specs=in_specs, out_specs=out_specs, check_vma=False)
```

time: 844 us -> 650 us (0.77)
  matrix products: 292 us -> 116 us
  Pallas kernels: 0 us -> 164 us
  other arithmetic: 126 us -> 31.3 us
  blocking collectives: 37.8 us -> 0 us
  starting transfers between devices: 63.5 us -> 33.8 us
  between operations: 15.7 us -> 1.97 us
  waiting for transfers between devices: 249 us -> 236 us
  local copies, waits for them, and re-layouts: 49.5 us -> 59.4 us
    pallas_call x0 -> x8, Pallas kernels: none -> 164 us  [the longest x1 34.1 us: attend_backward(): pl.pallas_call(partial(backward_body, head_dim=head_dim, spans=spans, hea...]
    dot_general x6 -> x2, matrix products: 118 us -> 3.3 us  [the longest x1 2.8 us: local(): lax.dot_general(forget_weight, first_all, (((0,), (1,)), ((), ())), prefe...]
    reduce_sum x7 -> x3, other arithmetic: 72.1 us -> 0.97 us  [the longest x1 0.82 us: local(): jnp.sum(gain_one_part, axis=0, keepdims=True)]
    dot_general x9 -> x2, matrix products: 68.5 us -> 21.6 us  [against(): lax.dot_general(former, latter, (((1,), (1,)), ((), ())), preferred_eleme...]
    ppermute x40 -> x36, waiting for transfers between devices: 190 us -> 236 us  [halve(): lax.ppermute(lax.dynamic_index_in_dim(stacked, 1 - mine, axis, keepdims=F...]
    psum x1 -> x0, blocking collectives: 37.8 us -> none  [local(): lax.psum((gain_one_part, gain_two_part, placed), ('dp', 'tensor'))]
    reduce_scatter x4 -> x0, waiting for transfers between devices: 30.6 us -> none  [the longest x1 15.3 us: local(): lax.psum_scatter(matmul(gated_out, output_weight), 'tensor', scatter_dime...]
    ppermute x40 -> x36, starting transfers between devices: 63.1 us -> 33.8 us  [halve(): lax.ppermute(lax.dynamic_index_in_dim(stacked, 1 - mine, axis, keepdims=F...]
  transfers between devices with their start and end apart: 48 -> 36, of which waited for: 25 -> 23; matrix products, arithmetic and copies ran while one was open for 37% -> 19% of each run, Pallas kernels for 0% -> 19%
where the time goes in v2:
time: 650 us; the launch traced here: 642 us
  waiting for transfers between devices  236 us (36%)
  Pallas kernels  164 us (25%)
  matrix products  116 us (18%)
  local copies, waits for them, and re-layouts  59.4 us (9%)
  starting transfers between devices  33.8 us (5%)
  other arithmetic  31.3 us (5%)
    ppermute x36, waiting for transfers between devices, halve(): lax.ppermute(lax.dynamic_index_in_dim(stacked, 1 - mine, axis, keepdims=F...  236 us
    dot_general x9, matrix products, inner_rows(): lax.dot_general(former, latter, (((0,), (0,)), ((), ())), preferred_eleme...  50.6 us
    dot_general x6, matrix products, matmul(): return jnp.dot(former, latter, preferred_element_type=jnp.float32)  40 us
    pallas_call x1, Pallas kernels, attend_backward(): pl.pallas_call(partial(backward_body, head_dim=head_dim, spans=spans, hea...  34.1 us
    ppermute x36, starting transfers between devices, halve(): lax.ppermute(lax.dynamic_index_in_dim(stacked, 1 - mine, axis, keepdims=F...  33.8 us
    pallas_call x1, Pallas kernels, middle_back(): pl.pallas_call(back_body, out_shape=[jax.ShapeDtypeStruct((half, width),...  30 us
    dynamic_slice x7, local copies, waits for them, and re-layouts, halve(): kept = lax.dynamic_index_in_dim(stacked, mine, axis, keepdims=False)  26.5 us
    pallas_call x1, Pallas kernels, first_back(): pl.pallas_call(first_body, out_shape=[jax.ShapeDtypeStruct((half, width),...  24 us
  transfers between devices with their start and end apart: 36, of which 23 were waited for; matrix products, arithmetic and copies ran while one was open for 19% of the time, Pallas kernels for 19%

profile of v2, /device:TPU:0, one launch (start us, length us, event | category | flops | bytes accessed | tf_op | source)
XLA Modules:
  0.0 641.5 jit_solution(4267548946427933604)
XLA Ops:
  1.9 5.6 norm_gather.1
  7.6 6.6 %add_divide_fusion.1.gate_ref = f32[1024,768]{1,0:T(8,128)} fusion(bf16[1024,1536]{1,0:T(8,128)(2,1)} %norm_gather.1, bf16[1536,768]{1,0:T(8,128)(2,1)S(1)} %copy-done.34), kind=kOutput, calls=%fused_computation.32 | convolution fusion | flops 2418278400 | bytes 8650752 | tf_op jit(solution)/shard_map/dot_general | solution.py:15
  14.1 3.7 convolution_convert_fusion.10.v_ref
  17.9 3.7 convolution_convert_fusion.11.k_ref
  21.5 2.6 convolution_convert_fusion.12.q_ref
  25.2 2.8 fusion.23
  28.1 20.7 %attend_forward.1 = (f32[1024,768]{1,0:T(8,128)}, bf16[1024,768]{1,0:T(8,128)(2,1)S(1)}, f32[1024,768]{1,0:T(8,128)}) custom-call(bf16[1024,768]{1,0:T(8,128)(2,1)S(1)} %convolution_convert_fusion.12.q_ref, bf16[1024,768]{1,0:T(8,128)(2,1)} %convolution_convert_fusion.11.k_ref, bf16[1024,768]{1,0:T(8,128)(2,1)} %convolution_convert_fusion.10.v_ref, ...), custom_call_target="tpu_custom_call" | custom-call | flops 7247757312 | bytes 15728640 | tf_op jit(solution)/shard_map/attend_forward/pallas_call | solution.py:174
  49.9 15.9 %project.1 = (f32[512,1536]{1,0:T(8,128)}, bf16[1024,1536]{1,0:T(8,128)(2,1)}, bf16[1024,1536]{1,0:T(8,128)(2,1)}) custom-call(bf16[1024,768]{1,0:T(8,128)(2,1)} %copy-done.2, bf16[768,1536]{1,0:T(8,128)(2,1)} %weight_ref.2, bf16[512,1536]{1,0:T(8,128)(2,1)} %token_ref.5, bf16[512,1536]{1,0:T(8,128)(2,1)} %cot_ref.3, f32[1,1536]{1,0:T(1,128)} %reshape.137.gain_ref), custom_call_target="tpu_custom_call" | custom-call | flops 2415919104 | bytes 18874368 | tf_op jit(solution)/shard_map/project/pallas_call | solution.py:569
  65.8 12.6 %fusion.33 = f32[1024,2048]{1,0:T(8,128)} fusion(bf16[1024,1536]{1,0:T(8,128)(2,1)} %get-tuple-element.41, bf16[1536,2048]{1,0:T(8,128)(2,1)} %gate_weight_ref.1), kind=kOutput, calls=%fused_computation.157 | convolution fusion | flops 6442450944 | bytes 17825792 | tf_op jit(solution)/shard_map/dot_general | solution.py:15
  78.4 10.9 %fusion.34 = f32[1024,2048]{1,0:T(8,128)} fusion(bf16[1024,1536]{1,0:T(8,128)(2,1)S(1)} %copy-done.35, bf16[1536,2048]{1,0:T(8,128)(2,1)} %up_weight_ref.1), kind=kOutput, calls=%fused_computation.158 | convolution fusion | flops 6442450944 | bytes 17825792 | tf_op jit(solution)/shard_map/dot_general | solution.py:15
  89.2 17.6 %multiply_convert_fusion = (bf16[1024,2048]{1,0:T(8,128)(2,1)}, bf16[1024,2048]{1,0:T(8,128)(2,1)}, bf16[1024,2048]{1,0:T(8,128)(2,1)}) fusion(f32[1024,2048]{1,0:T(8,128)} %fusion.33, f32[1024,2048]{1,0:T(8,128)} %fusion.34, bf16[1024,1536]{1,0:T(8,128)(2,1)S(1)} %copy-done.37, bf16[2048,1536]{1,0:T(8,128)(2,1)} %weight_ref.3), kind=kOutput, calls=%fused_computation | convolution fusion | flops 6473908224 | bytes 38797312 | tf_op jit(solution)/shard_map/dot_general | solution.py:25
  106.8 6.7 %convolution_convert_fusion.2 = bf16[1536,1024]{1,0:T(8,128)(2,1)} fusion(bf16[1024,1536]{1,0:T(8,128)(2,1)S(1)} %copy-done.37, bf16[1024,2048]{1,0:T(8,128)(2,1)} %get-tuple-element.98.hidden_ref), kind=kOutput, calls=%fused_computation.11 | convolution fusion | flops 3222798336 | bytes 8388608 | tf_op jit(solution)/shard_map/dot_general | solution.py:19
  113.4 4.9 convolution_convert_fusion.3
  118.3 3.4 constant_dynamic-slice_fusion.3
  123.1 2.8 collective-permute-start.28
  125.9 3.6 constant_dynamic-slice_fusion.1
  132.3 9.2 %convolution_convert_fusion = bf16[1536,2048]{1,0:T(8,128)(2,1)} fusion(bf16[1024,1536]{1,0:T(8,128)(2,1)S(1)} %copy-done.36, bf16[1024,2048]{1,0:T(8,128)(2,1)S(1)} %copy-done.43), kind=kOutput, calls=%fused_computation.5 | convolution fusion | flops 6445596672 | bytes 13631488 | tf_op jit(solution)/shard_map/dot_general | solution.py:19
  141.4 8.8 %convolution_convert_fusion.1 = bf16[1536,2048]{1,0:T(8,128)(2,1)} fusion(bf16[1024,1536]{1,0:T(8,128)(2,1)S(1)} %copy-done.36, bf16[1024,2048]{1,0:T(8,128)(2,1)S(1)} %copy-done.44), kind=kOutput, calls=%fused_computation.6 | convolution fusion | flops 6445596672 | bytes 13631488 | tf_op jit(solution)/shard_map/dot_general | solution.py:19
  150.2 30.0 %middle_back.1 = (f32[512,1536]{1,0:T(8,128)}, bf16[1024,1536]{1,0:T(8,128)(2,1)}, f32[8,1536]{1,0:T(8,128)}) custom-call(bf16[1024,2048]{1,0:T(8,128)(2,1)} %get-tuple-element.46.gate_ref, bf16[1024,2048]{1,0:T(8,128)(2,1)} %get-tuple-element.47.up_ref, bf16[1536,2048]{1,0:T(8,128)(2,1)} %gate_weight_ref.1, bf16[1536,2048]{1,0:T(8,128)(2,1)} %up_weight_ref.1, ...), custom_call_target="tpu_custom_call" | custom-call | flops 12884901888 | bytes 39321600 | tf_op jit(solution)/shard_map/middle_back/pallas_call | solution.py:604
  180.3 4.7 convolution_convert_fusion.8
  185.6 4.1 multiply_convert_fusion.3
  189.7 2.9 convolution_convert_fusion.7
  195.6 34.1 %attend_backward.1 = (bf16[1024,768]{1,0:T(8,128)(2,1)S(1)}, bf16[1024,768]{1,0:T(8,128)(2,1)S(1)}, bf16[1024,768]{1,0:T(8,128)(2,1)}, bf16[16,1024]{1,0:T(8,128)(2,1)S(1)}) custom-call(bf16[1024,768]{1,0:T(8,128)(2,1)} %copy-done.6, bf16[1024,768]{1,0:T(8,128)(2,1)} %convolution_convert_fusion.11.k_ref, bf16[1024,768]{1,0:T(8,128)(2,1)} %convolution_convert_fusion.10.v_ref, ...), custom_call_target="tpu_custom_call" | custom-call | flops 18119393280 | bytes 15728640 | tf_op jit(solution)/shard_map/attend_backward/pallas_call | solution.py:277
  229.7 3.2 convolution_convert_fusion.5
  237.0 6.4 %convolution_convert_fusion.4 = bf16[1536,768]{1,0:T(8,128)(2,1)} fusion(bf16[1024,1536]{1,0:T(8,128)(2,1)} %norm_gather.1, bf16[1024,768]{1,0:T(8,128)(2,1)} %get-tuple-element.54.value_ref), kind=kOutput, calls=%fused_computation.13 | convolution fusion | flops 2417098752 | bytes 7077888 | tf_op jit(solution)/shard_map/dot_general | solution.py:19
  243.5 2.9 constant_dynamic-slice_fusion.13
  249.7 6.6 %constant_dynamic-slice_fusion.5 = (bf16[2,2,1,2,96,2048]{5,4,3,2,1,0:T(8,128)(2,1)}, bf16[2,2,1,2,96,2048]{5,4,3,2,1,0:T(8,128)(2,1)}) fusion(bf16[2,2,2,2,96,2048]{5,4,3,2,1,0:T(8,128)(2,1)} %bitcast.263, s32[]{:T(128)S(6)} %select_n.115, s32[]{:T(128)S(6)} %select_n.116), kind=kLoop, calls=%fused_computation.143 | loop fusion | bytes 12582920 | tf_op jit(solution)/shard_map/jit(dynamic_index_in_dim)/dynamic_slice | solution.py:47
  256.4 6.8 %constant_dynamic-slice_fusion.7 = (bf16[2,2,2,1,96,2048]{5,4,3,2,1,0:T(8,128)(2,1)}, bf16[2,2,2,1,96,2048]{5,4,3,2,1,0:T(8,128)(2,1)}) fusion(bf16[2,2,2,2,96,2048]{5,4,3,2,1,0:T(8,128)(2,1)} %bitcast.262, s32[]{:T(128)S(6)} %select_n.113, s32[]{:T(128)S(6)} %select_n.114), kind=kLoop, calls=%fused_computation.145 | loop fusion | bytes 12582920 | tf_op jit(solution)/shard_map/jit(dynamic_index_in_dim)/dynamic_slice | solution.py:47
  263.2 3.9 convolution_convert_fusion.6
  267.7 24.0 %first_back.1 = (f32[512,1536]{1,0:T(8,128)}, f32[8,1536]{1,0:T(8,128)}) custom-call(bf16[1024,768]{1,0:T(8,128)(2,1)} %copy-done.4, bf16[1024,768]{1,0:T(8,128)(2,1)} %copy-done.5, bf16[1024,768]{1,0:T(8,128)(2,1)} %get-tuple-element.54.value_ref, bf16[1024,768]{1,0:T(8,128)(2,1)} %copy-done.42, bf16[16,1024]{1,0:T(8,128)(2,1)} %copy-done, ...), custom_call_target="tpu_custom_call" | custom-call | flops 9663676416 | bytes 31457280 | tf_op jit(solution)/shard_map/first_back/pallas_call | solution.py:626
  293.6 3.4 pad_maximum_fusion
  303.2 3.2 copy.50
  306.4 18.0 %all_sum.1 = f32[8,1536]{1,0:T(8,128)} custom-call(f32[8,1536]{1,0:T(8,128)} %maximum_maximum_fusion.part_ref), custom_call_target="tpu_custom_call" | custom-call | tf_op jit(solution)/shard_map/all_sum/pallas_call | solution.py:644
  324.4 15.8 %result_rows.1 = bf16[512,1536]{1,0:T(8,128)(2,1)} custom-call(bf16[1024,2048]{1,0:T(8,128)(2,1)} %get-tuple-element.98.hidden_ref, bf16[2048,1536]{1,0:T(8,128)(2,1)} %weight_ref.3, f32[512,1536]{1,0:T(8,128)} %get-tuple-element.42.middle_ref), custom_call_target="tpu_custom_call" | custom-call | flops 6442450944 | bytes 23592960 | tf_op jit(solution)/shard_map/result_rows/pallas_call | solution.py:588
  350.8 21.1 %collective-permute-done.4 = bf16[2,2,2,96,768]{4,3,0,1,2:T(8,128)(2,1)S(1)} collective-permute-done((bf16[2,2,2,96,768]{4,3,0,1,2:T(8,128)(2,1)S(1)}, bf16[2,2,2,96,768]{4,3,0,1,2:T(8,128)(2,1)S(1)}, u32[]{:S(2)}, u32[]{:S(2)}) %collective-permute-start.4) | collective-permute-done | bytes 1179680 | tf_op jit(solution)/shard_map/ppermute | solution.py:42
  372.7 6.9 %collective-permute-done = bf16[2,2,2,96,780]{4,3,2,1,0:T(8,128)(2,1)S(1)} collective-permute-done((bf16[2,2,2,96,780]{4,3,2,1,0:T(8,128)(2,1)S(1)}, bf16[2,2,2,96,780]{4,3,2,1,0:T(8,128)(2,1)S(1)}, u32[]{:S(2)}, u32[]{:S(2)}) %collective-permute-start) | collective-permute-done | bytes 1198112 | tf_op jit(solution)/shard_map/ppermute | solution.py:42
  380.7 2.2 fusion.4
  384.5 2.1 fusion.3
  387.6 64.4 %collective-permute-done.17 = bf16[2,2,96,768]{3,2,0,1:T(8,128)(2,1)S(1)} collective-permute-done((bf16[2,2,96,768]{3,2,0,1:T(8,128)(2,1)S(1)}, bf16[2,2,96,768]{3,2,0,1:T(8,128)(2,1)S(1)}, u32[]{:S(2)}, u32[]{:S(2)}) %collective-permute-start.17) | collective-permute-done | bytes 589856 | tf_op jit(solution)/shard_map/ppermute | solution.py:42
  452.5 7.2 %collective-permute-done.13 = bf16[2,2,96,768]{3,2,0,1:T(8,128)(2,1)S(1)} collective-permute-done((bf16[2,2,96,768]{3,2,0,1:T(8,128)(2,1)S(1)}, bf16[2,2,96,768]{3,2,0,1:T(8,128)(2,1)S(1)}, u32[]{:S(2)}, u32[]{:S(2)}) %collective-permute-start.13) | collective-permute-done | bytes 589856 | tf_op jit(solution)/shard_map/ppermute | solution.py:42
  460.1 4.5 collective-permute-done.9
  466.7 4.9 collective-permute-done.5
  471.9 7.5 %collective-permute-done.1 = bf16[2,2,96,780]{3,2,1,0:T(8,128)(2,1)S(1)} collective-permute-done((bf16[2,2,96,780]{3,2,1,0:T(8,128)(2,1)S(1)}, bf16[2,2,96,780]{3,2,1,0:T(8,128)(2,1)S(1)}, u32[]{:S(2)}, u32[]{:S(2)}) %collective-permute-start.1) | collective-permute-done | bytes 599072 | tf_op jit(solution)/shard_map/ppermute | solution.py:42
  481.6 6.1 collective-permute-done.14
  490.0 5.7 collective-permute-done.6
  497.1 7.0 %collective-permute-done.2 = bf16[2,96,780]{2,1,0:T(8,128)(2,1)S(1)} collective-permute-done((bf16[2,96,780]{2,1,0:T(8,128)(2,1)S(1)}, bf16[2,96,780]{2,1,0:T(8,128)(2,1)S(1)}, u32[]{:S(2)}, u32[]{:S(2)}) %collective-permute-start.2) | collective-permute-done | bytes 299552 | tf_op jit(solution)/shard_map/ppermute | solution.py:42
  504.1 2.9 collective-permute-start.19
  507.1 7.5 %collective-permute-done.19 = bf16[96,768]{1,0:T(8,128)(2,1)S(1)} collective-permute-done((bf16[96,768]{1,0:T(8,128)(2,1)S(1)}, bf16[96,768]{1,0:T(8,128)(2,1)S(1)}, u32[]{:S(2)}, u32[]{:S(2)}) %collective-permute-start.19) | collective-permute-done | bytes 147488 | tf_op jit(solution)/shard_map/ppermute | solution.py:42
  515.4 8.6 %collective-permute-done.15 = bf16[96,768]{1,0:T(8,128)(2,1)S(1)} collective-permute-done((bf16[96,768]{1,0:T(8,128)(2,1)S(1)}, bf16[96,768]{1,0:T(8,128)(2,1)S(1)}, u32[]{:S(2)}, u32[]{:S(2)}) %collective-permute-start.15) | collective-permute-done | bytes 147488 | tf_op jit(solution)/shard_map/ppermute | solution.py:42
  524.8 8.2 %collective-permute-done.11 = bf16[96,768]{1,0:T(8,128)(2,1)S(1)} collective-permute-done((bf16[96,768]{1,0:T(8,128)(2,1)S(1)}, bf16[96,768]{1,0:T(8,128)(2,1)S(1)}, u32[]{:S(2)}, u32[]{:S(2)}) %collective-permute-start.11) | collective-permute-done | bytes 147488 | tf_op jit(solution)/shard_map/ppermute | solution.py:42
  533.7 9.0 %collective-permute-done.7 = bf16[96,768]{1,0:T(8,128)(2,1)S(1)} collective-permute-done((bf16[96,768]{1,0:T(8,128)(2,1)S(1)}, bf16[96,768]{1,0:T(8,128)(2,1)S(1)}, u32[]{:S(2)}, u32[]{:S(2)}) %collective-permute-start.7) | collective-permute-done | bytes 147488 | tf_op jit(solution)/shard_map/ppermute | solution.py:42
  544.6 2.3 collective-permute-start.30
  546.8 2.9 collective-permute-done.3
  553.1 7.1 %collective-permute-done.30 = bf16[2,96,1024]{2,1,0:T(8,128)(2,1)S(1)} collective-permute-done((bf16[2,96,1024]{2,1,0:T(8,128)(2,1)}, bf16[2,96,1024]{2,1,0:T(8,128)(2,1)S(1)}, u32[]{:S(2)}, u32[]{:S(2)}) %collective-permute-start.30) | collective-permute-done | bytes 393248 | tf_op jit(solution)/shard_map/ppermute | solution.py:42
  560.7 3.2 fusion.1
  565.9 3.2 fusion.2
  570.4 2.3 collective-permute-start.35
  572.8 5.9 collective-permute-done.35
  578.8 9.0 %collective-permute-done.25 = bf16[2,2,96,2048]{3,2,0,1:T(8,128)(2,1)S(1)} collective-permute-done((bf16[2,2,96,2048]{3,2,0,1:T(8,128)(2,1)S(1)}, bf16[2,2,96,2048]{3,2,0,1:T(8,128)(2,1)S(1)}, u32[]{:S(2)}, u32[]{:S(2)}) %collective-permute-start.25) | collective-permute-done | bytes 1572896 | tf_op jit(solution)/shard_map/ppermute | solution.py:42
  588.9 4.1 collective-permute-done.21
  594.9 12.5 %collective-permute-done.26 = bf16[2,96,2048]{2,1,0:T(8,128)(2,1)S(1)} collective-permute-done((bf16[2,96,2048]{2,1,0:T(8,128)(2,1)S(1)}, bf16[2,96,2048]{2,1,0:T(8,128)(2,1)S(1)}, u32[]{:S(2)}, u32[]{:S(2)}) %collective-permute-start.26) | collective-permute-done | bytes 786464 | tf_op jit(solution)/shard_map/ppermute | solution.py:42
  607.7 2.6 collective-permute-start.27
  610.3 13.8 %collective-permute-done.22 = bf16[2,96,2048]{2,1,0:T(8,128)(2,1)S(1)} collective-permute-done((bf16[2,96,2048]{2,1,0:T(8,128)(2,1)S(1)}, bf16[2,96,2048]{2,1,0:T(8,128)(2,1)S(1)}, u32[]{:S(2)}, u32[]{:S(2)}) %collective-permute-start.22) | collective-permute-done | bytes 786464 | tf_op jit(solution)/shard_map/ppermute | solution.py:42
  626.4 10.9 %collective-permute-done.23 = bf16[96,2048]{1,0:T(8,128)(2,1)S(1)} collective-permute-done((bf16[96,2048]{1,0:T(8,128)(2,1)S(1)}, bf16[96,2048]{1,0:T(8,128)(2,1)S(1)}, u32[]{:S(2)}, u32[]{:S(2)}) %collective-permute-start.23) | collective-permute-done | bytes 393248 | tf_op jit(solution)/shard_map/ppermute | solution.py:42
  (229 shorter events, 72.1 us)
Async XLA Ops:
  1.9 5.6 copy-start.34
  7.5 6.6 %copy-start.7 = (bf16[1024,1536]{1,0:T(8,128)(2,1)S(1)}, bf16[1024,1536]{1,0:T(8,128)(2,1)}, u32[]{:S(2)}) copy-start(bf16[1024,1536]{1,0:T(8,128)(2,1)} %norm_gather.1) | copy-start | bytes 9437188
  7.5 6.6 %copy-start.33 = (bf16[1536,768]{1,0:T(8,128)(2,1)S(1)}, bf16[1536,768]{1,0:T(8,128)(2,1)}, u32[]{:S(2)}) copy-start(bf16[1536,768]{1,0:T(8,128)(2,1)} %wv_ref.1) | copy-start | bytes 7077892
  24.1 3.9 copy-start.6
  65.8 12.6 %copy-start.35 = (bf16[1024,1536]{1,0:T(8,128)(2,1)S(1)}, bf16[1024,1536]{1,0:T(8,128)(2,1)}, u32[]{:S(2)}) copy-start(bf16[1024,1536]{1,0:T(8,128)(2,1)} %get-tuple-element.41) | copy-start | bytes 9437188
  78.4 10.9 %copy-start.37 = (bf16[1024,1536]{1,0:T(8,128)(2,1)S(1)}, bf16[1024,1536]{1,0:T(8,128)(2,1)}, u32[]{:S(2)}) copy-start(bf16[1024,1536]{1,0:T(8,128)(2,1)} %get-tuple-element.43) | copy-start | bytes 9437188
  106.8 6.7 %copy-start.41 = (bf16[1024,2048]{1,0:T(8,128)(2,1)S(1)}, bf16[1024,2048]{1,0:T(8,128)(2,1)}, u32[]{:S(2)}) copy-start(bf16[1024,2048]{1,0:T(8,128)(2,1)} %get-tuple-element.98.hidden_ref) | copy-start | bytes 12582916
  123.1 257.2 %collective-permute-start.28 = (bf16[2,2,2,96,1024]{4,3,0,1,2:T(8,128)(2,1)}, bf16[2,2,2,96,1024]{4,3,0,1,2:T(8,128)(2,1)}, u32[]{:S(2)}, u32[]{:S(2)}) collective-permute-start(bf16[2,2,2,96,1024]{4,3,0,1,2:T(8,128)(2,1)} %bitcast.254), channel_id=1, source_target_pairs={{0,2},{2,0},{4,6},{6,4},{8,10},{10,8},{12,14},{14,12},{16,18},{18,... | collective-permute-start | bytes 4718600 | tf_op jit(solution)/shard_map/ppermute | solution.py:42
  125.9 6.4 copy-start.43
  130.7 10.7 %copy-start.44 = (bf16[1024,2048]{1,0:T(8,128)(2,1)S(1)}, bf16[1024,2048]{1,0:T(8,128)(2,1)}, u32[]{:S(2)}) copy-start(bf16[1024,2048]{1,0:T(8,128)(2,1)} %get-tuple-element.46.gate_ref) | copy-start | bytes 12582916
  130.7 252.2 %collective-permute-start.32 = (bf16[2,2,2,96,1024]{4,3,0,1,2:T(8,128)(2,1)}, bf16[2,2,2,96,1024]{4,3,0,1,2:T(8,128)(2,1)}, u32[]{:S(2)}, u32[]{:S(2)}) collective-permute-start(bf16[2,2,2,96,1024]{4,3,0,1,2:T(8,128)(2,1)} %bitcast.253), channel_id=1, source_target_pairs={{0,4},{2,6},{4,0},{6,2},{8,12},{10,14},{12,8},{14,10},{16,20},{18,... | collective-permute-start | bytes 4718600 | tf_op jit(solution)/shard_map/ppermute | solution.py:42
  150.2 30.1 %copy-start.3 = (bf16[1024,768]{1,0:T(8,128)(2,1)S(1)}, bf16[1024,768]{1,0:T(8,128)(2,1)}, u32[]{:S(2)}) copy-start(bf16[1024,768]{1,0:T(8,128)(2,1)} %copy-done.2) | copy-start | bytes 4718596
  180.3 4.8 copy-start.30
  180.3 4.8 copy-start.38
  180.3 4.8 copy-start.39
  180.3 5.4 copy-start.40
  185.6 4.1 copy-start.8
  195.0 148.1 %collective-permute-start.16 = (bf16[2,2,2,96,768]{4,3,0,1,2:T(8,128)(2,1)}, bf16[2,2,2,96,768]{4,3,0,1,2:T(8,128)(2,1)}, u32[]{:S(2)}, u32[]{:S(2)}) collective-permute-start(bf16[2,2,2,96,768]{4,3,0,1,2:T(8,128)(2,1)} %bitcast.255), channel_id=1, source_target_pairs={{0,2},{2,0},{4,6},{6,4},{8,10},{10,8},{12,14},{14,12},{16,18},{18,... | collective-permute-start | bytes 3538952 | tf_op jit(solution)/shard_map/ppermute | solution.py:42
  229.7 19.9 %copy-start = (bf16[16,1024]{1,0:T(8,128)(2,1)}, bf16[16,1024]{1,0:T(8,128)(2,1)S(1)}, u32[]{:S(2)}) copy-start(bf16[16,1024]{1,0:T(8,128)(2,1)S(1)} %get-tuple-element.55.forget_ref) | copy-start | bytes 98308
  229.7 33.5 %copy-start.4 = (bf16[1024,768]{1,0:T(8,128)(2,1)}, bf16[1024,768]{1,0:T(8,128)(2,1)S(1)}, u32[]{:S(2)}) copy-start(bf16[1024,768]{1,0:T(8,128)(2,1)S(1)} %get-tuple-element.52.query_ref) | copy-start | bytes 4718596
  235.9 110.7 %collective-permute-start.12 = (bf16[2,2,2,96,768]{4,3,0,1,2:T(8,128)(2,1)}, bf16[2,2,2,96,768]{4,3,0,1,2:T(8,128)(2,1)}, u32[]{:S(2)}, u32[]{:S(2)}) collective-permute-start(bf16[2,2,2,96,768]{4,3,0,1,2:T(8,128)(2,1)} %bitcast.256), channel_id=1, source_target_pairs={{0,4},{2,6},{4,0},{6,2},{8,12},{10,14},{12,8},{14,10},{16,20},{18,... | collective-permute-start | bytes 3538952 | tf_op jit(solution)/shard_map/ppermute | solution.py:42
  243.5 5.6 copy-start.9
  247.5 100.9 %collective-permute-start.8 = (bf16[2,2,2,96,768]{4,3,0,2,1:T(8,128)(2,1)}, bf16[2,2,2,96,768]{4,3,0,2,1:T(8,128)(2,1)}, u32[]{:S(2)}, u32[]{:S(2)}) collective-permute-start(bf16[2,2,2,96,768]{4,3,0,2,1:T(8,128)(2,1)} %bitcast.257), channel_id=1, source_target_pairs={{0,8},{2,10},{4,12},{6,14},{8,0},{10,2},{12,4},{14,6},{16,24},{18,... | collective-permute-start | bytes 3538952 | tf_op jit(solution)/shard_map/ppermute | solution.py:42
  256.3 6.8 %copy-start.10 = (bf16[1024,1536]{1,0:T(8,128)(2,1)S(1)}, bf16[1024,1536]{1,0:T(8,128)(2,1)}, u32[]{:S(2)}) copy-start(bf16[1024,1536]{1,0:T(8,128)(2,1)} %norm_gather.1) | copy-start | bytes 9437188
  263.2 3.9 copy-start.26
  267.7 24.9 %copy-start.27 = (f32[8,1536]{1,0:T(8,128)S(1)}, f32[8,1536]{1,0:T(8,128)}, u32[]{:S(2)}) copy-start(f32[8,1536]{1,0:T(8,128)} %get-tuple-element.59) | copy-start | bytes 147460
  340.1 4.8 copy-start.20
  340.3 6.3 copy-start.18
  343.1 28.8 %collective-permute-start.4 = (bf16[2,2,2,96,768]{4,3,0,1,2:T(8,128)(2,1)S(1)}, bf16[2,2,2,96,768]{4,3,0,1,2:T(8,128)(2,1)S(1)}, u32[]{:S(2)}, u32[]{:S(2)}) collective-permute-start(bf16[2,2,2,96,768]{4,3,0,1,2:T(8,128)(2,1)S(1)} %bitcast.270), channel_id=1, source_target_pairs={{0,4},{2,6},{4,0},{6,2},{8,12},{10,14},{12,8},{14,10},{16,20},{18,... | collective-permute-start | bytes 3538952 | tf_op jit(solution)/shard_map/ppermute | solution.py:42
  346.5 33.1 %collective-permute-start = (bf16[2,2,2,96,780]{4,3,2,1,0:T(8,128)(2,1)S(1)}, bf16[2,2,2,96,780]{4,3,2,1,0:T(8,128)(2,1)S(1)}, u32[]{:S(2)}, u32[]{:S(2)}) collective-permute-start(bf16[2,2,2,96,780]{4,3,2,1,0:T(8,128)(2,1)S(1)} %dynamic-slice_bitcast_fusion.2), channel_id=1, source_target_pairs={{0,2},{2,0},{4,6},{6,4},{8,10},{10,8},{12,14},{14,12},{16,18},{18,... | collective-permute-start | bytes 3594248 | tf_op jit(solution)/shard_map/ppermute | solution.py:42
  348.4 212.3 %collective-permute-start.24 = (bf16[2,2,2,96,2048]{4,3,0,1,2:T(8,128)(2,1)}, bf16[2,2,2,96,2048]{4,3,0,1,2:T(8,128)(2,1)}, u32[]{:S(2)}, u32[]{:S(2)}) collective-permute-start(bf16[2,2,2,96,2048]{4,3,0,1,2:T(8,128)(2,1)} %bitcast.251), channel_id=1, source_target_pairs={{0,4},{2,6},{4,0},{6,2},{8,12},{10,14},{12,8},{14,10},{16,20},{18,... | collective-permute-start | bytes 9437192 | tf_op jit(solution)/shard_map/ppermute | solution.py:42
  349.0 23.3 %copy-start.17 = (bf16[2,2,1,2,96,768]{5,4,3,2,1,0:T(8,128)(2,1)S(1)}, bf16[2,2,1,2,96,768]{5,4,3,2,1,0:T(8,128)(2,1)}, u32[]{:S(2)}) copy-start(bf16[2,2,1,2,96,768]{5,4,3,2,1,0:T(8,128)(2,1)} %get-tuple-element.118) | copy-start | bytes 3538948
  371.9 192.9 %collective-permute-start.20 = (bf16[2,2,2,96,2048]{4,3,0,1,2:T(8,128)(2,1)}, bf16[2,2,2,96,2048]{4,3,0,1,2:T(8,128)(2,1)}, u32[]{:S(2)}, u32[]{:S(2)}) collective-permute-start(bf16[2,2,2,96,2048]{4,3,0,1,2:T(8,128)(2,1)} %bitcast.252), channel_id=1, source_target_pairs={{0,2},{2,0},{4,6},{6,4},{8,10},{10,8},{12,14},{14,12},{16,18},{18,... | collective-permute-start | bytes 9437192 | tf_op jit(solution)/shard_map/ppermute | solution.py:42
  372.7 8.0 %copy-start.15 = (bf16[2,2,2,1,96,1024]{5,4,3,2,1,0:T(8,128)(2,1)S(1)}, bf16[2,2,2,1,96,1024]{5,4,3,2,1,0:T(8,128)(2,1)}, u32[]{:S(2)}) copy-start(bf16[2,2,2,1,96,1024]{5,4,3,2,1,0:T(8,128)(2,1)} %get-tuple-element.105) | copy-start | bytes 4718596
  379.7 72.3 %collective-permute-start.17 = (bf16[2,2,96,768]{3,2,0,1:T(8,128)(2,1)S(1)}, bf16[2,2,96,768]{3,2,0,1:T(8,128)(2,1)S(1)}, u32[]{:S(2)}, u32[]{:S(2)}) collective-permute-start(bf16[2,2,96,768]{3,2,0,1:T(8,128)(2,1)S(1)} %dynamic-slice_bitcast_fusion.8), channel_id=1, source_target_pairs={{0,4},{2,6},{4,0},{6,2},{8,12},{10,14},{12,8},{14,10},{16,20},{18,... | collective-permute-start | bytes 1769480 | tf_op jit(solution)/shard_map/ppermute | solution.py:42
  380.3 79.5 %collective-permute-start.13 = (bf16[2,2,96,768]{3,2,0,1:T(8,128)(2,1)S(1)}, bf16[2,2,96,768]{3,2,0,1:T(8,128)(2,1)S(1)}, u32[]{:S(2)}, u32[]{:S(2)}) collective-permute-start(bf16[2,2,96,768]{3,2,0,1:T(8,128)(2,1)S(1)} %dynamic-slice_bitcast_fusion.9), channel_id=1, source_target_pairs={{0,2},{2,0},{4,6},{6,4},{8,10},{10,8},{12,14},{14,12},{16,18},{18,... | collective-permute-start | bytes 1769480 | tf_op jit(solution)/shard_map/ppermute | solution.py:42
  383.0 81.7 %collective-permute-start.9 = (bf16[2,2,96,768]{3,2,0,1:T(8,128)(2,1)S(1)}, bf16[2,2,96,768]{3,2,0,1:T(8,128)(2,1)S(1)}, u32[]{:S(2)}, u32[]{:S(2)}) collective-permute-start(bf16[2,2,96,768]{3,2,0,1:T(8,128)(2,1)S(1)} %dynamic-slice_bitcast_fusion.10), channel_id=1, source_target_pairs={{0,4},{2,6},{4,0},{6,2},{8,12},{10,14},{12,8},{14,10},{16,20},{18,... | collective-permute-start | bytes 1769480 | tf_op jit(solution)/shard_map/ppermute | solution.py:42
  452.0 19.6 %collective-permute-start.5 = (bf16[2,2,96,768]{3,2,0,1:T(8,128)(2,1)S(1)}, bf16[2,2,96,768]{3,2,0,1:T(8,128)(2,1)S(1)}, u32[]{:S(2)}, u32[]{:S(2)}) collective-permute-start(bf16[2,2,96,768]{3,2,0,1:T(8,128)(2,1)S(1)} %dynamic-slice_bitcast_fusion.11), channel_id=1, source_target_pairs={{0,2},{2,0},{4,6},{6,4},{8,10},{10,8},{12,14},{14,12},{16,18},{18,... | collective-permute-start | bytes 1769480 | tf_op jit(solution)/shard_map/ppermute | solution.py:42
  459.7 19.6 %collective-permute-start.1 = (bf16[2,2,96,780]{3,2,1,0:T(8,128)(2,1)S(1)}, bf16[2,2,96,780]{3,2,1,0:T(8,128)(2,1)S(1)}, u32[]{:S(2)}, u32[]{:S(2)}) collective-permute-start(bf16[2,2,96,780]{3,2,1,0:T(8,128)(2,1)S(1)} %dynamic-slice_bitcast_fusion.7), channel_id=1, source_target_pairs={{0,4},{2,6},{4,0},{6,2},{8,12},{10,14},{12,8},{14,10},{16,20},{18,... | collective-permute-start | bytes 1797128 | tf_op jit(solution)/shard_map/ppermute | solution.py:42
  464.6 78.8 %collective-permute-start.29 = (bf16[2,2,96,1024]{3,2,0,1:T(8,128)(2,1)S(1)}, bf16[2,2,96,1024]{3,2,0,1:T(8,128)(2,1)S(1)}, u32[]{:S(2)}, u32[]{:S(2)}) collective-permute-start(bf16[2,2,96,1024]{3,2,0,1:T(8,128)(2,1)S(1)} %dynamic-slice_bitcast_fusion.4), channel_id=1, source_target_pairs={{0,4},{2,6},{4,0},{6,2},{8,12},{10,14},{12,8},{14,10},{16,20},{18,... | collective-permute-start | bytes 2359304 | tf_op jit(solution)/shard_map/ppermute | solution.py:42
  471.6 9.1 %collective-permute-start.18 = (bf16[2,96,768]{2,1,0:T(8,128)(2,1)S(1)}, bf16[2,96,768]{2,1,0:T(8,128)(2,1)S(1)}, u32[]{:S(2)}, u32[]{:S(2)}) collective-permute-start(bf16[2,96,768]{2,1,0:T(8,128)(2,1)S(1)} %dynamic-slice_bitcast_fusion.17), channel_id=1, source_target_pairs={{0,8},{2,10},{4,12},{6,14},{8,0},{10,2},{12,4},{14,6},{16,24},{18,... | collective-permute-start | bytes 884744 | tf_op jit(solution)/shard_map/ppermute | solution.py:42
  479.4 8.3 %collective-permute-start.14 = (bf16[2,96,768]{2,1,0:T(8,128)(2,1)S(1)}, bf16[2,96,768]{2,1,0:T(8,128)(2,1)S(1)}, u32[]{:S(2)}, u32[]{:S(2)}) collective-permute-start(bf16[2,96,768]{2,1,0:T(8,128)(2,1)S(1)} %dynamic-slice_bitcast_fusion.18), channel_id=1, source_target_pairs={{0,8},{2,10},{4,12},{6,14},{8,0},{10,2},{12,4},{14,6},{16,24},{18,... | collective-permute-start | bytes 884744 | tf_op jit(solution)/shard_map/ppermute | solution.py:42
  480.7 7.9 %collective-permute-start.10 = (bf16[2,96,768]{2,1,0:T(8,128)(2,1)S(1)}, bf16[2,96,768]{2,1,0:T(8,128)(2,1)S(1)}, u32[]{:S(2)}, u32[]{:S(2)}) collective-permute-start(bf16[2,96,768]{2,1,0:T(8,128)(2,1)S(1)} %dynamic-slice_bitcast_fusion.19), channel_id=1, source_target_pairs={{0,2},{2,0},{4,6},{6,4},{8,10},{10,8},{12,14},{14,12},{16,18},{18,... | collective-permute-start | bytes 884744 | tf_op jit(solution)/shard_map/ppermute | solution.py:42
  487.7 64.9 %collective-permute-start.33 = (bf16[2,2,96,1024]{3,2,0,1:T(8,128)(2,1)}, bf16[2,2,96,1024]{3,2,0,1:T(8,128)(2,1)S(1)}, u32[]{:S(2)}, u32[]{:S(2)}) collective-permute-start(bf16[2,2,96,1024]{3,2,0,1:T(8,128)(2,1)} %dynamic-slice_bitcast_fusion.3), channel_id=1, source_target_pairs={{0,2},{2,0},{4,6},{6,4},{8,10},{10,8},{12,14},{14,12},{16,18},{18,... | collective-permute-start | bytes 2359304 | tf_op jit(solution)/shard_map/ppermute | solution.py:42
  488.6 7.2 %collective-permute-start.6 = (bf16[2,96,768]{2,1,0:T(8,128)(2,1)S(1)}, bf16[2,96,768]{2,1,0:T(8,128)(2,1)S(1)}, u32[]{:S(2)}, u32[]{:S(2)}) collective-permute-start(bf16[2,96,768]{2,1,0:T(8,128)(2,1)S(1)} %dynamic-slice_bitcast_fusion.20), channel_id=1, source_target_pairs={{0,8},{2,10},{4,12},{6,14},{8,0},{10,2},{12,4},{14,6},{16,24},{18,... | collective-permute-start | bytes 884744 | tf_op jit(solution)/shard_map/ppermute | solution.py:42
  495.7 8.3 %collective-permute-start.2 = (bf16[2,96,780]{2,1,0:T(8,128)(2,1)S(1)}, bf16[2,96,780]{2,1,0:T(8,128)(2,1)S(1)}, u32[]{:S(2)}, u32[]{:S(2)}) collective-permute-start(bf16[2,96,780]{2,1,0:T(8,128)(2,1)S(1)} %dynamic-slice_bitcast_fusion.16), channel_id=1, source_target_pairs={{0,8},{2,10},{4,12},{6,14},{8,0},{10,2},{12,4},{14,6},{16,24},{18,... | collective-permute-start | bytes 898568 | tf_op jit(solution)/shard_map/ppermute | solution.py:42
  504.1 10.6 %collective-permute-start.19 = (bf16[96,768]{1,0:T(8,128)(2,1)S(1)}, bf16[96,768]{1,0:T(8,128)(2,1)S(1)}, u32[]{:S(2)}, u32[]{:S(2)}) collective-permute-start(bf16[96,768]{1,0:T(8,128)(2,1)S(1)} %dynamic-slice_bitcast_fusion.24), channel_id=1, source_target_pairs={{0,16},{2,18},{4,20},{6,22},{8,24},{10,26},{12,28},{14,30},{16,0},... | collective-permute-start | bytes 442376 | tf_op jit(solution)/shard_map/ppermute | solution.py:42
  514.6 9.4 %collective-permute-start.15 = (bf16[96,768]{1,0:T(8,128)(2,1)S(1)}, bf16[96,768]{1,0:T(8,128)(2,1)S(1)}, u32[]{:S(2)}, u32[]{:S(2)}) collective-permute-start(bf16[96,768]{1,0:T(8,128)(2,1)S(1)} %dynamic-slice_bitcast_fusion.25), channel_id=1, source_target_pairs={{0,16},{2,18},{4,20},{6,22},{8,24},{10,26},{12,28},{14,30},{16,0},... | collective-permute-start | bytes 442376 | tf_op jit(solution)/shard_map/ppermute | solution.py:42
  524.0 8.9 %collective-permute-start.11 = (bf16[96,768]{1,0:T(8,128)(2,1)S(1)}, bf16[96,768]{1,0:T(8,128)(2,1)S(1)}, u32[]{:S(2)}, u32[]{:S(2)}) collective-permute-start(bf16[96,768]{1,0:T(8,128)(2,1)S(1)} %dynamic-slice_bitcast_fusion.26), channel_id=1, source_target_pairs={{0,16},{2,18},{4,20},{6,22},{8,24},{10,26},{12,28},{14,30},{16,0},... | collective-permute-start | bytes 442376 | tf_op jit(solution)/shard_map/ppermute | solution.py:42
  532.9 9.8 %collective-permute-start.7 = (bf16[96,768]{1,0:T(8,128)(2,1)S(1)}, bf16[96,768]{1,0:T(8,128)(2,1)S(1)}, u32[]{:S(2)}, u32[]{:S(2)}) collective-permute-start(bf16[96,768]{1,0:T(8,128)(2,1)S(1)} %dynamic-slice_bitcast_fusion.27), channel_id=1, source_target_pairs={{0,16},{2,18},{4,20},{6,22},{8,24},{10,26},{12,28},{14,30},{16,0},... | collective-permute-start | bytes 442376 | tf_op jit(solution)/shard_map/ppermute | solution.py:42
  542.7 7.0 %collective-permute-start.3 = (bf16[96,780]{1,0:T(8,128)(2,1)S(1)}, bf16[96,780]{1,0:T(8,128)(2,1)S(1)}, u32[]{:S(2)}, u32[]{:S(2)}) collective-permute-start(bf16[96,780]{1,0:T(8,128)(2,1)S(1)} %dynamic-slice_bitcast_fusion.23), channel_id=1, source_target_pairs={{0,16},{2,18},{4,20},{6,22},{8,24},{10,26},{12,28},{14,30},{16,0},... | collective-permute-start | bytes 449288 | tf_op jit(solution)/shard_map/ppermute | solution.py:42
  544.6 15.6 %collective-permute-start.30 = (bf16[2,96,1024]{2,1,0:T(8,128)(2,1)}, bf16[2,96,1024]{2,1,0:T(8,128)(2,1)S(1)}, u32[]{:S(2)}, u32[]{:S(2)}) collective-permute-start(bf16[2,96,1024]{2,1,0:T(8,128)(2,1)} %dynamic-slice_bitcast_fusion.13), channel_id=1, source_target_pairs={{0,8},{2,10},{4,12},{6,14},{8,0},{10,2},{12,4},{14,6},{16,24},{18,... | collective-permute-start | bytes 1179656 | tf_op jit(solution)/shard_map/ppermute | solution.py:42
  552.6 8.1 %copy-start.14 = (bf16[2,2,1,2,96,2048]{5,4,3,2,1,0:T(8,128)(2,1)S(1)}, bf16[2,2,1,2,96,2048]{5,4,3,2,1,0:T(8,128)(2,1)}, u32[]{:S(2)}) copy-start(bf16[2,2,1,2,96,2048]{5,4,3,2,1,0:T(8,128)(2,1)} %get-tuple-element.99) | copy-start | bytes 9437188
  553.0 17.3 %collective-permute-start.34 = (bf16[2,96,1024]{2,1,0:T(8,128)(2,1)S(1)}, bf16[2,96,1024]{2,1,0:T(8,128)(2,1)S(1)}, u32[]{:S(2)}, u32[]{:S(2)}) collective-permute-start(bf16[2,96,1024]{2,1,0:T(8,128)(2,1)S(1)} %dynamic-slice_bitcast_fusion.12), channel_id=1, source_target_pairs={{0,8},{2,10},{4,12},{6,14},{8,0},{10,2},{12,4},{14,6},{16,24},{18,... | collective-permute-start | bytes 1179656 | tf_op jit(solution)/shard_map/ppermute | solution.py:42
  560.3 12.4 %collective-permute-start.31 = (bf16[96,1024]{1,0:T(8,128)(2,1)S(1)}, bf16[96,1024]{1,0:T(8,128)(2,1)S(1)}, u32[]{:S(2)}, u32[]{:S(2)}) collective-permute-start(bf16[96,1024]{1,0:T(8,128)(2,1)S(1)} %dynamic-slice_bitcast_fusion.22), channel_id=1, source_target_pairs={{0,16},{2,18},{4,20},{6,22},{8,24},{10,26},{12,28},{14,30},{16,0},... | collective-permute-start | bytes 589832 | tf_op jit(solution)/shard_map/ppermute | solution.py:42
  564.2 23.7 %collective-permute-start.25 = (bf16[2,2,96,2048]{3,2,0,1:T(8,128)(2,1)S(1)}, bf16[2,2,96,2048]{3,2,0,1:T(8,128)(2,1)S(1)}, u32[]{:S(2)}, u32[]{:S(2)}) collective-permute-start(bf16[2,2,96,2048]{3,2,0,1:T(8,128)(2,1)S(1)} %dynamic-slice_bitcast_fusion), channel_id=1, source_target_pairs={{0,2},{2,0},{4,6},{6,4},{8,10},{10,8},{12,14},{14,12},{16,18},{18,... | collective-permute-start | bytes 4718600 | tf_op jit(solution)/shard_map/ppermute | solution.py:42
  569.3 23.7 %collective-permute-start.21 = (bf16[2,2,96,2048]{3,2,0,1:T(8,128)(2,1)S(1)}, bf16[2,2,96,2048]{3,2,0,1:T(8,128)(2,1)S(1)}, u32[]{:S(2)}, u32[]{:S(2)}) collective-permute-start(bf16[2,2,96,2048]{3,2,0,1:T(8,128)(2,1)S(1)} %dynamic-slice_bitcast_fusion.1), channel_id=1, source_target_pairs={{0,4},{2,6},{4,0},{6,2},{8,12},{10,14},{12,8},{14,10},{16,20},{18,... | collective-permute-start | bytes 4718600 | tf_op jit(solution)/shard_map/ppermute | solution.py:42
  570.4 8.3 %collective-permute-start.35 = (bf16[96,1024]{1,0:T(8,128)(2,1)S(1)}, bf16[96,1024]{1,0:T(8,128)(2,1)S(1)}, u32[]{:S(2)}, u32[]{:S(2)}) collective-permute-start(bf16[96,1024]{1,0:T(8,128)(2,1)S(1)} %dynamic-slice_bitcast_fusion.21), channel_id=1, source_target_pairs={{0,16},{2,18},{4,20},{6,22},{8,24},{10,26},{12,28},{14,30},{16,0},... | collective-permute-start | bytes 589832 | tf_op jit(solution)/shard_map/ppermute | solution.py:42
  588.5 18.9 %collective-permute-start.26 = (bf16[2,96,2048]{2,1,0:T(8,128)(2,1)S(1)}, bf16[2,96,2048]{2,1,0:T(8,128)(2,1)S(1)}, u32[]{:S(2)}, u32[]{:S(2)}) collective-permute-start(bf16[2,96,2048]{2,1,0:T(8,128)(2,1)S(1)} %dynamic-slice_bitcast_fusion.5), channel_id=1, source_target_pairs={{0,8},{2,10},{4,12},{6,14},{8,0},{10,2},{12,4},{14,6},{16,24},{18,... | collective-permute-start | bytes 2359304 | tf_op jit(solution)/shard_map/ppermute | solution.py:42
  593.6 30.5 %collective-permute-start.22 = (bf16[2,96,2048]{2,1,0:T(8,128)(2,1)S(1)}, bf16[2,96,2048]{2,1,0:T(8,128)(2,1)S(1)}, u32[]{:S(2)}, u32[]{:S(2)}) collective-permute-start(bf16[2,96,2048]{2,1,0:T(8,128)(2,1)S(1)} %dynamic-slice_bitcast_fusion.6), channel_id=1, source_target_pairs={{0,8},{2,10},{4,12},{6,14},{8,0},{10,2},{12,4},{14,6},{16,24},{18,... | collective-permute-start | bytes 2359304 | tf_op jit(solution)/shard_map/ppermute | solution.py:42
  607.7 17.7 %collective-permute-start.27 = (bf16[96,2048]{1,0:T(8,128)(2,1)S(1)}, bf16[96,2048]{1,0:T(8,128)(2,1)S(1)}, u32[]{:S(2)}, u32[]{:S(2)}) collective-permute-start(bf16[96,2048]{1,0:T(8,128)(2,1)S(1)} %dynamic-slice_bitcast_fusion.14), channel_id=1, source_target_pairs={{0,16},{2,18},{4,20},{6,22},{8,24},{10,26},{12,28},{14,30},{16,0},... | collective-permute-start | bytes 1179656 | tf_op jit(solution)/shard_map/ppermute | solution.py:42
  624.4 13.9 %copy-start.23 = (bf16[512,1536]{1,0:T(8,128)(2,1)S(1)}, bf16[512,1536]{1,0:T(8,128)(2,1)}, u32[]{:S(2)}) copy-start(bf16[512,1536]{1,0:T(8,128)(2,1)} %result_rows.1) | copy-start | bytes 4718596
  624.5 12.8 %collective-permute-start.23 = (bf16[96,2048]{1,0:T(8,128)(2,1)S(1)}, bf16[96,2048]{1,0:T(8,128)(2,1)S(1)}, u32[]{:S(2)}, u32[]{:S(2)}) collective-permute-start(bf16[96,2048]{1,0:T(8,128)(2,1)S(1)} %dynamic-slice_bitcast_fusion.15), channel_id=1, source_target_pairs={{0,16},{2,18},{4,20},{6,22},{8,24},{10,26},{12,28},{14,30},{16,0},... | collective-permute-start | bytes 1179656 | tf_op jit(solution)/shard_map/ppermute | solution.py:42
  626.4 13.0 %copy-start.22 = (f32[512,1536]{1,0:T(8,128)S(1)}, f32[512,1536]{1,0:T(8,128)}, u32[]{:S(2)}) copy-start(f32[512,1536]{1,0:T(8,128)} %get-tuple-element.134) | copy-start | bytes 9437188
  (17 other events, 49.9 us)

commit v3 on v2

--- a/solution.py
+++ b/solution.py
@@ -36,32 +36,57 @@
     return scaling * (weighted - normed * jnp.mean(weighted * normed, axis=1, keepdims=True))
 
 
-def halve(stacked, bit, axis, wide):
-    mine = (lax.axis_index("dp") >> bit) & 1
-    count = lax.axis_size("dp")
-    sent = lax.ppermute(
-        lax.dynamic_index_in_dim(stacked, 1 - mine, axis, keepdims=False),
-        "dp",
-        [(place, place ^ (1 << bit)) for place in range(count)],
-    )
-    kept = lax.dynamic_index_in_dim(stacked, mine, axis, keepdims=False)
-    total = kept.astype(jnp.float32) + sent.astype(jnp.float32)
-    return total if wide else total.astype(jnp.bfloat16)
-
-
-def spread_sum(gradient, swap):
-    count = lax.axis_size("dp")
-    bits = count.bit_length() - 1
-    order = list(range(bits))
-    for front, back in swap:
-        order[front], order[back] = order[back], order[front]
-    live = list(range(bits - 1, -1, -1))
-    stacked = gradient.reshape((2,) * bits + (gradient.shape[0] // count, gradient.shape[1]))
-    for place, bit in enumerate(order):
-        axis = live.index(bit)
-        live.pop(axis)
-        stacked = halve(stacked, bit, axis, place == bits - 1)
-    return stacked
+class Flow:
+    def __init__(self, gradient, swap):
+        self.count = lax.axis_size("dp")
+        self.bits = self.count.bit_length() - 1
+        self.order = list(range(self.bits))
+        for front, back in swap:
+            self.order[front], self.order[back] = self.order[back], self.order[front]
+        self.live = list(range(self.bits - 1, -1, -1))
+        self.whole = gradient.reshape(
+            (2,) * self.bits + (gradient.shape[0] // self.count, gradient.shape[1])
+        )
+        self.stage = 0
+        self.cut()
+
+    def cut(self):
+        bit = self.order[self.stage]
+        axis = self.live.index(bit)
+        self.live.pop(axis)
+        mine = (lax.axis_index("dp") >> bit) & 1
+        self.sent = lax.dynamic_index_in_dim(self.whole, 1 - mine, axis, keepdims=False)
+        self.kept = lax.dynamic_index_in_dim(self.whole, mine, axis, keepdims=False)
+
+    def fly(self):
+        bit = self.order[self.stage]
+        pairs = [(place, place ^ (1 << bit)) for place in range(self.count)]
+        self.got = lax.ppermute(self.sent, "dp", pairs)
+
+    def land(self):
+        total = self.kept.astype(jnp.float32) + self.got.astype(jnp.float32)
+        self.stage += 1
+        if self.stage == self.bits:
+            self.whole = total
+            return
+        self.whole = total.astype(jnp.bfloat16)
+        self.cut()
+
+    def done(self):
+        return self.stage == self.bits
+
+
+def tie(values, start=(), end=()):
+    values, sent, got = lax.optimization_barrier(
+        (values, tuple(flow.sent for flow in start), tuple(flow.got for flow in end))
+    )
+    for flow, one in zip(start, sent):
+        flow.sent = one
+        flow.fly()
+    for flow, one in zip(end, got):
+        flow.got = one
+        flow.land()
+    return values
 
 
 block_rows = 256
@@ -708,21 +733,23 @@
     hidden = (swish_out * up_pre).astype(low)
     along, across, deep = (), ((0, 1),), ((0, 2),)
     half = hidden.shape[1] // 2
-    down_front = inner_rows(upstream, hidden[:, :half]).astype(low)
-    down_back = inner_rows(upstream, hidden[:, half:]).astype(low)
     hidden_grad = against(upstream, down_weight)
     gate_grad = (
         hidden_grad * up_pre * sigmoid_gate * (1.0 + gate_pre * (1.0 - sigmoid_gate))
     ).astype(low)
     up_grad = (hidden_grad * swish_out).astype(low)
-    gate_grad, up_grad, down_front, down_back = lax.optimization_barrier(
-        (gate_grad, up_grad, down_front, down_back)
-    )
-    grad_gate = inner_rows(second_all, gate_grad).astype(low)
-    grad_up = inner_rows(second_all, up_grad).astype(low)
-    gate_grad, up_grad, grad_gate, grad_up = lax.optimization_barrier(
-        (gate_grad, up_grad, grad_gate, grad_up)
-    )
+    hidden, gate_grad, up_grad = lax.optimization_barrier((hidden, gate_grad, up_grad))
+    down = [
+        Flow(inner_rows(upstream, hidden[:, :half]).astype(low), along),
+        Flow(inner_rows(upstream, hidden[:, half:]).astype(low), across),
+    ]
+    gate_grad, up_grad = tie((gate_grad, up_grad), start=down)
+    gated = [
+        Flow(inner_rows(second_all, gate_grad).astype(low), along),
+        Flow(inner_rows(second_all, up_grad).astype(low), across),
+    ]
+    gate_grad, up_grad = tie((gate_grad, up_grad), start=gated, end=down)
+    gate_grad, up_grad = tie((gate_grad, up_grad), start=down)
     if paired:
         middle_grad, middle_all, gain_two_part = middle_back(
             gate_grad, up_grad, gate_weight, up_weight, middle, cotangent, second_gain
@@ -734,24 +761,49 @@
         )
         gain_two_part = jnp.sum(second_grad * normed_two, axis=0, keepdims=True)
         middle_all = gather(middle_grad.astype(low))
-    grad_output = inner_rows(middle_all, gated_out).astype(low)
+    middle_all, outgate = tie((middle_all, outgate), end=down)
+    middle_all, outgate = tie((middle_all, outgate), start=down)
     gated_grad = against(middle_all, output_weight)
     mixed_grad = (gated_grad * outgate).astype(low)
     outgate_grad = (gated_grad * mixed_out * outgate * (1.0 - outgate)).astype(low)
-    grad_outgate = inner_rows(first_all, outgate_grad).astype(low)
-    mixed_grad, grad_output, grad_outgate = lax.optimization_barrier(
-        (mixed_grad, grad_output, grad_outgate)
-    )
+    width = query_weight.shape[1]
+    shared = Flow(
+        jnp.concatenate(
+            [inner_rows(middle_all, gated_out).astype(low), inner_rows(first_all, outgate_grad).astype(low)],
+            axis=1,
+        ),
+        deep,
+    )
+    mixed_grad = tie(mixed_grad, start=[shared])
     query_grad, key_grad, value_grad, forget_rows = attend_backward(
         query_rows, key_rows, value_rows, mixed_grad, peaks, logit_t, segment, head_dim
     )
-    grad_query = inner_rows(first_all, query_grad).astype(low)
-    grad_key = inner_rows(first_all, key_grad).astype(low)
-    grad_value = inner_rows(first_all, value_grad).astype(low)
+    query_grad, key_grad, value_grad, forget_rows = tie(
+        (query_grad, key_grad, value_grad, forget_rows), end=down + gated
+    )
+    query_grad, key_grad, value_grad, forget_rows = tie(
+        (query_grad, key_grad, value_grad, forget_rows), start=down + gated
+    )
     forget_grad = forget_rows[:local_heads]
     grad_forget = lax.dot_general(
         first_all, forget_grad, (((0,), (1,)), ((), ())), preferred_element_type=jnp.float32
-    ).astype(low)
+    )
+    inward = [
+        Flow(
+            jnp.concatenate([inner_rows(first_all, query_grad).astype(low), grad_forget.astype(low)], axis=1),
+            along,
+        ),
+        Flow(inner_rows(first_all, key_grad).astype(low), across),
+        Flow(inner_rows(first_all, value_grad).astype(low), deep),
+    ]
+    query_grad, hidden = tie((query_grad, hidden), start=inward)
+    if paired:
+        result = result_rows(hidden, down_weight, middle)
+    else:
+        rows = scatter(matmul(hidden, down_weight).astype(low)).astype(jnp.float32)
+        result = (middle + rows).astype(low)
+    result, query_grad = tie((result, query_grad), end=gated + [shared])
+    query_grad = tie(query_grad, start=gated + [shared])
     bias_part = jnp.sum(forget_grad.astype(jnp.float32), axis=1)
     forget_t = forget_weight.T
     if paired:
@@ -784,26 +836,36 @@
             jnp.zeros((5, tokens.shape[1]), jnp.float32),
         ]
     )
-    sums = all_sum(shares)
-    width = grad_query.shape[1]
-    query_part = spread_sum(jnp.concatenate([grad_query, grad_forget], axis=1), along)
+    live = down + gated + [shared] + inward
+    tokens_grad, shares = tie((tokens_grad, shares), end=live)
+    first = True
+    while live:
+        live = [flow for flow in live if not flow.done()]
+        if not live:
+            break
+        shares = tie(shares, start=live)
+        if first:
+            sums = all_sum(shares)
+            shares = sums
+            first = False
+        shares = tie(shares, end=live)
+    sums = shares
+    query_part, shared_part = inward[0].whole, shared.whole
     return (
-        result_rows(hidden, down_weight, middle)
-        if paired
-        else (middle + scatter(matmul(hidden, down_weight).astype(low)).astype(jnp.float32)).astype(low),
+        result,
         tokens_grad,
         sums[0],
         query_part[:, :width],
-        spread_sum(grad_key, across),
-        spread_sum(grad_value, deep),
-        spread_sum(grad_outgate, across),
+        inward[1].whole,
+        inward[2].whole,
+        shared_part[:, width:],
         query_part[:, width:],
         sums[2, :all_heads],
-        spread_sum(grad_output, along).T,
+        shared_part[:, :width].T,
         sums[1],
-        spread_sum(grad_gate, along),
-        spread_sum(grad_up, across),
-        jnp.concatenate([spread_sum(down_front, along), spread_sum(down_back, across)], axis=1).T,
+        gated[0].whole,
+        gated[1].whole,
+        jnp.concatenate([down[0].whole, down[1].whole], axis=1).T,
     )
 
 

time: 650 us -> 552 us (0.85)
  waiting for transfers between devices: 236 us -> 80.7 us
  other arithmetic: 31.3 us -> 53 us
  local copies, waits for them, and re-layouts: 59.4 us -> 78.4 us
  Pallas kernels: 164 us -> 182 us
  matrix products: 116 us -> 108 us
    ppermute x36 -> x32, waiting for transfers between devices: 236 us -> 80.7 us  [fly(): self.got = lax.ppermute(self.sent, 'dp', pairs)]
    pallas_call x1, Pallas kernels: 18 us -> 36.1 us  [all_sum(): pl.pallas_call(partial(all_sum_body, bits), out_shape=jax.ShapeDtypeStruc...]
    convert_element_type x27 -> x23, other arithmetic: 20.2 us -> 37.9 us  [land(): self.whole = total.astype(jnp.bfloat16)]
    squeeze x28 -> x26, local copies, waits for them, and re-layouts: 3.05 us -> 19.2 us  [cut(): lax.dynamic_index_in_dim(self.whole, 1 - mine, axis, keepdims=False)]
    dynamic_slice x15 -> x12, local copies, waits for them, and re-layouts: 37.5 us -> 22.6 us  [the longest x6 14.1 us: cut(): self.kept = lax.dynamic_index_in_dim(self.whole, mine, axis, keepdims=False)]
    unnamed x93 -> x129, local copies, waits for them, and re-layouts: 8.27 us -> 19 us
    dot_general x9, matrix products: 50.6 us -> 43.4 us  [inner_rows(): lax.dot_general(former, latter, (((0,), (0,)), ((), ())), preferred_eleme...]
    concatenate x1 -> x2, local copies, waits for them, and re-layouts: 3.21 us -> 9.85 us  [the longest x1 6.64 us: local(): jnp.concatenate([inner_rows(middle_all, gated_out).astype(low), inner_row...]
  transfers between devices with their start and end apart: 36 -> 32, of which waited for: 23 -> 11; matrix products, arithmetic and copies ran while one was open for 19% -> 19% of each run, Pallas kernels for 19% -> 26%
where the time goes in v3:
time: 552 us; the launch traced here: 543 us
  Pallas kernels  182 us (33%)
  matrix products  108 us (20%)
  waiting for transfers between devices  80.7 us (15%)
  local copies, waits for them, and re-layouts  78.4 us (14%)
  other arithmetic  53 us (10%)
  starting transfers between devices  38.1 us (7%)
    ppermute x32, waiting for transfers between devices, fly(): self.got = lax.ppermute(self.sent, 'dp', pairs)  80.7 us
    dot_general x9, matrix products, inner_rows(): lax.dot_general(former, latter, (((0,), (0,)), ((), ())), preferred_eleme...  43.4 us
    dot_general x6, matrix products, matmul(): return jnp.dot(former, latter, preferred_element_type=jnp.float32)  40.2 us
    ppermute x32, starting transfers between devices, fly(): self.got = lax.ppermute(self.sent, 'dp', pairs)  38.1 us
    convert_element_type x23, other arithmetic, land(): self.whole = total.astype(jnp.bfloat16)  37.9 us
    pallas_call x1, Pallas kernels, all_sum(): pl.pallas_call(partial(all_sum_body, bits), out_shape=jax.ShapeDtypeStruc...  36.1 us
    pallas_call x1, Pallas kernels, attend_backward(): pl.pallas_call(partial(backward_body, head_dim=head_dim, spans=spans, hea...  34.4 us
    pallas_call x1, Pallas kernels, middle_back(): pl.pallas_call(back_body, out_shape=[jax.ShapeDtypeStruct((half, width),...  30.1 us
  transfers between devices with their start and end apart: 32, of which 11 were waited for; matrix products, arithmetic and copies ran while one was open for 19% of the time, Pallas kernels for 26%

profile of v3, /device:TPU:0, one launch (start us, length us, event | category | flops | bytes accessed | tf_op | source)
XLA Modules:
  0.0 542.7 jit_solution(4547444836000699405)
XLA Ops:
  2.1 5.4 %norm_gather.1 = bf16[1024,1536]{1,0:T(8,128)(2,1)} custom-call(bf16[512,1536]{1,0:T(8,128)(2,1)} %token_ref.5, f32[1,1536]{1,0:T(1,128)} %reshape.125.gain_ref), custom_call_target="tpu_custom_call" | custom-call | flops 6291456 | bytes 9437184 | tf_op jit(solution)/shard_map/norm_gather/pallas_call | solution.py:573
  7.6 6.6 %add_divide_fusion.1.gate_ref = f32[1024,768]{1,0:T(8,128)} fusion(bf16[1024,1536]{1,0:T(8,128)(2,1)} %norm_gather.1, bf16[1536,768]{1,0:T(8,128)(2,1)S(1)} %copy-done.52), kind=kOutput, calls=%fused_computation.35 | convolution fusion | flops 2418278400 | bytes 8650752 | tf_op jit(solution)/shard_map/dot_general | solution.py:15
  14.2 3.7 convolution_convert_fusion.10.v_ref
  17.9 3.7 convolution_convert_fusion.11.k_ref
  21.6 2.6 convolution_convert_fusion.12.q_ref
  25.2 2.8 fusion.22
  28.1 20.6 %attend_forward.1 = (f32[1024,768]{1,0:T(8,128)}, bf16[1024,768]{1,0:T(8,128)(2,1)S(1)}, f32[1024,768]{1,0:T(8,128)}) custom-call(bf16[1024,768]{1,0:T(8,128)(2,1)S(1)} %convolution_convert_fusion.12.q_ref, bf16[1024,768]{1,0:T(8,128)(2,1)} %convolution_convert_fusion.11.k_ref, bf16[1024,768]{1,0:T(8,128)(2,1)} %convolution_convert_fusion.10.v_ref, ...), custom_call_target="tpu_custom_call" | custom-call | flops 7247757312 | bytes 15728640 | tf_op jit(solution)/shard_map/attend_forward/pallas_call | solution.py:199
  49.9 15.7 %project.1 = (f32[512,1536]{1,0:T(8,128)}, bf16[1024,1536]{1,0:T(8,128)(2,1)}, bf16[1024,1536]{1,0:T(8,128)(2,1)}) custom-call(bf16[1024,768]{1,0:T(8,128)(2,1)} %copy-done.2, bf16[768,1536]{1,0:T(8,128)(2,1)} %weight_ref.2, bf16[512,1536]{1,0:T(8,128)(2,1)} %token_ref.5, bf16[512,1536]{1,0:T(8,128)(2,1)} %cot_ref.3, f32[1,1536]{1,0:T(1,128)} %reshape.126.gain_ref), custom_call_target="tpu_custom_call" | custom-call | flops 2415919104 | bytes 18874368 | tf_op jit(solution)/shard_map/project/pallas_call | solution.py:594
  65.6 12.7 %fusion.29 = f32[1024,2048]{1,0:T(8,128)} fusion(bf16[1024,1536]{1,0:T(8,128)(2,1)} %get-tuple-element.129, bf16[1536,2048]{1,0:T(8,128)(2,1)} %gate_weight_ref.1), kind=kOutput, calls=%fused_computation.141 | convolution fusion | flops 6442450944 | bytes 17825792 | tf_op jit(solution)/shard_map/dot_general | solution.py:15
  78.3 11.0 %fusion.30 = f32[1024,2048]{1,0:T(8,128)} fusion(bf16[1024,1536]{1,0:T(8,128)(2,1)S(1)} %copy-done.53, bf16[1536,2048]{1,0:T(8,128)(2,1)} %up_weight_ref.1), kind=kOutput, calls=%fused_computation.142 | convolution fusion | flops 6442450944 | bytes 17825792 | tf_op jit(solution)/shard_map/dot_general | solution.py:15
  89.4 17.4 %multiply_convert_fusion = (bf16[1024,2048]{1,0:T(8,128)(2,1)}, bf16[1024,2048]{1,0:T(8,128)(2,1)}, bf16[1024,2048]{1,0:T(8,128)(2,1)}) fusion(f32[1024,2048]{1,0:T(8,128)} %fusion.29, f32[1024,2048]{1,0:T(8,128)} %fusion.30, bf16[1024,1536]{1,0:T(8,128)(2,1)S(1)} %copy-done.55, bf16[2048,1536]{1,0:T(8,128)(2,1)} %weight_ref.3), kind=kOutput, calls=%fused_computation | convolution fusion | flops 6473908224 | bytes 38797312 | tf_op jit(solution)/shard_map/dot_general | solution.py:25
  106.8 6.6 %convolution_convert_fusion.2 = bf16[1536,1024]{1,0:T(8,128)(2,1)} fusion(bf16[1024,1536]{1,0:T(8,128)(2,1)S(1)} %copy-done.55, bf16[1024,2048]{1,0:T(8,128)(2,1)} %get-tuple-element.177.hidden_ref), kind=kOutput, calls=%fused_computation.14 | convolution fusion | flops 3222798336 | bytes 8388608 | tf_op jit(solution)/shard_map/dot_general | solution.py:19
  113.4 4.9 convolution_convert_fusion.3
  118.3 3.3 constant_dynamic-slice_fusion.6
  123.0 3.4 constant_dynamic-slice_fusion.7
  127.6 2.8 collective-permute-start
  132.0 10.0 %convolution_convert_fusion = bf16[1536,2048]{1,0:T(8,128)(2,1)S(1)} fusion(bf16[1024,1536]{1,0:T(8,128)(2,1)} %get-tuple-element.129, bf16[1024,2048]{1,0:T(8,128)(2,1)} %get-tuple-element.143.up_ref), kind=kOutput, calls=%fused_computation.5 | convolution fusion | flops 6445596672 | bytes 13631488 | tf_op jit(solution)/shard_map/dot_general | solution.py:19
  142.0 2.5 constant_dynamic-slice_fusion.4
  144.6 1.9 copy.93
  147.7 7.2 %convolution_convert_fusion.1 = bf16[1536,2048]{1,0:T(8,128)(2,1)S(1)} fusion(bf16[1024,1536]{1,0:T(8,128)(2,1)S(1)} %copy-done.54, bf16[1024,2048]{1,0:T(8,128)(2,1)S(1)} %copy-done.62), kind=kOutput, calls=%fused_computation.6 | convolution fusion | flops 6445596672 | bytes 13631488 | tf_op jit(solution)/shard_map/dot_general | solution.py:19
  155.0 2.5 constant_dynamic-slice_fusion.5
  157.5 1.8 copy.94
  160.0 5.3 collective-permute-done
  166.9 4.4 fusion.6
  178.4 30.1 %middle_back.1 = (f32[512,1536]{1,0:T(8,128)}, bf16[1024,1536]{1,0:T(8,128)(2,1)}, f32[8,1536]{1,0:T(8,128)}) custom-call(bf16[1024,2048]{1,0:T(8,128)(2,1)} %get-tuple-element.142.gate_ref, bf16[1024,2048]{1,0:T(8,128)(2,1)} %get-tuple-element.143.up_ref, bf16[1536,2048]{1,0:T(8,128)(2,1)} %gate_weight_ref.1, bf16[1536,2048]{1,0:T(8,128)(2,1)} %up_weight_ref.1, ...), custom_call_target="tpu_custom_call" | custom-call | flops 12884901888 | bytes 39321600 | tf_op jit(solution)/shard_map/middle_back/pallas_call | solution.py:629
  209.3 1.8 fusion.16
  213.7 2.9 convolution_convert_fusion.8
  217.3 4.0 multiply_convert_fusion.3
  221.3 2.9 convolution_convert_fusion.7
  224.2 2.5 pad_maximum_fusion
  226.6 6.6 %copy.53 = bf16[1536,1536]{1,0:T(8,128)(2,1)} copy(bf16[1536,1536]{0,1:T(8,128)(2,1)} %pad_maximum_fusion) | data formatting | bytes 9437184 | tf_op jit(solution)/shard_map/concatenate | solution.py:771
  233.3 3.3 dynamic-slice_bitcast_fusion
  240.1 34.4 %attend_backward.1 = (bf16[1024,768]{1,0:T(8,128)(2,1)S(1)}, bf16[1024,768]{1,0:T(8,128)(2,1)S(1)}, bf16[1024,768]{1,0:T(8,128)(2,1)}, bf16[16,1024]{1,0:T(8,128)(2,1)S(1)}) custom-call(bf16[1024,768]{1,0:T(8,128)(2,1)} %copy-done.6, bf16[1024,768]{1,0:T(8,128)(2,1)} %convolution_convert_fusion.11.k_ref, bf16[1024,768]{1,0:T(8,128)(2,1)} %convolution_convert_fusion.10.v_ref, ...), custom_call_target="tpu_custom_call" | custom-call | flops 18119393280 | bytes 15728640 | tf_op jit(solution)/shard_map/attend_backward/pallas_call | solution.py:302
  274.6 4.8 fusion.1
  283.0 3.6 fusion.2
  291.3 2.9 convolution_convert_fusion.4
  294.2 2.9 convolution_convert_fusion.5
  302.4 2.9 convolution_convert_fusion.6
  309.7 3.2 copy.57
  315.6 15.7 %result_rows.1 = bf16[512,1536]{1,0:T(8,128)(2,1)} custom-call(bf16[1024,2048]{1,0:T(8,128)(2,1)} %get-tuple-element.177.hidden_ref, bf16[2048,1536]{1,0:T(8,128)(2,1)} %weight_ref.3, f32[512,1536]{1,0:T(8,128)} %get-tuple-element.144.middle_ref), custom_call_target="tpu_custom_call" | custom-call | flops 6442450944 | bytes 23592960 | tf_op jit(solution)/shard_map/result_rows/pallas_call | solution.py:613
  331.9 5.2 collective-permute-done.8
  337.1 2.6 collective-permute-start.11
  341.2 3.0 fusion.3
  344.2 2.9 fusion.4
  350.3 2.0 fusion.5
  353.7 8.9 %collective-permute-done.11 = bf16[96,1024]{1,0:T(8,128)(2,1)S(1)} collective-permute-done((bf16[96,1024]{1,0:T(8,128)(2,1)S(1)}, bf16[96,1024]{1,0:T(8,128)(2,1)S(1)}, u32[]{:S(2)}, u32[]{:S(2)}) %collective-permute-start.11) | collective-permute-done | bytes 196640 | tf_op jit(solution)/shard_map/ppermute | solution.py:64
  364.2 2.2 collective-permute-done.12
  366.4 4.6 collective-permute-start.13
  371.1 24.0 %first_back.1 = (f32[512,1536]{1,0:T(8,128)}, f32[8,1536]{1,0:T(8,128)}) custom-call(bf16[1024,768]{1,0:T(8,128)(2,1)} %copy-done.4, bf16[1024,768]{1,0:T(8,128)(2,1)} %copy-done.5, bf16[1024,768]{1,0:T(8,128)(2,1)} %get-tuple-element.176.value_ref, bf16[1024,768]{1,0:T(8,128)(2,1)} %copy-done.60, bf16[16,1024]{1,0:T(8,128)(2,1)} %copy-done, ...), custom_call_target="tpu_custom_call" | custom-call | flops 9663676416 | bytes 31457280 | tf_op jit(solution)/shard_map/first_back/pallas_call | solution.py:651
  396.7 8.9 %collective-permute-done.14 = bf16[2,96,2048]{2,1,0:T(8,128)(2,1)} collective-permute-done((bf16[2,96,2048]{2,1,0:T(8,128)(2,1)}, bf16[2,96,2048]{2,1,0:T(8,128)(2,1)}, u32[]{:S(2)}, u32[]{:S(2)}) %collective-permute-start.14) | collective-permute-done | bytes 786464 | tf_op jit(solution)/shard_map/ppermute | solution.py:64
  405.6 1.9 fusion.9
  412.2 1.7 fusion.8
  415.9 1.7 fusion.11
  428.7 36.1 %all_sum.1 = f32[8,1536]{1,0:T(8,128)} custom-call(f32[8,1536]{1,0:T(8,128)} %maximum_maximum_fusion.part_ref), custom_call_target="tpu_custom_call" | custom-call | tf_op jit(solution)/shard_map/all_sum/pallas_call | solution.py:669
  466.9 13.8 %collective-permute-done.20 = bf16[96,2048]{1,0:T(8,128)(2,1)S(1)} collective-permute-done((bf16[96,2048]{1,0:T(8,128)(2,1)}, bf16[96,2048]{1,0:T(8,128)(2,1)S(1)}, u32[]{:S(2)}, u32[]{:S(2)}) %collective-permute-start.20) | collective-permute-done | bytes 393248 | tf_op jit(solution)/shard_map/ppermute | solution.py:64
  480.7 2.0 convert_add_fusion.19
  491.3 2.0 convert_add_fusion.20
  493.2 9.4 %collective-permute-done.25 = bf16[96,1536]{1,0:T(8,128)(2,1)S(1)} collective-permute-done((bf16[96,1536]{1,0:T(8,128)(2,1)S(1)}, bf16[96,1536]{1,0:T(8,128)(2,1)S(1)}, u32[]{:S(2)}, u32[]{:S(2)}) %collective-permute-start.25) | collective-permute-done | bytes 294944 | tf_op jit(solution)/shard_map/ppermute | solution.py:64
  502.6 7.2 %collective-permute-done.27 = bf16[2,96,768]{2,1,0:T(8,128)(2,1)S(1)} collective-permute-done((bf16[2,96,768]{2,1,0:T(8,128)(2,1)S(1)}, bf16[2,96,768]{2,1,0:T(8,128)(2,1)S(1)}, u32[]{:S(2)}, u32[]{:S(2)}) %collective-permute-start.27) | collective-permute-done | bytes 294944 | tf_op jit(solution)/shard_map/ppermute | solution.py:64
  510.3 2.9 collective-permute-start.30
  514.2 15.1 %collective-permute-done.30 = bf16[96,768]{1,0:T(8,128)(2,1)S(1)} collective-permute-done((bf16[96,768]{1,0:T(8,128)(2,1)S(1)}, bf16[96,768]{1,0:T(8,128)(2,1)S(1)}, u32[]{:S(2)}, u32[]{:S(2)}) %collective-permute-start.30) | collective-permute-done | bytes 147488 | tf_op jit(solution)/shard_map/ppermute | solution.py:64
  529.2 3.1 collective-permute-done.31
  537.9 2.7 copy.102
  540.6 1.7 copy.103
  (250 shorter events, 91.5 us)
Async XLA Ops:
  0.6 6.9 %copy-start.52 = (bf16[1536,768]{1,0:T(8,128)(2,1)S(1)}, bf16[1536,768]{1,0:T(8,128)(2,1)}, u32[]{:S(2)}) copy-start(bf16[1536,768]{1,0:T(8,128)(2,1)} %wg_ref.1) | copy-start | bytes 7077892
  7.6 6.6 %copy-start.7 = (bf16[1024,1536]{1,0:T(8,128)(2,1)S(1)}, bf16[1024,1536]{1,0:T(8,128)(2,1)}, u32[]{:S(2)}) copy-start(bf16[1024,1536]{1,0:T(8,128)(2,1)} %norm_gather.1) | copy-start | bytes 9437188
  7.6 6.6 %copy-start.51 = (bf16[1536,768]{1,0:T(8,128)(2,1)S(1)}, bf16[1536,768]{1,0:T(8,128)(2,1)}, u32[]{:S(2)}) copy-start(bf16[1536,768]{1,0:T(8,128)(2,1)} %wv_ref.1) | copy-start | bytes 7077892
  24.2 24.5 %copy-start.6 = (bf16[1024,768]{1,0:T(8,128)(2,1)}, bf16[1024,768]{1,0:T(8,128)(2,1)S(1)}, u32[]{:S(2)}) copy-start(bf16[1024,768]{1,0:T(8,128)(2,1)S(1)} %convolution_convert_fusion.12.q_ref) | copy-start | bytes 4718596
  65.6 12.7 %copy-start.53 = (bf16[1024,1536]{1,0:T(8,128)(2,1)S(1)}, bf16[1024,1536]{1,0:T(8,128)(2,1)}, u32[]{:S(2)}) copy-start(bf16[1024,1536]{1,0:T(8,128)(2,1)} %get-tuple-element.129) | copy-start | bytes 9437188
  78.3 11.0 %copy-start.55 = (bf16[1024,1536]{1,0:T(8,128)(2,1)S(1)}, bf16[1024,1536]{1,0:T(8,128)(2,1)}, u32[]{:S(2)}) copy-start(bf16[1024,1536]{1,0:T(8,128)(2,1)} %get-tuple-element.130) | copy-start | bytes 9437188
  106.8 6.7 %copy-start.59 = (bf16[1024,2048]{1,0:T(8,128)(2,1)S(1)}, bf16[1024,2048]{1,0:T(8,128)(2,1)}, u32[]{:S(2)}) copy-start(bf16[1024,2048]{1,0:T(8,128)(2,1)} %get-tuple-element.177.hidden_ref) | copy-start | bytes 12582916
  127.6 37.8 %collective-permute-start = (bf16[2,2,2,96,1024]{4,3,0,1,2:T(8,128)(2,1)}, bf16[2,2,2,96,1024]{4,3,0,1,2:T(8,128)(2,1)S(1)}, u32[]{:S(2)}, u32[]{:S(2)}) collective-permute-start(bf16[2,2,2,96,1024]{4,3,0,1,2:T(8,128)(2,1)} %bitcast.229), channel_id=1, source_target_pairs={{0,2},{2,0},{4,6},{6,4},{8,10},{10,8},{12,14},{14,12},{16,18},{18,... | collective-permute-start | bytes 4718600 | tf_op jit(solution)/shard_map/ppermute | solution.py:64
  130.5 36.5 %collective-permute-start.1 = (bf16[2,2,2,96,1024]{4,3,0,1,2:T(8,128)(2,1)}, bf16[2,2,2,96,1024]{4,3,0,1,2:T(8,128)(2,1)}, u32[]{:S(2)}, u32[]{:S(2)}) collective-permute-start(bf16[2,2,2,96,1024]{4,3,0,1,2:T(8,128)(2,1)} %bitcast.228), channel_id=1, source_target_pairs={{0,4},{2,6},{4,0},{6,2},{8,12},{10,14},{12,8},{14,10},{16,20},{18,... | collective-permute-start | bytes 4718600 | tf_op jit(solution)/shard_map/ppermute | solution.py:64
  142.0 4.4 copy-start.62
  174.3 35.0 %collective-permute-start.2 = (bf16[2,2,96,1024]{3,2,0,1:T(8,128)(2,1)}, bf16[2,2,96,1024]{3,2,0,1:T(8,128)(2,1)S(1)}, u32[]{:S(2)}, u32[]{:S(2)}) collective-permute-start(bf16[2,2,96,1024]{3,2,0,1:T(8,128)(2,1)} %dynamic-slice_bitcast_fusion.8), channel_id=1, source_target_pairs={{0,4},{2,6},{4,0},{6,2},{8,12},{10,14},{12,8},{14,10},{16,20},{18,... | collective-permute-start | bytes 2359304 | tf_op jit(solution)/shard_map/ppermute | solution.py:64
  175.8 33.5 %collective-permute-start.3 = (bf16[2,2,96,1024]{3,2,0,1:T(8,128)(2,1)}, bf16[2,2,96,1024]{3,2,0,1:T(8,128)(2,1)}, u32[]{:S(2)}, u32[]{:S(2)}) collective-permute-start(bf16[2,2,96,1024]{3,2,0,1:T(8,128)(2,1)} %dynamic-slice_bitcast_fusion.7), channel_id=1, source_target_pairs={{0,2},{2,0},{4,6},{6,4},{8,10},{10,8},{12,14},{14,12},{16,18},{18,... | collective-permute-start | bytes 2359304 | tf_op jit(solution)/shard_map/ppermute | solution.py:64
  177.2 97.4 %collective-permute-start.6 = (bf16[2,2,2,96,2048]{4,3,0,1,2:T(8,128)(2,1)}, bf16[2,2,2,96,2048]{4,3,0,1,2:T(8,128)(2,1)}, u32[]{:S(2)}, u32[]{:S(2)}) collective-permute-start(bf16[2,2,2,96,2048]{4,3,0,1,2:T(8,128)(2,1)} %bitcast.227), channel_id=1, source_target_pairs={{0,2},{2,0},{4,6},{6,4},{8,10},{10,8},{12,14},{14,12},{16,18},{18,... | collective-permute-start | bytes 9437192 | tf_op jit(solution)/shard_map/ppermute | solution.py:64
  177.8 96.7 %collective-permute-start.7 = (bf16[2,2,2,96,2048]{4,3,0,1,2:T(8,128)(2,1)}, bf16[2,2,2,96,2048]{4,3,0,1,2:T(8,128)(2,1)}, u32[]{:S(2)}, u32[]{:S(2)}) collective-permute-start(bf16[2,2,2,96,2048]{4,3,0,1,2:T(8,128)(2,1)} %bitcast.226), channel_id=1, source_target_pairs={{0,4},{2,6},{4,0},{6,2},{8,12},{10,14},{12,8},{14,10},{16,20},{18,... | collective-permute-start | bytes 9437192 | tf_op jit(solution)/shard_map/ppermute | solution.py:64
  209.3 4.4 copy-start.3
  209.3 4.4 copy-start.58
  236.5 38.0 %collective-permute-start.4 = (bf16[2,96,1024]{2,1,0:T(8,128)(2,1)}, bf16[2,96,1024]{2,1,0:T(8,128)(2,1)S(1)}, u32[]{:S(2)}, u32[]{:S(2)}) collective-permute-start(bf16[2,96,1024]{2,1,0:T(8,128)(2,1)} %dynamic-slice_bitcast_fusion.16), channel_id=1, source_target_pairs={{0,8},{2,10},{4,12},{6,14},{8,0},{10,2},{12,4},{14,6},{16,24},{18,... | collective-permute-start | bytes 1179656 | tf_op jit(solution)/shard_map/ppermute | solution.py:64
  238.1 36.5 %collective-permute-start.5 = (bf16[2,96,1024]{2,1,0:T(8,128)(2,1)S(1)}, bf16[2,96,1024]{2,1,0:T(8,128)(2,1)S(1)}, u32[]{:S(2)}, u32[]{:S(2)}) collective-permute-start(bf16[2,96,1024]{2,1,0:T(8,128)(2,1)S(1)} %dynamic-slice_bitcast_fusion.15), channel_id=1, source_target_pairs={{0,8},{2,10},{4,12},{6,14},{8,0},{10,2},{12,4},{14,6},{16,24},{18,... | collective-permute-start | bytes 1179656 | tf_op jit(solution)/shard_map/ppermute | solution.py:64
  238.6 92.8 %collective-permute-start.10 = (bf16[2,2,2,96,1536]{4,3,2,1,0:T(8,128)(2,1)}, bf16[2,2,2,96,1536]{4,3,2,1,0:T(8,128)(2,1)}, u32[]{:S(2)}, u32[]{:S(2)}) collective-permute-start(bf16[2,2,2,96,1536]{4,3,2,1,0:T(8,128)(2,1)} %dynamic-slice_bitcast_fusion), channel_id=1, source_target_pairs={{0,8},{2,10},{4,12},{6,14},{8,0},{10,2},{12,4},{14,6},{16,24},{18,... | collective-permute-start | bytes 7077896 | tf_op jit(solution)/shard_map/ppermute | solution.py:64
  240.1 34.5 %copy-start.14 = (bf16[2,2,1,2,96,2048]{5,4,3,2,1,0:T(8,128)(2,1)S(1)}, bf16[2,2,1,2,96,2048]{5,4,3,2,1,0:T(8,128)(2,1)}, u32[]{:S(2)}) copy-start(bf16[2,2,1,2,96,2048]{5,4,3,2,1,0:T(8,128)(2,1)} %get-tuple-element.275) | copy-start | bytes 9437188
  274.5 19.7 %copy-start.5 = (bf16[1024,768]{1,0:T(8,128)(2,1)}, bf16[1024,768]{1,0:T(8,128)(2,1)S(1)}, u32[]{:S(2)}) copy-start(bf16[1024,768]{1,0:T(8,128)(2,1)S(1)} %get-tuple-element.175.key_ref) | copy-start | bytes 4718596
  274.5 27.9 %copy-start.4 = (bf16[1024,768]{1,0:T(8,128)(2,1)}, bf16[1024,768]{1,0:T(8,128)(2,1)S(1)}, u32[]{:S(2)}) copy-start(bf16[1024,768]{1,0:T(8,128)(2,1)S(1)} %get-tuple-element.187.query_ref) | copy-start | bytes 4718596
  274.5 40.8 %copy-start = (bf16[16,1024]{1,0:T(8,128)(2,1)}, bf16[16,1024]{1,0:T(8,128)(2,1)S(1)}, u32[]{:S(2)}) copy-start(bf16[16,1024]{1,0:T(8,128)(2,1)S(1)} %get-tuple-element.174.forget_ref) | copy-start | bytes 98308
  274.5 4.9 copy-start.38
  274.6 4.9 copy-start.40
  283.0 5.0 copy-start.32
  283.0 5.0 copy-start.41
  286.7 4.1 copy-start.9
  286.7 4.6 copy-start.61
  288.9 5.3 copy-start.37
  299.5 37.6 %collective-permute-start.8 = (bf16[2,2,96,2048]{3,2,0,1:T(8,128)(2,1)}, bf16[2,2,96,2048]{3,2,0,1:T(8,128)(2,1)}, u32[]{:S(2)}, u32[]{:S(2)}) collective-permute-start(bf16[2,2,96,2048]{3,2,0,1:T(8,128)(2,1)} %dynamic-slice_bitcast_fusion.2), channel_id=1, source_target_pairs={{0,4},{2,6},{4,0},{6,2},{8,12},{10,14},{12,8},{14,10},{16,20},{18,... | collective-permute-start | bytes 4718600 | tf_op jit(solution)/shard_map/ppermute | solution.py:64
  301.0 38.7 %collective-permute-start.9 = (bf16[2,2,96,2048]{3,2,0,1:T(8,128)(2,1)}, bf16[2,2,96,2048]{3,2,0,1:T(8,128)(2,1)}, u32[]{:S(2)}, u32[]{:S(2)}) collective-permute-start(bf16[2,2,96,2048]{3,2,0,1:T(8,128)(2,1)} %dynamic-slice_bitcast_fusion.1), channel_id=1, source_target_pairs={{0,2},{2,0},{4,6},{6,4},{8,10},{10,8},{12,14},{14,12},{16,18},{18,... | collective-permute-start | bytes 4718600 | tf_op jit(solution)/shard_map/ppermute | solution.py:64
  314.1 82.6 %collective-permute-start.16 = (bf16[2,2,2,96,780]{4,3,2,1,0:T(8,128)(2,1)}, bf16[2,2,2,96,780]{4,3,2,1,0:T(8,128)(2,1)}, u32[]{:S(2)}, u32[]{:S(2)}) collective-permute-start(bf16[2,2,2,96,780]{4,3,2,1,0:T(8,128)(2,1)} %dynamic-slice_bitcast_fusion.3), channel_id=1, source_target_pairs={{0,2},{2,0},{4,6},{6,4},{8,10},{10,8},{12,14},{14,12},{16,18},{18,... | collective-permute-start | bytes 3594248 | tf_op jit(solution)/shard_map/ppermute | solution.py:64
  314.8 56.3 %collective-permute-start.17 = (bf16[2,2,2,96,768]{4,3,0,1,2:T(8,128)(2,1)}, bf16[2,2,2,96,768]{4,3,0,1,2:T(8,128)(2,1)}, u32[]{:S(2)}, u32[]{:S(2)}) collective-permute-start(bf16[2,2,2,96,768]{4,3,0,1,2:T(8,128)(2,1)} %bitcast.244), channel_id=1, source_target_pairs={{0,4},{2,6},{4,0},{6,2},{8,12},{10,14},{12,8},{14,10},{16,20},{18,... | collective-permute-start | bytes 3538952 | tf_op jit(solution)/shard_map/ppermute | solution.py:64
  315.6 21.5 %copy-start.43 = (bf16[96,1024]{1,0:T(8,128)(2,1)S(1)}, bf16[96,1024]{1,0:T(8,128)(2,1)}, u32[]{:S(2)}) copy-start(bf16[96,1024]{1,0:T(8,128)(2,1)} %dynamic-slice_bitcast_fusion.22) | copy-start | bytes 589828
  331.4 12.9 %copy-start.11 = (bf16[2,2,2,96,2048]{4,3,0,1,2:T(8,128)(2,1)S(1)}, bf16[2,2,2,96,2048]{4,3,0,1,2:T(8,128)(2,1)}, u32[]{:S(2)}) copy-start(bf16[2,2,2,96,2048]{4,3,0,1,2:T(8,128)(2,1)} %copy-done.10) | copy-start | bytes 9437188
  331.4 65.3 %collective-permute-start.18 = (bf16[2,2,2,96,768]{4,3,0,2,1:T(8,128)(2,1)}, bf16[2,2,2,96,768]{4,3,0,2,1:T(8,128)(2,1)}, u32[]{:S(2)}, u32[]{:S(2)}) collective-permute-start(bf16[2,2,2,96,768]{4,3,0,2,1:T(8,128)(2,1)} %bitcast.243), channel_id=1, source_target_pairs={{0,8},{2,10},{4,12},{6,14},{8,0},{10,2},{12,4},{14,6},{16,24},{18,... | collective-permute-start | bytes 3538952 | tf_op jit(solution)/shard_map/ppermute | solution.py:64
  337.1 25.6 %collective-permute-start.11 = (bf16[96,1024]{1,0:T(8,128)(2,1)S(1)}, bf16[96,1024]{1,0:T(8,128)(2,1)S(1)}, u32[]{:S(2)}, u32[]{:S(2)}) collective-permute-start(bf16[96,1024]{1,0:T(8,128)(2,1)S(1)} %copy-done.43), channel_id=1, source_target_pairs={{0,16},{2,18},{4,20},{6,22},{8,24},{10,26},{12,28},{14,30},{16,0},... | collective-permute-start | bytes 589832 | tf_op jit(solution)/shard_map/ppermute | solution.py:64
  339.7 26.8 %collective-permute-start.12 = (bf16[96,1024]{1,0:T(8,128)(2,1)S(1)}, bf16[96,1024]{1,0:T(8,128)(2,1)S(1)}, u32[]{:S(2)}, u32[]{:S(2)}) collective-permute-start(bf16[96,1024]{1,0:T(8,128)(2,1)S(1)} %dynamic-slice_bitcast_fusion.21), channel_id=1, source_target_pairs={{0,16},{2,18},{4,20},{6,22},{8,24},{10,26},{12,28},{14,30},{16,0},... | collective-permute-start | bytes 589832 | tf_op jit(solution)/shard_map/ppermute | solution.py:64
  347.1 5.2 copy-start.18
  362.7 42.9 %collective-permute-start.15 = (bf16[2,2,96,1536]{3,2,1,0:T(8,128)(2,1)}, bf16[2,2,96,1536]{3,2,1,0:T(8,128)(2,1)}, u32[]{:S(2)}, u32[]{:S(2)}) collective-permute-start(bf16[2,2,96,1536]{3,2,1,0:T(8,128)(2,1)} %dynamic-slice_bitcast_fusion.4), channel_id=1, source_target_pairs={{0,4},{2,6},{4,0},{6,2},{8,12},{10,14},{12,8},{14,10},{16,20},{18,... | collective-permute-start | bytes 3538952 | tf_op jit(solution)/shard_map/ppermute | solution.py:64
  366.4 28.7 %copy-start.44 = (bf16[96,1024]{1,0:T(8,128)(2,1)}, bf16[96,1024]{1,0:T(8,128)(2,1)S(1)}, u32[]{:S(2)}) copy-start(bf16[96,1024]{1,0:T(8,128)(2,1)S(1)} %collective-permute-done.12) | copy-start | bytes 589828
  366.4 30.3 %collective-permute-start.13 = (bf16[2,96,2048]{2,1,0:T(8,128)(2,1)}, bf16[2,96,2048]{2,1,0:T(8,128)(2,1)}, u32[]{:S(2)}, u32[]{:S(2)}) collective-permute-start(bf16[2,96,2048]{2,1,0:T(8,128)(2,1)} %dynamic-slice_bitcast_fusion.6), channel_id=1, source_target_pairs={{0,8},{2,10},{4,12},{6,14},{8,0},{10,2},{12,4},{14,6},{16,24},{18,... | collective-permute-start | bytes 2359304 | tf_op jit(solution)/shard_map/ppermute | solution.py:64
  371.1 34.5 %collective-permute-start.14 = (bf16[2,96,2048]{2,1,0:T(8,128)(2,1)}, bf16[2,96,2048]{2,1,0:T(8,128)(2,1)}, u32[]{:S(2)}, u32[]{:S(2)}) collective-permute-start(bf16[2,96,2048]{2,1,0:T(8,128)(2,1)} %dynamic-slice_bitcast_fusion.5), channel_id=1, source_target_pairs={{0,8},{2,10},{4,12},{6,14},{8,0},{10,2},{12,4},{14,6},{16,24},{18,... | collective-permute-start | bytes 2359304 | tf_op jit(solution)/shard_map/ppermute | solution.py:64
  396.0 12.7 %copy-start.25 = (bf16[2,2,1,2,96,768]{5,4,3,2,1,0:T(8,128)(2,1)S(1)}, bf16[2,2,1,2,96,768]{5,4,3,2,1,0:T(8,128)(2,1)}, u32[]{:S(2)}) copy-start(bf16[2,2,1,2,96,768]{5,4,3,2,1,0:T(8,128)(2,1)} %get-tuple-element.287) | copy-start | bytes 3538948
  411.3 4.6 copy-start.17
  415.9 4.9 copy-start.21
  422.3 60.5 %copy-start.27 = (bf16[2,2,2,96,768]{4,3,0,2,1:T(8,128)(2,1)S(1)}, bf16[2,2,2,96,768]{4,3,0,2,1:T(8,128)(2,1)}, u32[]{:S(2)}) copy-start(bf16[2,2,2,96,768]{4,3,0,2,1:T(8,128)(2,1)} %copy-done.26) | copy-start | bytes 3538948
  423.0 41.8 %collective-permute-start.19 = (bf16[96,2048]{1,0:T(8,128)(2,1)}, bf16[96,2048]{1,0:T(8,128)(2,1)}, u32[]{:S(2)}, u32[]{:S(2)}) collective-permute-start(bf16[96,2048]{1,0:T(8,128)(2,1)} %dynamic-slice_bitcast_fusion.14), channel_id=1, source_target_pairs={{0,16},{2,18},{4,20},{6,22},{8,24},{10,26},{12,28},{14,30},{16,0},... | collective-permute-start | bytes 1179656 | tf_op jit(solution)/shard_map/ppermute | solution.py:64
  423.6 57.2 %collective-permute-start.22 = (bf16[2,2,96,780]{3,2,1,0:T(8,128)(2,1)}, bf16[2,2,96,780]{3,2,1,0:T(8,128)(2,1)}, u32[]{:S(2)}, u32[]{:S(2)}) collective-permute-start(bf16[2,2,96,780]{3,2,1,0:T(8,128)(2,1)} %dynamic-slice_bitcast_fusion.9), channel_id=1, source_target_pairs={{0,4},{2,6},{4,0},{6,2},{8,12},{10,14},{12,8},{14,10},{16,20},{18,... | collective-permute-start | bytes 1797128 | tf_op jit(solution)/shard_map/ppermute | solution.py:64
  425.1 55.6 %collective-permute-start.21 = (bf16[2,96,1536]{2,1,0:T(8,128)(2,1)}, bf16[2,96,1536]{2,1,0:T(8,128)(2,1)}, u32[]{:S(2)}, u32[]{:S(2)}) collective-permute-start(bf16[2,96,1536]{2,1,0:T(8,128)(2,1)} %dynamic-slice_bitcast_fusion.12), channel_id=1, source_target_pairs={{0,2},{2,0},{4,6},{6,4},{8,10},{10,8},{12,14},{14,12},{16,18},{18,... | collective-permute-start | bytes 1769480 | tf_op jit(solution)/shard_map/ppermute | solution.py:64
  426.5 54.3 %collective-permute-start.23 = (bf16[2,2,96,768]{3,2,0,1:T(8,128)(2,1)}, bf16[2,2,96,768]{3,2,0,1:T(8,128)(2,1)}, u32[]{:S(2)}, u32[]{:S(2)}) collective-permute-start(bf16[2,2,96,768]{3,2,0,1:T(8,128)(2,1)} %dynamic-slice_bitcast_fusion.11), channel_id=1, source_target_pairs={{0,2},{2,0},{4,6},{6,4},{8,10},{10,8},{12,14},{14,12},{16,18},{18,... | collective-permute-start | bytes 1769480 | tf_op jit(solution)/shard_map/ppermute | solution.py:64
  427.1 53.6 %collective-permute-start.24 = (bf16[2,2,96,768]{3,2,0,1:T(8,128)(2,1)}, bf16[2,2,96,768]{3,2,0,1:T(8,128)(2,1)}, u32[]{:S(2)}, u32[]{:S(2)}) collective-permute-start(bf16[2,2,96,768]{3,2,0,1:T(8,128)(2,1)} %dynamic-slice_bitcast_fusion.10), channel_id=1, source_target_pairs={{0,4},{2,6},{4,0},{6,2},{8,12},{10,14},{12,8},{14,10},{16,20},{18,... | collective-permute-start | bytes 1769480 | tf_op jit(solution)/shard_map/ppermute | solution.py:64
  464.8 19.2 %copy-start.29 = (bf16[2,2,2,96,768]{4,3,0,1,2:T(8,128)(2,1)S(1)}, bf16[2,2,2,96,768]{4,3,0,1,2:T(8,128)(2,1)}, u32[]{:S(2)}) copy-start(bf16[2,2,2,96,768]{4,3,0,1,2:T(8,128)(2,1)} %copy-done.28) | copy-start | bytes 3538948
  464.8 15.9 %collective-permute-start.20 = (bf16[96,2048]{1,0:T(8,128)(2,1)}, bf16[96,2048]{1,0:T(8,128)(2,1)S(1)}, u32[]{:S(2)}, u32[]{:S(2)}) collective-permute-start(bf16[96,2048]{1,0:T(8,128)(2,1)} %dynamic-slice_bitcast_fusion.13), channel_id=1, source_target_pairs={{0,16},{2,18},{4,20},{6,22},{8,24},{10,26},{12,28},{14,30},{16,0},... | collective-permute-start | bytes 1179656 | tf_op jit(solution)/shard_map/ppermute | solution.py:64
  466.9 18.3 %copy-start.24 = (bf16[2,2,2,96,780]{4,3,2,1,0:T(8,128)(2,1)S(1)}, bf16[2,2,2,96,780]{4,3,2,1,0:T(8,128)(2,1)}, u32[]{:S(2)}) copy-start(bf16[2,2,2,96,780]{4,3,2,1,0:T(8,128)(2,1)} %copy-done.23) | copy-start | bytes 3594244
  487.8 22.0 %collective-permute-start.26 = (bf16[2,96,780]{2,1,0:T(8,128)(2,1)S(1)}, bf16[2,96,780]{2,1,0:T(8,128)(2,1)S(1)}, u32[]{:S(2)}, u32[]{:S(2)}) collective-permute-start(bf16[2,96,780]{2,1,0:T(8,128)(2,1)S(1)} %dynamic-slice_bitcast_fusion.17), channel_id=1, source_target_pairs={{0,8},{2,10},{4,12},{6,14},{8,0},{10,2},{12,4},{14,6},{16,24},{18,... | collective-permute-start | bytes 898568 | tf_op jit(solution)/shard_map/ppermute | solution.py:64
  487.9 14.8 %collective-permute-start.25 = (bf16[96,1536]{1,0:T(8,128)(2,1)S(1)}, bf16[96,1536]{1,0:T(8,128)(2,1)S(1)}, u32[]{:S(2)}, u32[]{:S(2)}) collective-permute-start(bf16[96,1536]{1,0:T(8,128)(2,1)S(1)} %dynamic-slice_bitcast_fusion.20), channel_id=1, source_target_pairs={{0,16},{2,18},{4,20},{6,22},{8,24},{10,26},{12,28},{14,30},{16,0},... | collective-permute-start | bytes 884744 | tf_op jit(solution)/shard_map/ppermute | solution.py:64
  489.1 20.7 %collective-permute-start.27 = (bf16[2,96,768]{2,1,0:T(8,128)(2,1)S(1)}, bf16[2,96,768]{2,1,0:T(8,128)(2,1)S(1)}, u32[]{:S(2)}, u32[]{:S(2)}) collective-permute-start(bf16[2,96,768]{2,1,0:T(8,128)(2,1)S(1)} %dynamic-slice_bitcast_fusion.19), channel_id=1, source_target_pairs={{0,8},{2,10},{4,12},{6,14},{8,0},{10,2},{12,4},{14,6},{16,24},{18,... | collective-permute-start | bytes 884744 | tf_op jit(solution)/shard_map/ppermute | solution.py:64
  489.9 19.9 %collective-permute-start.28 = (bf16[2,96,768]{2,1,0:T(8,128)(2,1)S(1)}, bf16[2,96,768]{2,1,0:T(8,128)(2,1)S(1)}, u32[]{:S(2)}, u32[]{:S(2)}) collective-permute-start(bf16[2,96,768]{2,1,0:T(8,128)(2,1)S(1)} %dynamic-slice_bitcast_fusion.18), channel_id=1, source_target_pairs={{0,2},{2,0},{4,6},{6,4},{8,10},{10,8},{12,14},{14,12},{16,18},{18,... | collective-permute-start | bytes 884744 | tf_op jit(solution)/shard_map/ppermute | solution.py:64
  510.2 22.0 %collective-permute-start.29 = (bf16[96,780]{1,0:T(8,128)(2,1)S(1)}, bf16[96,780]{1,0:T(8,128)(2,1)S(1)}, u32[]{:S(2)}, u32[]{:S(2)}) collective-permute-start(bf16[96,780]{1,0:T(8,128)(2,1)S(1)} %dynamic-slice_bitcast_fusion.23), channel_id=1, source_target_pairs={{0,16},{2,18},{4,20},{6,22},{8,24},{10,26},{12,28},{14,30},{16,0},... | collective-permute-start | bytes 449288 | tf_op jit(solution)/shard_map/ppermute | solution.py:64
  510.3 18.9 %collective-permute-start.30 = (bf16[96,768]{1,0:T(8,128)(2,1)S(1)}, bf16[96,768]{1,0:T(8,128)(2,1)S(1)}, u32[]{:S(2)}, u32[]{:S(2)}) collective-permute-start(bf16[96,768]{1,0:T(8,128)(2,1)S(1)} %dynamic-slice_bitcast_fusion.25), channel_id=1, source_target_pairs={{0,16},{2,18},{4,20},{6,22},{8,24},{10,26},{12,28},{14,30},{16,0},... | collective-permute-start | bytes 442376 | tf_op jit(solution)/shard_map/ppermute | solution.py:64
  513.2 19.1 %collective-permute-start.31 = (bf16[96,768]{1,0:T(8,128)(2,1)S(1)}, bf16[96,768]{1,0:T(8,128)(2,1)S(1)}, u32[]{:S(2)}, u32[]{:S(2)}) collective-permute-start(bf16[96,768]{1,0:T(8,128)(2,1)S(1)} %dynamic-slice_bitcast_fusion.24), channel_id=1, source_target_pairs={{0,16},{2,18},{4,20},{6,22},{8,24},{10,26},{12,28},{14,30},{16,0},... | collective-permute-start | bytes 442376 | tf_op jit(solution)/shard_map/ppermute | solution.py:64
  514.2 26.4 %copy-start.30 = (f32[512,1536]{1,0:T(8,128)S(1)}, f32[512,1536]{1,0:T(8,128)}, u32[]{:S(2)}) copy-start(f32[512,1536]{1,0:T(8,128)} %get-tuple-element.308) | copy-start | bytes 9437188
  (31 other events, 79.7 us)

commit v4 on v3

--- a/solution.py
+++ b/solution.py
@@ -44,9 +44,11 @@
         for front, back in swap:
             self.order[front], self.order[back] = self.order[back], self.order[front]
         self.live = list(range(self.bits - 1, -1, -1))
-        self.whole = gradient.reshape(
-            (2,) * self.bits + (gradient.shape[0] // self.count, gradient.shape[1])
-        )
+        gradients = gradient if isinstance(gradient, list) else [gradient]
+        self.wholes = [
+            one.reshape((2,) * self.bits + (one.shape[0] // self.count, one.shape[1]))
+            for one in gradients
+        ]
         self.stage = 0
         self.cut()
 
@@ -55,8 +57,10 @@
         axis = self.live.index(bit)
         self.live.pop(axis)
         mine = (lax.axis_index("dp") >> bit) & 1
-        self.sent = lax.dynamic_index_in_dim(self.whole, 1 - mine, axis, keepdims=False)
-        self.kept = lax.dynamic_index_in_dim(self.whole, mine, axis, keepdims=False)
+        pick = lambda side: jnp.concatenate(
+            [lax.dynamic_index_in_dim(one, side, axis, keepdims=False) for one in self.wholes], axis=-1
+        )
+        self.sent, self.kept = pick(1 - mine), pick(mine)
 
     def fly(self):
         bit = self.order[self.stage]
@@ -69,11 +73,18 @@
         if self.stage == self.bits:
             self.whole = total
             return
-        self.whole = total.astype(jnp.bfloat16)
+        self.wholes = [total.astype(jnp.bfloat16)]
         self.cut()
 
     def done(self):
         return self.stage == self.bits
+
+
+def merged(flows):
+    front = flows[0]
+    front.sent = jnp.concatenate([flow.sent for flow in flows], axis=-1)
+    front.kept = jnp.concatenate([flow.kept for flow in flows], axis=-1)
+    return front
 
 
 def tie(values, start=(), end=()):
@@ -762,16 +773,14 @@
         gain_two_part = jnp.sum(second_grad * normed_two, axis=0, keepdims=True)
         middle_all = gather(middle_grad.astype(low))
     middle_all, outgate = tie((middle_all, outgate), end=down)
+    down = [merged(down)]
     middle_all, outgate = tie((middle_all, outgate), start=down)
     gated_grad = against(middle_all, output_weight)
     mixed_grad = (gated_grad * outgate).astype(low)
     outgate_grad = (gated_grad * mixed_out * outgate * (1.0 - outgate)).astype(low)
     width = query_weight.shape[1]
     shared = Flow(
-        jnp.concatenate(
-            [inner_rows(middle_all, gated_out).astype(low), inner_rows(first_all, outgate_grad).astype(low)],
-            axis=1,
-        ),
+        [inner_rows(middle_all, gated_out).astype(low), inner_rows(first_all, outgate_grad).astype(low)],
         deep,
     )
     mixed_grad = tie(mixed_grad, start=[shared])
@@ -785,12 +794,14 @@
         (query_grad, key_grad, value_grad, forget_rows), start=down + gated
     )
     forget_grad = forget_rows[:local_heads]
+    spare = -(query_weight.shape[1] + local_heads) % 128
     grad_forget = lax.dot_general(
-        first_all, forget_grad, (((0,), (1,)), ((), ())), preferred_element_type=jnp.float32
+        first_all, jnp.pad(forget_grad, ((0, spare), (0, 0))), (((0,), (1,)), ((), ())),
+        preferred_element_type=jnp.float32,
     )
     inward = [
         Flow(
-            jnp.concatenate([inner_rows(first_all, query_grad).astype(low), grad_forget.astype(low)], axis=1),
+            [inner_rows(first_all, query_grad).astype(low), grad_forget.astype(low)],
             along,
         ),
         Flow(inner_rows(first_all, key_grad).astype(low), across),
@@ -803,6 +814,7 @@
         rows = scatter(matmul(hidden, down_weight).astype(low)).astype(jnp.float32)
         result = (middle + rows).astype(low)
     result, query_grad = tie((result, query_grad), end=gated + [shared])
+    gated = [merged(gated)]
     query_grad = tie(query_grad, start=gated + [shared])
     bias_part = jnp.sum(forget_grad.astype(jnp.float32), axis=1)
     forget_t = forget_weight.T
@@ -838,34 +850,38 @@
     )
     live = down + gated + [shared] + inward
     tokens_grad, shares = tie((tokens_grad, shares), end=live)
-    first = True
-    while live:
-        live = [flow for flow in live if not flow.done()]
-        if not live:
+    while True:
+        flying = [flow for flow in live if not flow.done()]
+        last = all(flow.stage == flow.bits - 1 for flow in flying)
+        shares = tie(shares, start=flying)
+        if last:
+            shares = all_sum(shares)
+        shares = tie(shares, end=flying)
+        if inward[0].stage == 2:
+            inward[:2] = [merged(inward[:2])]
+            live = [flow for flow in live if flow not in flying] + [shared] + gated + down + inward
+            live = list(dict.fromkeys(live))
+        if last:
             break
-        shares = tie(shares, start=live)
-        if first:
-            sums = all_sum(shares)
-            shares = sums
-            first = False
-        shares = tie(shares, end=live)
     sums = shares
-    query_part, shared_part = inward[0].whole, shared.whole
+    inner = inward[0].whole
+    shared_part = shared.whole
+    after = inner.shape[1] - width
     return (
         result,
         tokens_grad,
         sums[0],
-        query_part[:, :width],
+        inner[:, :width],
+        inner[:, after:],
         inward[1].whole,
-        inward[2].whole,
         shared_part[:, width:],
-        query_part[:, width:],
+        inner[:, width : width + local_heads],
         sums[2, :all_heads],
         shared_part[:, :width].T,
         sums[1],
-        gated[0].whole,
-        gated[1].whole,
-        jnp.concatenate([down[0].whole, down[1].whole], axis=1).T,
+        gated[0].whole[:, : gate_weight.shape[1]],
+        gated[0].whole[:, gate_weight.shape[1] :],
+        down[0].whole.T,
     )
 
 

time: 552 us -> 519 us (0.940)
  local copies, waits for them, and re-layouts: 78.4 us -> 60 us
  Pallas kernels: 182 us -> 172 us
  other arithmetic: 53 us -> 47.1 us
    dynamic_slice x12 -> x8, local copies, waits for them, and re-layouts: 22.6 us -> 5.11 us  [cut(): lax.dynamic_index_in_dim(one, side, axis, keepdims=False)]
    pallas_call x1, Pallas kernels: 36.1 us -> 26.1 us  [all_sum(): pl.pallas_call(partial(all_sum_body, bits), out_shape=jax.ShapeDtypeStruc...]
    concatenate x2 -> x0, local copies, waits for them, and re-layouts: 9.85 us -> none  [the longest x1 6.64 us: local(): jnp.concatenate([inner_rows(middle_all, gated_out).astype(low), inner_row...]
    squeeze x26 -> x28, local copies, waits for them, and re-layouts: 19.2 us -> 24.7 us  [cut(): lax.dynamic_index_in_dim(one, side, axis, keepdims=False)]
    convert_element_type x23 -> x20, other arithmetic: 37.9 us -> 35.3 us  [land(): self.wholes = [total.astype(jnp.bfloat16)]]
    unnamed x129 -> x125, local copies, waits for them, and re-layouts: 19 us -> 21.2 us
    ppermute x32 -> x26, waiting for transfers between devices: 80.7 us -> 79.3 us  [fly(): self.got = lax.ppermute(self.sent, 'dp', pairs)]
    ppermute x32 -> x26, starting transfers between devices: 38.1 us -> 36.8 us  [fly(): self.got = lax.ppermute(self.sent, 'dp', pairs)]
  transfers between devices with their start and end apart: 32 -> 26, of which waited for: 11 -> 12; matrix products, arithmetic and copies ran while one was open for 19% -> 18% of each run, Pallas kernels for 26% -> 25%
where the time goes in v4:
time: 519 us; the launch traced here: 511 us
  Pallas kernels  172 us (33%)
  matrix products  113 us (22%)
  waiting for transfers between devices  79.3 us (15%)
  local copies, waits for them, and re-layouts  60 us (12%)
  other arithmetic  47.1 us (9%)
  starting transfers between devices  36.8 us (7%)
    ppermute x26, waiting for transfers between devices, fly(): self.got = lax.ppermute(self.sent, 'dp', pairs)  79.3 us
    dot_general x9, matrix products, inner_rows(): lax.dot_general(former, latter, (((0,), (0,)), ((), ())), preferred_eleme...  45.9 us
    dot_general x6, matrix products, matmul(): return jnp.dot(former, latter, preferred_element_type=jnp.float32)  40.2 us
    ppermute x26, starting transfers between devices, fly(): self.got = lax.ppermute(self.sent, 'dp', pairs)  36.8 us
    convert_element_type x20, other arithmetic, land(): self.wholes = [total.astype(jnp.bfloat16)]  35.3 us
    pallas_call x1, Pallas kernels, attend_backward(): pl.pallas_call(partial(backward_body, head_dim=head_dim, spans=spans, hea...  34.3 us
    pallas_call x1, Pallas kernels, middle_back(): pl.pallas_call(back_body, out_shape=[jax.ShapeDtypeStruct((half, width),...  30 us
    pallas_call x1, Pallas kernels, all_sum(): pl.pallas_call(partial(all_sum_body, bits), out_shape=jax.ShapeDtypeStruc...  26.1 us
  transfers between devices with their start and end apart: 26, of which 12 were waited for; matrix products, arithmetic and copies ran while one was open for 18% of the time, Pallas kernels for 25%

profile of v4, /device:TPU:0, one launch (start us, length us, event | category | flops | bytes accessed | tf_op | source)
XLA Modules:
  0.0 510.6 jit_solution(17915486341731883946)
XLA Ops:
  1.9 5.6 %norm_gather.1 = bf16[1024,1536]{1,0:T(8,128)(2,1)} custom-call(bf16[512,1536]{1,0:T(8,128)(2,1)} %token_ref.5, f32[1,1536]{1,0:T(1,128)} %reshape.109.gain_ref), custom_call_target="tpu_custom_call" | custom-call | flops 6291456 | bytes 9437184 | tf_op jit(solution)/shard_map/norm_gather/pallas_call | solution.py:584
  7.6 6.6 %add_divide_fusion.1.gate_ref = f32[1024,768]{1,0:T(8,128)} fusion(bf16[1024,1536]{1,0:T(8,128)(2,1)} %norm_gather.1, bf16[1536,768]{1,0:T(8,128)(2,1)S(1)} %copy-done.50), kind=kOutput, calls=%fused_computation.32 | convolution fusion | flops 2418278400 | bytes 8650752 | tf_op jit(solution)/shard_map/dot_general | solution.py:15
  14.2 3.7 convolution_convert_fusion.10.v_ref
  17.8 3.7 convolution_convert_fusion.11.k_ref
  21.5 2.6 convolution_convert_fusion.12.q_ref
  25.2 2.8 fusion.18
  28.1 20.6 %attend_forward.1 = (f32[1024,768]{1,0:T(8,128)}, bf16[1024,768]{1,0:T(8,128)(2,1)S(1)}, f32[1024,768]{1,0:T(8,128)}) custom-call(bf16[1024,768]{1,0:T(8,128)(2,1)S(1)} %convolution_convert_fusion.12.q_ref, bf16[1024,768]{1,0:T(8,128)(2,1)} %convolution_convert_fusion.11.k_ref, bf16[1024,768]{1,0:T(8,128)(2,1)} %convolution_convert_fusion.10.v_ref, ...), custom_call_target="tpu_custom_call" | custom-call | flops 7247757312 | bytes 15728640 | tf_op jit(solution)/shard_map/attend_forward/pallas_call | solution.py:210
  49.9 15.7 %project.1 = (f32[512,1536]{1,0:T(8,128)}, bf16[1024,1536]{1,0:T(8,128)(2,1)}, bf16[1024,1536]{1,0:T(8,128)(2,1)}) custom-call(bf16[1024,768]{1,0:T(8,128)(2,1)} %copy-done.2, bf16[768,1536]{1,0:T(8,128)(2,1)} %weight_ref.2, bf16[512,1536]{1,0:T(8,128)(2,1)} %token_ref.5, bf16[512,1536]{1,0:T(8,128)(2,1)} %cot_ref.3, f32[1,1536]{1,0:T(1,128)} %reshape.110.gain_ref), custom_call_target="tpu_custom_call" | custom-call | flops 2415919104 | bytes 18874368 | tf_op jit(solution)/shard_map/project/pallas_call | solution.py:605
  65.6 12.7 %fusion.25 = f32[1024,2048]{1,0:T(8,128)} fusion(bf16[1024,1536]{1,0:T(8,128)(2,1)} %get-tuple-element.117, bf16[1536,2048]{1,0:T(8,128)(2,1)} %gate_weight_ref.1), kind=kOutput, calls=%fused_computation.131 | convolution fusion | flops 6442450944 | bytes 17825792 | tf_op jit(solution)/shard_map/dot_general | solution.py:15
  78.3 11.0 %fusion.26 = f32[1024,2048]{1,0:T(8,128)} fusion(bf16[1024,1536]{1,0:T(8,128)(2,1)S(1)} %copy-done.51, bf16[1536,2048]{1,0:T(8,128)(2,1)} %up_weight_ref.1), kind=kOutput, calls=%fused_computation.132 | convolution fusion | flops 6442450944 | bytes 17825792 | tf_op jit(solution)/shard_map/dot_general | solution.py:15
  89.3 17.4 %multiply_convert_fusion = (bf16[1024,2048]{1,0:T(8,128)(2,1)}, bf16[1024,2048]{1,0:T(8,128)(2,1)}, bf16[1024,2048]{1,0:T(8,128)(2,1)}) fusion(f32[1024,2048]{1,0:T(8,128)} %fusion.25, f32[1024,2048]{1,0:T(8,128)} %fusion.26, bf16[1024,1536]{1,0:T(8,128)(2,1)S(1)} %copy-done.52, bf16[2048,1536]{1,0:T(8,128)(2,1)} %weight_ref.3), kind=kOutput, calls=%fused_computation | convolution fusion | flops 6473908224 | bytes 38797312 | tf_op jit(solution)/shard_map/dot_general | solution.py:25
  106.7 6.6 %convolution_convert_fusion.2 = bf16[1536,1024]{1,0:T(8,128)(2,1)} fusion(bf16[1024,1536]{1,0:T(8,128)(2,1)S(1)} %copy-done.52, bf16[1024,2048]{1,0:T(8,128)(2,1)} %get-tuple-element.163.hidden_ref), kind=kOutput, calls=%fused_computation.12 | convolution fusion | flops 3222798336 | bytes 8388608 | tf_op jit(solution)/shard_map/dot_general | solution.py:19
  113.4 4.9 convolution_convert_fusion.3
  118.3 2.7 dynamic-slice_bitcast_fusion.4
  120.9 2.7 dynamic-slice_bitcast_fusion.5
  123.6 2.9 collective-permute-start
  128.0 10.0 %convolution_convert_fusion = bf16[1536,2048]{1,0:T(8,128)(2,1)S(1)} fusion(bf16[1024,1536]{1,0:T(8,128)(2,1)} %get-tuple-element.117, bf16[1024,2048]{1,0:T(8,128)(2,1)} %get-tuple-element.131.up_ref), kind=kOutput, calls=%fused_computation.5 | convolution fusion | flops 6445596672 | bytes 13631488 | tf_op jit(solution)/shard_map/dot_general | solution.py:19
  138.0 2.7 copy-done.13
  140.7 2.0 dynamic-slice_bitcast_fusion
  142.7 9.6 %convolution_convert_fusion.1 = bf16[1536,2048]{1,0:T(8,128)(2,1)S(1)} fusion(bf16[1024,1536]{1,0:T(8,128)(2,1)} %get-tuple-element.117, bf16[1024,2048]{1,0:T(8,128)(2,1)} %get-tuple-element.130.gate_ref), kind=kOutput, calls=%fused_computation.6 | convolution fusion | flops 6445596672 | bytes 13631488 | tf_op jit(solution)/shard_map/dot_general | solution.py:19
  152.4 2.0 dynamic-slice_bitcast_fusion.1
  154.5 2.6 copy-done.14
  157.1 4.3 collective-permute-done
  163.0 3.5 fusion.5
  172.8 30.0 %middle_back.1 = (f32[512,1536]{1,0:T(8,128)}, bf16[1024,1536]{1,0:T(8,128)(2,1)}, f32[8,1536]{1,0:T(8,128)}) custom-call(bf16[1024,2048]{1,0:T(8,128)(2,1)} %get-tuple-element.130.gate_ref, bf16[1024,2048]{1,0:T(8,128)(2,1)} %get-tuple-element.131.up_ref, bf16[1536,2048]{1,0:T(8,128)(2,1)} %gate_weight_ref.1, bf16[1536,2048]{1,0:T(8,128)(2,1)} %up_weight_ref.1, ...), custom_call_target="tpu_custom_call" | custom-call | flops 12884901888 | bytes 39321600 | tf_op jit(solution)/shard_map/middle_back/pallas_call | solution.py:640
  202.9 1.6 fusion.13
  204.5 1.6 fusion.12
  208.1 6.0 %multiply_convert_fusion.3 = (bf16[1024,768]{1,0:T(8,128)(2,1)S(1)}, bf16[1024,768]{1,0:T(8,128)(2,1)}) fusion(f32[1024,768]{1,0:T(8,128)S(1)} %copy-done.53, f32[1024,768]{1,0:T(8,128)S(1)} %copy-done.54, bf16[1024,1536]{1,0:T(8,128)(2,1)} %get-tuple-element.140, bf16[768,1536]{1,0:T(8,128)(2,1)S(1)} %copy-done.46), kind=kOutput, calls=%fused_computation.28 | convolution fusion | flops 2421424128 | bytes 14942208 | tf_op jit(solution)/shard_map/dot_general | solution.py:25
  214.1 3.0 convolution_convert_fusion.8
  217.4 1.6 copy-done.8
  219.0 2.9 convolution_convert_fusion.7
  225.8 34.3 %attend_backward.1 = (bf16[1024,768]{1,0:T(8,128)(2,1)S(1)}, bf16[1024,768]{1,0:T(8,128)(2,1)S(1)}, bf16[1024,768]{1,0:T(8,128)(2,1)}, bf16[16,1024]{1,0:T(8,128)(2,1)S(1)}) custom-call(bf16[1024,768]{1,0:T(8,128)(2,1)} %copy-done.6, bf16[1024,768]{1,0:T(8,128)(2,1)} %convolution_convert_fusion.11.k_ref, bf16[1024,768]{1,0:T(8,128)(2,1)} %convolution_convert_fusion.10.v_ref, ...), custom_call_target="tpu_custom_call" | custom-call | flops 18119393280 | bytes 15728640 | tf_op jit(solution)/shard_map/attend_backward/pallas_call | solution.py:313
  262.4 5.3 %fusion.1 = bf16[2,2,2,96,2048]{4,3,2,1,0:T(8,128)(2,1)S(1)} fusion(bf16[2,2,2,96,2048]{4,3,2,1,0:T(8,128)(2,1)} %collective-permute-done.6, bf16[2,2,2,2,96,2048]{5,4,3,2,1,0:T(8,128)(2,1)} %bitcast.220, s32[]{:T(128)S(6)} %select_n.108), kind=kLoop, calls=%fused_computation.8 | loop fusion | flops 6291456 | bytes 9437188 | tf_op jit(solution)/shard_map/convert_element_type | solution.py:76
  269.0 3.4 fusion.2
  276.3 2.9 convolution_convert_fusion.4
  279.2 2.9 convolution_convert_fusion.5
  282.2 1.6 collective-permute-start.7
  289.7 2.9 convolution_convert_fusion.6
  295.0 2.6 collective-permute-start.10
  297.6 15.7 %result_rows.1 = bf16[512,1536]{1,0:T(8,128)(2,1)} custom-call(bf16[1024,2048]{1,0:T(8,128)(2,1)} %get-tuple-element.163.hidden_ref, bf16[2048,1536]{1,0:T(8,128)(2,1)} %weight_ref.3, f32[512,1536]{1,0:T(8,128)} %get-tuple-element.132.middle_ref), custom_call_target="tpu_custom_call" | custom-call | flops 6442450944 | bytes 23592960 | tf_op jit(solution)/shard_map/result_rows/pallas_call | solution.py:624
  313.4 5.1 collective-permute-done.7
  319.7 2.5 fusion.4
  324.4 2.0 fusion.3
  338.2 24.0 %first_back.1 = (f32[512,1536]{1,0:T(8,128)}, f32[8,1536]{1,0:T(8,128)}) custom-call(bf16[1024,768]{1,0:T(8,128)(2,1)} %copy-done.4, bf16[1024,768]{1,0:T(8,128)(2,1)} %copy-done.5, bf16[1024,768]{1,0:T(8,128)(2,1)} %get-tuple-element.162.value_ref, bf16[1024,768]{1,0:T(8,128)(2,1)} %copy-done.57, bf16[16,1024]{1,0:T(8,128)(2,1)} %copy-done, ...), custom_call_target="tpu_custom_call" | custom-call | flops 9663676416 | bytes 31457280 | tf_op jit(solution)/shard_map/first_back/pallas_call | solution.py:662
  364.7 27.3 %collective-permute-done.15 = bf16[2,2,2,96,768]{4,3,0,2,1:T(8,128)(2,1)} collective-permute-done((bf16[2,2,2,96,768]{4,3,0,2,1:T(8,128)(2,1)}, bf16[2,2,2,96,768]{4,3,0,2,1:T(8,128)(2,1)}, u32[]{:S(2)}, u32[]{:S(2)}) %collective-permute-start.15) | collective-permute-done | bytes 1179680 | tf_op jit(solution)/shard_map/ppermute | solution.py:68
  392.0 2.1 fusion.7
  395.0 1.7 fusion.8
  397.9 1.7 add_convert_fusion.2
  400.6 1.7 fusion.9
  403.4 1.9 add_convert_fusion.1
  406.3 2.6 collective-permute-start.16
  412.9 2.1 fusion.19
  415.0 10.7 %collective-permute-done.17 = bf16[2,96,1536]{2,1,0:T(8,128)(2,1)} collective-permute-done((bf16[2,96,1536]{2,1,0:T(8,128)(2,1)S(1)}, bf16[2,96,1536]{2,1,0:T(8,128)(2,1)}, u32[]{:S(2)}, u32[]{:S(2)}) %collective-permute-start.17) | collective-permute-done | bytes 589856 | tf_op jit(solution)/shard_map/ppermute | solution.py:68
  425.7 8.8 %collective-permute-done.19 = bf16[2,2,96,768]{3,2,1,0:T(8,128)(2,1)} collective-permute-done((bf16[2,2,96,768]{3,2,1,0:T(8,128)(2,1)}, bf16[2,2,96,768]{3,2,1,0:T(8,128)(2,1)}, u32[]{:S(2)}, u32[]{:S(2)}) %collective-permute-start.19) | collective-permute-done | bytes 589856 | tf_op jit(solution)/shard_map/ppermute | solution.py:68
  434.5 2.0 collective-permute-done.20
  436.5 4.9 collective-permute-done.16
  449.0 3.4 collective-permute-start.21
  455.0 12.8 %collective-permute-done.21 = bf16[96,1536]{1,0:T(8,128)(2,1)S(1)} collective-permute-done((bf16[96,1536]{1,0:T(8,128)(2,1)S(1)}, bf16[96,1536]{1,0:T(8,128)(2,1)S(1)}, u32[]{:S(2)}, u32[]{:S(2)}) %collective-permute-start.21) | collective-permute-done | bytes 294944 | tf_op jit(solution)/shard_map/ppermute | solution.py:68
  468.9 2.7 collective-permute-start.24
  472.0 26.1 %all_sum.1 = f32[8,1536]{1,0:T(8,128)} custom-call(f32[8,1536]{1,0:T(8,128)} %maximum_maximum_fusion.part_ref), custom_call_target="tpu_custom_call" | custom-call | tf_op jit(solution)/shard_map/all_sum/pallas_call | solution.py:680
  500.6 1.7 slice_reduce_fusion
  503.5 1.7 convert_add_fusion.20
  505.9 2.7 copy.89
  508.5 1.7 copy.90
  (228 shorter events, 77.6 us)
Async XLA Ops:
  1.9 5.6 %copy-start.50 = (bf16[1536,768]{1,0:T(8,128)(2,1)S(1)}, bf16[1536,768]{1,0:T(8,128)(2,1)}, u32[]{:S(2)}) copy-start(bf16[1536,768]{1,0:T(8,128)(2,1)} %wg_ref.1) | copy-start | bytes 7077892
  7.5 6.6 %copy-start.7 = (bf16[1024,1536]{1,0:T(8,128)(2,1)S(1)}, bf16[1024,1536]{1,0:T(8,128)(2,1)}, u32[]{:S(2)}) copy-start(bf16[1024,1536]{1,0:T(8,128)(2,1)} %norm_gather.1) | copy-start | bytes 9437188
  7.6 6.6 %copy-start.49 = (bf16[1536,768]{1,0:T(8,128)(2,1)S(1)}, bf16[1536,768]{1,0:T(8,128)(2,1)}, u32[]{:S(2)}) copy-start(bf16[1536,768]{1,0:T(8,128)(2,1)} %wv_ref.1) | copy-start | bytes 7077892
  14.1 3.7 copy-start.48
  17.8 3.7 copy-start.47
  21.5 2.9 copy-start.44
  21.5 3.7 copy-start.40
  21.5 3.7 copy-start.45
  24.1 3.9 copy-start.6
  65.6 12.7 %copy-start.51 = (bf16[1024,1536]{1,0:T(8,128)(2,1)S(1)}, bf16[1024,1536]{1,0:T(8,128)(2,1)}, u32[]{:S(2)}) copy-start(bf16[1024,1536]{1,0:T(8,128)(2,1)} %get-tuple-element.117) | copy-start | bytes 9437188
  78.3 11.0 %copy-start.52 = (bf16[1024,1536]{1,0:T(8,128)(2,1)S(1)}, bf16[1024,1536]{1,0:T(8,128)(2,1)}, u32[]{:S(2)}) copy-start(bf16[1024,1536]{1,0:T(8,128)(2,1)} %get-tuple-element.118) | copy-start | bytes 9437188
  106.7 6.6 %copy-start.56 = (bf16[1024,2048]{1,0:T(8,128)(2,1)S(1)}, bf16[1024,2048]{1,0:T(8,128)(2,1)}, u32[]{:S(2)}) copy-start(bf16[1024,2048]{1,0:T(8,128)(2,1)} %get-tuple-element.163.hidden_ref) | copy-start | bytes 12582916
  123.6 37.8 %collective-permute-start = (bf16[2,2,2,96,1024]{4,3,2,1,0:T(8,128)(2,1)}, bf16[2,2,2,96,1024]{4,3,2,1,0:T(8,128)(2,1)S(1)}, u32[]{:S(2)}, u32[]{:S(2)}) collective-permute-start(bf16[2,2,2,96,1024]{4,3,2,1,0:T(8,128)(2,1)} %dynamic-slice_bitcast_fusion.5), channel_id=1, source_target_pairs={{0,2},{2,0},{4,6},{6,4},{8,10},{10,8},{12,14},{14,12},{16,18},{18,... | collective-permute-start | bytes 4718600 | tf_op jit(solution)/shard_map/ppermute | solution.py:68
  126.5 36.5 %collective-permute-start.1 = (bf16[2,2,2,96,1024]{4,3,2,1,0:T(8,128)(2,1)}, bf16[2,2,2,96,1024]{4,3,2,1,0:T(8,128)(2,1)}, u32[]{:S(2)}, u32[]{:S(2)}) collective-permute-start(bf16[2,2,2,96,1024]{4,3,2,1,0:T(8,128)(2,1)} %dynamic-slice_bitcast_fusion.4), channel_id=1, source_target_pairs={{0,4},{2,6},{4,0},{6,2},{8,12},{10,14},{12,8},{14,10},{16,20},{18,... | collective-permute-start | bytes 4718600 | tf_op jit(solution)/shard_map/ppermute | solution.py:68
  152.4 4.7 copy-start.14
  152.4 10.6 %copy-start.26 = (bf16[1536,1024]{1,0:T(8,128)(2,1)S(1)}, bf16[1536,1024]{1,0:T(8,128)(2,1)}, u32[]{:S(2)}) copy-start(bf16[1536,1024]{1,0:T(8,128)(2,1)} %convolution_convert_fusion.2) | copy-start | bytes 9437188
  152.4 10.6 %copy-start.27 = (bf16[1536,1024]{1,0:T(8,128)(2,1)S(1)}, bf16[1536,1024]{1,0:T(8,128)(2,1)}, u32[]{:S(2)}) copy-start(bf16[1536,1024]{1,0:T(8,128)(2,1)} %convolution_convert_fusion.3) | copy-start | bytes 9437188
  168.8 34.1 %collective-permute-start.2 = (bf16[2,2,96,1024]{3,2,1,0:T(8,128)(2,1)}, bf16[2,2,96,1024]{3,2,1,0:T(8,128)(2,1)S(1)}, u32[]{:S(2)}, u32[]{:S(2)}) collective-permute-start(bf16[2,2,96,1024]{3,2,1,0:T(8,128)(2,1)} %dynamic-slice_bitcast_fusion.16), channel_id=1, source_target_pairs={{0,4},{2,6},{4,0},{6,2},{8,12},{10,14},{12,8},{14,10},{16,20},{18,... | collective-permute-start | bytes 2359304 | tf_op jit(solution)/shard_map/ppermute | solution.py:68
  170.3 32.6 %collective-permute-start.3 = (bf16[2,2,96,1024]{3,2,1,0:T(8,128)(2,1)}, bf16[2,2,96,1024]{3,2,1,0:T(8,128)(2,1)}, u32[]{:S(2)}, u32[]{:S(2)}) collective-permute-start(bf16[2,2,96,1024]{3,2,1,0:T(8,128)(2,1)} %dynamic-slice_bitcast_fusion.15), channel_id=1, source_target_pairs={{0,2},{2,0},{4,6},{6,4},{8,10},{10,8},{12,14},{14,12},{16,18},{18,... | collective-permute-start | bytes 2359304 | tf_op jit(solution)/shard_map/ppermute | solution.py:68
  171.6 90.7 %collective-permute-start.5 = (bf16[2,2,2,96,2048]{4,3,2,1,0:T(8,128)(2,1)}, bf16[2,2,2,96,2048]{4,3,2,1,0:T(8,128)(2,1)}, u32[]{:S(2)}, u32[]{:S(2)}) collective-permute-start(bf16[2,2,2,96,2048]{4,3,2,1,0:T(8,128)(2,1)} %dynamic-slice_bitcast_fusion.1), channel_id=1, source_target_pairs={{0,2},{2,0},{4,6},{6,4},{8,10},{10,8},{12,14},{14,12},{16,18},{18,... | collective-permute-start | bytes 9437192 | tf_op jit(solution)/shard_map/ppermute | solution.py:68
  172.3 90.0 %collective-permute-start.6 = (bf16[2,2,2,96,2048]{4,3,2,1,0:T(8,128)(2,1)}, bf16[2,2,2,96,2048]{4,3,2,1,0:T(8,128)(2,1)}, u32[]{:S(2)}, u32[]{:S(2)}) collective-permute-start(bf16[2,2,2,96,2048]{4,3,2,1,0:T(8,128)(2,1)} %dynamic-slice_bitcast_fusion), channel_id=1, source_target_pairs={{0,4},{2,6},{4,0},{6,2},{8,12},{10,14},{12,8},{14,10},{16,20},{18,... | collective-permute-start | bytes 9437192 | tf_op jit(solution)/shard_map/ppermute | solution.py:68
  202.9 5.1 copy-start.54
  204.5 3.5 copy-start.53
  208.1 6.0 %copy-start.3 = (bf16[1024,768]{1,0:T(8,128)(2,1)S(1)}, bf16[1024,768]{1,0:T(8,128)(2,1)}, u32[]{:S(2)}) copy-start(bf16[1024,768]{1,0:T(8,128)(2,1)} %copy-done.2) | copy-start | bytes 4718596
  208.1 6.0 %copy-start.55 = (bf16[1024,1536]{1,0:T(8,128)(2,1)S(1)}, bf16[1024,1536]{1,0:T(8,128)(2,1)}, u32[]{:S(2)}) copy-start(bf16[1024,1536]{1,0:T(8,128)(2,1)} %get-tuple-element.140) | copy-start | bytes 9437188
  214.1 3.3 copy-start.57
  223.8 38.6 %collective-permute-start.4 = (bf16[2,96,2048]{2,1,0:T(8,128)(2,1)}, bf16[2,96,2048]{2,1,0:T(8,128)(2,1)S(1)}, u32[]{:S(2)}, u32[]{:S(2)}) collective-permute-start(bf16[2,96,2048]{2,1,0:T(8,128)(2,1)} %pad_maximum_fusion.3), channel_id=1, source_target_pairs={{0,8},{2,10},{4,12},{6,14},{8,0},{10,2},{12,4},{14,6},{16,24},{18,... | collective-permute-start | bytes 2359304 | tf_op jit(solution)/shard_map/ppermute | solution.py:68
  225.3 88.0 %collective-permute-start.9 = (bf16[2,2,2,96,1536]{4,3,0,2,1:T(8,128)(2,1)}, bf16[2,2,2,96,1536]{4,3,0,2,1:T(8,128)(2,1)S(1)}, u32[]{:S(2)}, u32[]{:S(2)}) collective-permute-start(bf16[2,2,2,96,1536]{4,3,0,2,1:T(8,128)(2,1)} %pad_maximum_fusion), channel_id=1, source_target_pairs={{0,8},{2,10},{4,12},{6,14},{8,0},{10,2},{12,4},{14,6},{16,24},{18,... | collective-permute-start | bytes 7077896 | tf_op jit(solution)/shard_map/ppermute | solution.py:68
  260.0 19.2 %copy-start.5 = (bf16[1024,768]{1,0:T(8,128)(2,1)}, bf16[1024,768]{1,0:T(8,128)(2,1)S(1)}, u32[]{:S(2)}) copy-start(bf16[1024,768]{1,0:T(8,128)(2,1)S(1)} %get-tuple-element.161.key_ref) | copy-start | bytes 4718596
  260.1 29.6 %copy-start.4 = (bf16[1024,768]{1,0:T(8,128)(2,1)}, bf16[1024,768]{1,0:T(8,128)(2,1)S(1)}, u32[]{:S(2)}) copy-start(bf16[1024,768]{1,0:T(8,128)(2,1)S(1)} %get-tuple-element.173.query_ref) | copy-start | bytes 4718596
  260.1 75.3 %copy-start = (bf16[16,1024]{1,0:T(8,128)(2,1)}, bf16[16,1024]{1,0:T(8,128)(2,1)S(1)}, u32[]{:S(2)}) copy-start(bf16[16,1024]{1,0:T(8,128)(2,1)S(1)} %get-tuple-element.160.forget_ref) | copy-start | bytes 98308
  261.3 7.8 %slice-start = ((s8[6291456]{0:T(1024)(128)(4,1)}), s8[4194304]{0:T(1024)(128)(4,1)S(1)}, s32[]{:S(2)}) async-start(s8[6291456]{0:T(1024)(128)(4,1)} %bitcast.222), calls=%async_computation | async-start | bytes 8388608
  262.3 5.3 %copy-start.37 = (bf16[2,96,2048]{2,1,0:T(8,128)(2,1)}, bf16[2,96,2048]{2,1,0:T(8,128)(2,1)S(1)}, u32[]{:S(2)}) copy-start(bf16[2,96,2048]{2,1,0:T(8,128)(2,1)S(1)} %collective-permute-done.4) | copy-start | bytes 2359300
  262.4 6.7 %slice-start.1 = ((s8[6291456]{0:T(1024)(128)(4,1)}), s8[2097152]{0:T(1024)(128)(4,1)S(1)}, s32[]{:S(2)}) async-start(s8[6291456]{0:T(1024)(128)(4,1)} %bitcast.222), calls=%async_computation.1 | async-start | bytes 4194304
  267.6 4.8 copy-start.9
  274.9 4.3 copy-start.30
  282.2 5.2 %copy-start.33 = (bf16[1536,768]{1,0:T(8,128)(2,1)}, bf16[1536,768]{1,0:T(8,128)(2,1)S(1)}, u32[]{:S(2)}) copy-start(bf16[1536,768]{1,0:T(8,128)(2,1)S(1)} %convolution_convert_fusion.5) | copy-start | bytes 7077892
  282.2 36.3 %collective-permute-start.7 = (bf16[2,2,96,2048]{3,2,1,0:T(8,128)(2,1)}, bf16[2,2,96,2048]{3,2,1,0:T(8,128)(2,1)}, u32[]{:S(2)}, u32[]{:S(2)}) collective-permute-start(bf16[2,2,96,2048]{3,2,1,0:T(8,128)(2,1)} %dynamic-slice_bitcast_fusion.3), channel_id=1, source_target_pairs={{0,4},{2,6},{4,0},{6,2},{8,12},{10,14},{12,8},{14,10},{16,20},{18,... | collective-permute-start | bytes 4718600 | tf_op jit(solution)/shard_map/ppermute | solution.py:68
  283.8 35.9 %collective-permute-start.8 = (bf16[2,2,96,2048]{3,2,1,0:T(8,128)(2,1)}, bf16[2,2,96,2048]{3,2,1,0:T(8,128)(2,1)}, u32[]{:S(2)}, u32[]{:S(2)}) collective-permute-start(bf16[2,2,96,2048]{3,2,1,0:T(8,128)(2,1)} %dynamic-slice_bitcast_fusion.2), channel_id=1, source_target_pairs={{0,2},{2,0},{4,6},{6,4},{8,10},{10,8},{12,14},{14,12},{16,18},{18,... | collective-permute-start | bytes 4718600 | tf_op jit(solution)/shard_map/ppermute | solution.py:68
  295.0 41.6 %collective-permute-start.10 = (bf16[96,2048]{1,0:T(8,128)(2,1)S(1)}, bf16[96,2048]{1,0:T(8,128)(2,1)S(1)}, u32[]{:S(2)}, u32[]{:S(2)}) collective-permute-start(bf16[96,2048]{1,0:T(8,128)(2,1)S(1)} %dynamic-slice_bitcast_fusion.21), channel_id=1, source_target_pairs={{0,16},{2,18},{4,20},{6,22},{8,24},{10,26},{12,28},{14,30},{16,0},... | collective-permute-start | bytes 1179656 | tf_op jit(solution)/shard_map/ppermute | solution.py:68
  313.3 8.8 %copy-start.31 = (bf16[2,2,2,96,1536]{4,3,0,2,1:T(8,128)(2,1)}, bf16[2,2,2,96,1536]{4,3,0,2,1:T(8,128)(2,1)S(1)}, u32[]{:S(2)}) copy-start(bf16[2,2,2,96,1536]{4,3,0,2,1:T(8,128)(2,1)S(1)} %collective-permute-done.9) | copy-start | bytes 7077892
  330.4 2.8 copy-start.41
  330.5 3.5 copy-start.43
  331.6 60.4 %collective-permute-start.11 = (bf16[2,96,4096]{2,1,0:T(8,128)(2,1)}, bf16[2,96,4096]{2,1,0:T(8,128)(2,1)}, u32[]{:S(2)}, u32[]{:S(2)}) collective-permute-start(bf16[2,96,4096]{2,1,0:T(8,128)(2,1)} %pad_maximum_fusion.1), channel_id=1, source_target_pairs={{0,8},{2,10},{4,12},{6,14},{8,0},{10,2},{12,4},{14,6},{16,24},{18,... | collective-permute-start | bytes 4718600 | tf_op jit(solution)/shard_map/ppermute | solution.py:68
  333.9 58.0 %collective-permute-start.13 = (bf16[2,2,2,96,896]{4,3,2,1,0:T(8,128)(2,1)}, bf16[2,2,2,96,896]{4,3,2,1,0:T(8,128)(2,1)}, u32[]{:S(2)}, u32[]{:S(2)}) collective-permute-start(bf16[2,2,2,96,896]{4,3,2,1,0:T(8,128)(2,1)} %pad_maximum_fusion.2), channel_id=1, source_target_pairs={{0,2},{2,0},{4,6},{6,4},{8,10},{10,8},{12,14},{14,12},{16,18},{18,... | collective-permute-start | bytes 4128776 | tf_op jit(solution)/shard_map/ppermute | solution.py:68
  335.5 29.2 %collective-permute-start.14 = (bf16[2,2,2,96,768]{4,3,2,1,0:T(8,128)(2,1)}, bf16[2,2,2,96,768]{4,3,2,1,0:T(8,128)(2,1)}, u32[]{:S(2)}, u32[]{:S(2)}) collective-permute-start(bf16[2,2,2,96,768]{4,3,2,1,0:T(8,128)(2,1)} %dynamic-slice_bitcast_fusion.8), channel_id=1, source_target_pairs={{0,4},{2,6},{4,0},{6,2},{8,12},{10,14},{12,8},{14,10},{16,20},{18,... | collective-permute-start | bytes 3538952 | tf_op jit(solution)/shard_map/ppermute | solution.py:68
  336.0 55.9 %collective-permute-start.15 = (bf16[2,2,2,96,768]{4,3,0,2,1:T(8,128)(2,1)}, bf16[2,2,2,96,768]{4,3,0,2,1:T(8,128)(2,1)}, u32[]{:S(2)}, u32[]{:S(2)}) collective-permute-start(bf16[2,2,2,96,768]{4,3,0,2,1:T(8,128)(2,1)} %bitcast.239), channel_id=1, source_target_pairs={{0,8},{2,10},{4,12},{6,14},{8,0},{10,2},{12,4},{14,6},{16,24},{18,... | collective-permute-start | bytes 3538952 | tf_op jit(solution)/shard_map/ppermute | solution.py:68
  336.6 25.6 %copy-start.39 = (bf16[96,2048]{1,0:T(8,128)(2,1)}, bf16[96,2048]{1,0:T(8,128)(2,1)S(1)}, u32[]{:S(2)}) copy-start(bf16[96,2048]{1,0:T(8,128)(2,1)S(1)} %collective-permute-done.10) | copy-start | bytes 1179652
  336.6 55.3 %collective-permute-start.12 = (bf16[2,2,96,1536]{3,2,0,1:T(8,128)(2,1)}, bf16[2,2,96,1536]{3,2,0,1:T(8,128)(2,1)}, u32[]{:S(2)}, u32[]{:S(2)}) collective-permute-start(bf16[2,2,96,1536]{3,2,0,1:T(8,128)(2,1)} %dynamic-slice_bitcast_fusion.7), channel_id=1, source_target_pairs={{0,4},{2,6},{4,0},{6,2},{8,12},{10,14},{12,8},{14,10},{16,20},{18,... | collective-permute-start | bytes 3538952 | tf_op jit(solution)/shard_map/ppermute | solution.py:68
  392.0 3.0 copy-start.34
  395.0 2.9 copy-start.20
  400.6 2.7 copy-start.29
  406.2 36.5 %copy-start.16 = (bf16[2,2,2,96,896]{4,3,2,1,0:T(8,128)(2,1)S(1)}, bf16[2,2,2,96,896]{4,3,2,1,0:T(8,128)(2,1)}, u32[]{:S(2)}) copy-start(bf16[2,2,2,96,896]{4,3,2,1,0:T(8,128)(2,1)} %copy-done.15) | copy-start | bytes 4128772
  406.3 35.1 %collective-permute-start.16 = (bf16[96,4096]{1,0:T(8,128)(2,1)}, bf16[96,4096]{1,0:T(8,128)(2,1)}, u32[]{:S(2)}, u32[]{:S(2)}) collective-permute-start(bf16[96,4096]{1,0:T(8,128)(2,1)} %dynamic-slice_bitcast_fusion.10), channel_id=1, source_target_pairs={{0,16},{2,18},{4,20},{6,22},{8,24},{10,26},{12,28},{14,30},{16,0},... | collective-permute-start | bytes 2359304 | tf_op jit(solution)/shard_map/ppermute | solution.py:68
  408.8 27.6 %collective-permute-start.18 = (bf16[2,2,96,896]{3,2,1,0:T(8,128)(2,1)}, bf16[2,2,96,896]{3,2,1,0:T(8,128)(2,1)}, u32[]{:S(2)}, u32[]{:S(2)}) collective-permute-start(bf16[2,2,96,896]{3,2,1,0:T(8,128)(2,1)} %dynamic-slice_bitcast_fusion.17), channel_id=1, source_target_pairs={{0,4},{2,6},{4,0},{6,2},{8,12},{10,14},{12,8},{14,10},{16,20},{18,... | collective-permute-start | bytes 2064392 | tf_op jit(solution)/shard_map/ppermute | solution.py:68
  409.4 16.3 %collective-permute-start.17 = (bf16[2,96,1536]{2,1,0:T(8,128)(2,1)S(1)}, bf16[2,96,1536]{2,1,0:T(8,128)(2,1)}, u32[]{:S(2)}, u32[]{:S(2)}) collective-permute-start(bf16[2,96,1536]{2,1,0:T(8,128)(2,1)S(1)} %dynamic-slice_bitcast_fusion.20), channel_id=1, source_target_pairs={{0,2},{2,0},{4,6},{6,4},{8,10},{10,8},{12,14},{14,12},{16,18},{18,... | collective-permute-start | bytes 1769480 | tf_op jit(solution)/shard_map/ppermute | solution.py:68
  410.7 23.7 %collective-permute-start.19 = (bf16[2,2,96,768]{3,2,1,0:T(8,128)(2,1)}, bf16[2,2,96,768]{3,2,1,0:T(8,128)(2,1)}, u32[]{:S(2)}, u32[]{:S(2)}) collective-permute-start(bf16[2,2,96,768]{3,2,1,0:T(8,128)(2,1)} %dynamic-slice_bitcast_fusion.19), channel_id=1, source_target_pairs={{0,2},{2,0},{4,6},{6,4},{8,10},{10,8},{12,14},{14,12},{16,18},{18,... | collective-permute-start | bytes 1769480 | tf_op jit(solution)/shard_map/ppermute | solution.py:68
  411.4 25.0 %collective-permute-start.20 = (bf16[2,2,96,768]{3,2,0,1:T(8,128)(2,1)}, bf16[2,2,96,768]{3,2,0,1:T(8,128)(2,1)}, u32[]{:S(2)}, u32[]{:S(2)}) collective-permute-start(bf16[2,2,96,768]{3,2,0,1:T(8,128)(2,1)} %dynamic-slice_bitcast_fusion.18), channel_id=1, source_target_pairs={{0,4},{2,6},{4,0},{6,2},{8,12},{10,14},{12,8},{14,10},{16,20},{18,... | collective-permute-start | bytes 1769480 | tf_op jit(solution)/shard_map/ppermute | solution.py:68
  446.9 21.7 %collective-permute-start.22 = (bf16[2,96,1664]{2,1,0:T(8,128)(2,1)S(1)}, bf16[2,96,1664]{2,1,0:T(8,128)(2,1)S(1)}, u32[]{:S(2)}, u32[]{:S(2)}) collective-permute-start(bf16[2,96,1664]{2,1,0:T(8,128)(2,1)S(1)} %pad_maximum_fusion.4), channel_id=1, source_target_pairs={{0,8},{2,10},{4,12},{6,14},{8,0},{10,2},{12,4},{14,6},{16,24},{18,... | collective-permute-start | bytes 1916936 | tf_op jit(solution)/shard_map/ppermute | solution.py:68
  449.0 18.8 %collective-permute-start.21 = (bf16[96,1536]{1,0:T(8,128)(2,1)S(1)}, bf16[96,1536]{1,0:T(8,128)(2,1)S(1)}, u32[]{:S(2)}, u32[]{:S(2)}) collective-permute-start(bf16[96,1536]{1,0:T(8,128)(2,1)S(1)} %dynamic-slice_bitcast_fusion.32), channel_id=1, source_target_pairs={{0,16},{2,18},{4,20},{6,22},{8,24},{10,26},{12,28},{14,30},{16,0},... | collective-permute-start | bytes 884744 | tf_op jit(solution)/shard_map/ppermute | solution.py:68
  452.4 15.4 %collective-permute-start.23 = (bf16[2,96,768]{2,1,0:T(8,128)(2,1)S(1)}, bf16[2,96,768]{2,1,0:T(8,128)(2,1)S(1)}, u32[]{:S(2)}, u32[]{:S(2)}) collective-permute-start(bf16[2,96,768]{2,1,0:T(8,128)(2,1)S(1)} %dynamic-slice_bitcast_fusion.30), channel_id=1, source_target_pairs={{0,2},{2,0},{4,6},{6,4},{8,10},{10,8},{12,14},{14,12},{16,18},{18,... | collective-permute-start | bytes 884744 | tf_op jit(solution)/shard_map/ppermute | solution.py:68
  468.9 30.1 %collective-permute-start.24 = (bf16[96,1664]{1,0:T(8,128)(2,1)S(1)}, bf16[96,1664]{1,0:T(8,128)(2,1)S(1)}, u32[]{:S(2)}, u32[]{:S(2)}) collective-permute-start(bf16[96,1664]{1,0:T(8,128)(2,1)S(1)} %dynamic-slice_bitcast_fusion.28), channel_id=1, source_target_pairs={{0,16},{2,18},{4,20},{6,22},{8,24},{10,26},{12,28},{14,30},{16,0},... | collective-permute-start | bytes 958472 | tf_op jit(solution)/shard_map/ppermute | solution.py:68
  471.6 27.4 %collective-permute-start.25 = (bf16[96,768]{1,0:T(8,128)(2,1)S(1)}, bf16[96,768]{1,0:T(8,128)(2,1)S(1)}, u32[]{:S(2)}, u32[]{:S(2)}) collective-permute-start(bf16[96,768]{1,0:T(8,128)(2,1)S(1)} %dynamic-slice_bitcast_fusion.35), channel_id=1, source_target_pairs={{0,16},{2,18},{4,20},{6,22},{8,24},{10,26},{12,28},{14,30},{16,0},... | collective-permute-start | bytes 442376 | tf_op jit(solution)/shard_map/ppermute | solution.py:68
  499.7 8.8 %copy-start.25 = (f32[512,1536]{1,0:T(8,128)S(1)}, f32[512,1536]{1,0:T(8,128)}, u32[]{:S(2)}) copy-start(f32[512,1536]{1,0:T(8,128)} %get-tuple-element.312) | copy-start | bytes 9437188
  (23 other events, 44.0 us)

commit v5 on v4

--- a/solution.py
+++ b/solution.py
@@ -849,13 +849,12 @@
         ]
     )
     live = down + gated + [shared] + inward
+    shares = all_sum(shares)
     tokens_grad, shares = tie((tokens_grad, shares), end=live)
     while True:
         flying = [flow for flow in live if not flow.done()]
         last = all(flow.stage == flow.bits - 1 for flow in flying)
         shares = tie(shares, start=flying)
-        if last:
-            shares = all_sum(shares)
         shares = tie(shares, end=flying)
         if inward[0].stage == 2:
             inward[:2] = [merged(inward[:2])]

time: 519 us -> 515 us (level)
  Pallas kernels: 172 us -> 180 us
  waiting for transfers between devices: 79.3 us -> 71.9 us
    pallas_call x1, Pallas kernels: 26.1 us -> 34.5 us  [all_sum(): pl.pallas_call(partial(all_sum_body, bits), out_shape=jax.ShapeDtypeStruc...]
    ppermute x26, waiting for transfers between devices: 79.3 us -> 71.9 us  [fly(): self.got = lax.ppermute(self.sent, 'dp', pairs)]
    unnamed x125 -> x123, local copies, waits for them, and re-layouts: 21.2 us -> 20.6 us
  transfers between devices with their start and end apart: 26 -> 26, of which waited for: 12 -> 11; matrix products, arithmetic and copies ran while one was open for 18% -> 18% of each run, Pallas kernels for 25% -> 27%
where the time goes in v5:
time: 515 us; the launch traced here: 506 us
  Pallas kernels  180 us (35%)
  matrix products  113 us (22%)
  waiting for transfers between devices  71.9 us (14%)
  local copies, waits for them, and re-layouts  59.4 us (12%)
  other arithmetic  46.2 us (9%)
  starting transfers between devices  32.7 us (6%)
    ppermute x26, waiting for transfers between devices, fly(): self.got = lax.ppermute(self.sent, 'dp', pairs)  71.9 us
    dot_general x9, matrix products, inner_rows(): lax.dot_general(former, latter, (((0,), (0,)), ((), ())), preferred_eleme...  45.9 us
    dot_general x6, matrix products, matmul(): return jnp.dot(former, latter, preferred_element_type=jnp.float32)  40.1 us
    convert_element_type x20, other arithmetic, land(): self.wholes = [total.astype(jnp.bfloat16)]  35.3 us
    pallas_call x1, Pallas kernels, all_sum(): pl.pallas_call(partial(all_sum_body, bits), out_shape=jax.ShapeDtypeStruc...  34.5 us
    pallas_call x1, Pallas kernels, attend_backward(): pl.pallas_call(partial(backward_body, head_dim=head_dim, spans=spans, hea...  34.3 us
    ppermute x26, starting transfers between devices, fly(): self.got = lax.ppermute(self.sent, 'dp', pairs)  32.7 us
    pallas_call x1, Pallas kernels, middle_back(): pl.pallas_call(back_body, out_shape=[jax.ShapeDtypeStruct((half, width),...  30.1 us
  transfers between devices with their start and end apart: 26, of which 11 were waited for; matrix products, arithmetic and copies ran while one was open for 18% of the time, Pallas kernels for 27%

profile of v5, /device:TPU:0, one launch (start us, length us, event | category | flops | bytes accessed | tf_op | source)
XLA Modules:
  0.0 506.2 jit_solution(17073823966568280749)
XLA Ops:
  1.9 5.6 %norm_gather.1 = bf16[1024,1536]{1,0:T(8,128)(2,1)} custom-call(bf16[512,1536]{1,0:T(8,128)(2,1)} %token_ref.5, f32[1,1536]{1,0:T(1,128)} %reshape.109.gain_ref), custom_call_target="tpu_custom_call" | custom-call | flops 6291456 | bytes 9437184 | tf_op jit(solution)/shard_map/norm_gather/pallas_call | solution.py:584
  7.6 6.6 %add_divide_fusion.1.gate_ref = f32[1024,768]{1,0:T(8,128)} fusion(bf16[1024,1536]{1,0:T(8,128)(2,1)} %norm_gather.1, bf16[1536,768]{1,0:T(8,128)(2,1)S(1)} %copy-done.49), kind=kOutput, calls=%fused_computation.32 | convolution fusion | flops 2418278400 | bytes 8650752 | tf_op jit(solution)/shard_map/dot_general | solution.py:15
  14.2 3.7 convolution_convert_fusion.10.v_ref
  17.8 3.7 convolution_convert_fusion.11.k_ref
  21.5 2.6 convolution_convert_fusion.12.q_ref
  25.2 2.8 fusion.18
  28.1 20.7 %attend_forward.1 = (f32[1024,768]{1,0:T(8,128)}, bf16[1024,768]{1,0:T(8,128)(2,1)S(1)}, f32[1024,768]{1,0:T(8,128)}) custom-call(bf16[1024,768]{1,0:T(8,128)(2,1)S(1)} %convolution_convert_fusion.12.q_ref, bf16[1024,768]{1,0:T(8,128)(2,1)} %convolution_convert_fusion.11.k_ref, bf16[1024,768]{1,0:T(8,128)(2,1)} %convolution_convert_fusion.10.v_ref, ...), custom_call_target="tpu_custom_call" | custom-call | flops 7247757312 | bytes 15728640 | tf_op jit(solution)/shard_map/attend_forward/pallas_call | solution.py:210
  49.9 15.7 %project.1 = (f32[512,1536]{1,0:T(8,128)}, bf16[1024,1536]{1,0:T(8,128)(2,1)}, bf16[1024,1536]{1,0:T(8,128)(2,1)}) custom-call(bf16[1024,768]{1,0:T(8,128)(2,1)} %copy-done.2, bf16[768,1536]{1,0:T(8,128)(2,1)} %weight_ref.2, bf16[512,1536]{1,0:T(8,128)(2,1)} %token_ref.5, bf16[512,1536]{1,0:T(8,128)(2,1)} %cot_ref.3, f32[1,1536]{1,0:T(1,128)} %reshape.110.gain_ref), custom_call_target="tpu_custom_call" | custom-call | flops 2415919104 | bytes 18874368 | tf_op jit(solution)/shard_map/project/pallas_call | solution.py:605
  65.6 12.6 %fusion.25 = f32[1024,2048]{1,0:T(8,128)} fusion(bf16[1024,1536]{1,0:T(8,128)(2,1)} %get-tuple-element.117, bf16[1536,2048]{1,0:T(8,128)(2,1)} %gate_weight_ref.1), kind=kOutput, calls=%fused_computation.131 | convolution fusion | flops 6442450944 | bytes 17825792 | tf_op jit(solution)/shard_map/dot_general | solution.py:15
  78.2 11.0 %fusion.26 = f32[1024,2048]{1,0:T(8,128)} fusion(bf16[1024,1536]{1,0:T(8,128)(2,1)S(1)} %copy-done.50, bf16[1536,2048]{1,0:T(8,128)(2,1)} %up_weight_ref.1), kind=kOutput, calls=%fused_computation.132 | convolution fusion | flops 6442450944 | bytes 17825792 | tf_op jit(solution)/shard_map/dot_general | solution.py:15
  89.2 17.4 %multiply_convert_fusion = (bf16[1024,2048]{1,0:T(8,128)(2,1)}, bf16[1024,2048]{1,0:T(8,128)(2,1)}, bf16[1024,2048]{1,0:T(8,128)(2,1)}) fusion(f32[1024,2048]{1,0:T(8,128)} %fusion.25, f32[1024,2048]{1,0:T(8,128)} %fusion.26, bf16[1024,1536]{1,0:T(8,128)(2,1)S(1)} %copy-done.51, bf16[2048,1536]{1,0:T(8,128)(2,1)} %weight_ref.3), kind=kOutput, calls=%fused_computation | convolution fusion | flops 6473908224 | bytes 38797312 | tf_op jit(solution)/shard_map/dot_general | solution.py:25
  106.6 6.6 %convolution_convert_fusion.2 = bf16[1536,1024]{1,0:T(8,128)(2,1)} fusion(bf16[1024,1536]{1,0:T(8,128)(2,1)S(1)} %copy-done.51, bf16[1024,2048]{1,0:T(8,128)(2,1)} %get-tuple-element.163.hidden_ref), kind=kOutput, calls=%fused_computation.12 | convolution fusion | flops 3222798336 | bytes 8388608 | tf_op jit(solution)/shard_map/dot_general | solution.py:19
  113.3 4.9 convolution_convert_fusion.3
  118.2 2.7 dynamic-slice_bitcast_fusion.4
  120.8 2.7 dynamic-slice_bitcast_fusion.5
  123.5 2.8 collective-permute-start
  127.9 10.0 %convolution_convert_fusion = bf16[1536,2048]{1,0:T(8,128)(2,1)S(1)} fusion(bf16[1024,1536]{1,0:T(8,128)(2,1)} %get-tuple-element.117, bf16[1024,2048]{1,0:T(8,128)(2,1)} %get-tuple-element.131.up_ref), kind=kOutput, calls=%fused_computation.5 | convolution fusion | flops 6445596672 | bytes 13631488 | tf_op jit(solution)/shard_map/dot_general | solution.py:19
  137.9 2.7 copy-done.13
  140.6 2.0 dynamic-slice_bitcast_fusion
  142.6 9.6 %convolution_convert_fusion.1 = bf16[1536,2048]{1,0:T(8,128)(2,1)S(1)} fusion(bf16[1024,1536]{1,0:T(8,128)(2,1)} %get-tuple-element.117, bf16[1024,2048]{1,0:T(8,128)(2,1)} %get-tuple-element.130.gate_ref), kind=kOutput, calls=%fused_computation.6 | convolution fusion | flops 6445596672 | bytes 13631488 | tf_op jit(solution)/shard_map/dot_general | solution.py:19
  152.3 2.1 dynamic-slice_bitcast_fusion.1
  154.3 2.6 copy-done.14
  156.9 4.3 collective-permute-done
  162.8 3.5 fusion.5
  172.7 30.1 %middle_back.1 = (f32[512,1536]{1,0:T(8,128)}, bf16[1024,1536]{1,0:T(8,128)(2,1)}, f32[8,1536]{1,0:T(8,128)}) custom-call(bf16[1024,2048]{1,0:T(8,128)(2,1)} %get-tuple-element.130.gate_ref, bf16[1024,2048]{1,0:T(8,128)(2,1)} %get-tuple-element.131.up_ref, bf16[1536,2048]{1,0:T(8,128)(2,1)} %gate_weight_ref.1, bf16[1536,2048]{1,0:T(8,128)(2,1)} %up_weight_ref.1, ...), custom_call_target="tpu_custom_call" | custom-call | flops 12884901888 | bytes 39321600 | tf_op jit(solution)/shard_map/middle_back/pallas_call | solution.py:640
  202.8 1.6 fusion.13
  204.4 1.6 fusion.12
  208.0 6.0 %multiply_convert_fusion.3 = (bf16[1024,768]{1,0:T(8,128)(2,1)S(1)}, bf16[1024,768]{1,0:T(8,128)(2,1)}) fusion(f32[1024,768]{1,0:T(8,128)S(1)} %copy-done.52, f32[1024,768]{1,0:T(8,128)S(1)} %copy-done.53, bf16[1024,1536]{1,0:T(8,128)(2,1)} %get-tuple-element.140, bf16[768,1536]{1,0:T(8,128)(2,1)S(1)} %copy-done.45), kind=kOutput, calls=%fused_computation.28 | convolution fusion | flops 2421424128 | bytes 14942208 | tf_op jit(solution)/shard_map/dot_general | solution.py:25
  214.0 3.0 convolution_convert_fusion.8
  217.3 1.6 copy-done.8
  218.9 2.9 convolution_convert_fusion.7
  225.7 34.3 %attend_backward.1 = (bf16[1024,768]{1,0:T(8,128)(2,1)S(1)}, bf16[1024,768]{1,0:T(8,128)(2,1)S(1)}, bf16[1024,768]{1,0:T(8,128)(2,1)}, bf16[16,1024]{1,0:T(8,128)(2,1)S(1)}) custom-call(bf16[1024,768]{1,0:T(8,128)(2,1)} %copy-done.6, bf16[1024,768]{1,0:T(8,128)(2,1)} %convolution_convert_fusion.11.k_ref, bf16[1024,768]{1,0:T(8,128)(2,1)} %convolution_convert_fusion.10.v_ref, ...), custom_call_target="tpu_custom_call" | custom-call | flops 18119393280 | bytes 15728640 | tf_op jit(solution)/shard_map/attend_backward/pallas_call | solution.py:313
  262.3 5.3 %fusion.1 = bf16[2,2,2,96,2048]{4,3,2,1,0:T(8,128)(2,1)S(1)} fusion(bf16[2,2,2,96,2048]{4,3,2,1,0:T(8,128)(2,1)} %collective-permute-done.6, bf16[2,2,2,2,96,2048]{5,4,3,2,1,0:T(8,128)(2,1)} %bitcast.220, s32[]{:T(128)S(6)} %select_n.108), kind=kLoop, calls=%fused_computation.8 | loop fusion | flops 6291456 | bytes 9437188 | tf_op jit(solution)/shard_map/convert_element_type | solution.py:76
  269.0 3.4 fusion.2
  276.2 2.9 convolution_convert_fusion.4
  279.2 2.9 convolution_convert_fusion.5
  282.1 1.6 collective-permute-start.7
  289.6 2.9 convolution_convert_fusion.6
  295.0 2.6 collective-permute-start.10
  297.6 15.7 %result_rows.1 = bf16[512,1536]{1,0:T(8,128)(2,1)} custom-call(bf16[1024,2048]{1,0:T(8,128)(2,1)} %get-tuple-element.163.hidden_ref, bf16[2048,1536]{1,0:T(8,128)(2,1)} %weight_ref.3, f32[512,1536]{1,0:T(8,128)} %get-tuple-element.132.middle_ref), custom_call_target="tpu_custom_call" | custom-call | flops 6442450944 | bytes 23592960 | tf_op jit(solution)/shard_map/result_rows/pallas_call | solution.py:624
  313.3 5.1 collective-permute-done.7
  319.6 2.5 fusion.4
  324.3 2.0 fusion.3
  336.6 1.6 collective-permute-start.12
  338.1 24.0 %first_back.1 = (f32[512,1536]{1,0:T(8,128)}, f32[8,1536]{1,0:T(8,128)}) custom-call(bf16[1024,768]{1,0:T(8,128)(2,1)} %copy-done.4, bf16[1024,768]{1,0:T(8,128)(2,1)} %copy-done.5, bf16[1024,768]{1,0:T(8,128)(2,1)} %get-tuple-element.162.value_ref, bf16[1024,768]{1,0:T(8,128)(2,1)} %copy-done.56, bf16[16,1024]{1,0:T(8,128)(2,1)} %copy-done, ...), custom_call_target="tpu_custom_call" | custom-call | flops 9663676416 | bytes 31457280 | tf_op jit(solution)/shard_map/first_back/pallas_call | solution.py:662
  363.7 34.5 %all_sum.1 = f32[8,1536]{1,0:T(8,128)} custom-call(f32[8,1536]{1,0:T(8,128)} %maximum_maximum_fusion.part_ref), custom_call_target="tpu_custom_call" | custom-call | tf_op jit(solution)/shard_map/all_sum/pallas_call | solution.py:680
  398.3 2.1 fusion.7
  401.3 1.7 fusion.8
  404.2 1.7 add_convert_fusion.2
  406.9 1.7 fusion.9
  409.6 1.9 add_convert_fusion.1
  416.9 2.1 fusion.19
  419.0 10.7 %collective-permute-done.17 = bf16[2,96,1536]{2,1,0:T(8,128)(2,1)} collective-permute-done((bf16[2,96,1536]{2,1,0:T(8,128)(2,1)S(1)}, bf16[2,96,1536]{2,1,0:T(8,128)(2,1)}, u32[]{:S(2)}, u32[]{:S(2)}) %collective-permute-start.17) | collective-permute-done | bytes 589856 | tf_op jit(solution)/shard_map/ppermute | solution.py:68
  429.7 8.5 %collective-permute-done.19 = bf16[2,2,96,768]{3,2,1,0:T(8,128)(2,1)} collective-permute-done((bf16[2,2,96,768]{3,2,1,0:T(8,128)(2,1)}, bf16[2,2,96,768]{3,2,1,0:T(8,128)(2,1)}, u32[]{:S(2)}, u32[]{:S(2)}) %collective-permute-start.19) | collective-permute-done | bytes 589856 | tf_op jit(solution)/shard_map/ppermute | solution.py:68
  438.2 2.0 collective-permute-done.20
  440.2 6.6 %collective-permute-done.16 = bf16[96,4096]{1,0:T(8,128)(2,1)} collective-permute-done((bf16[96,4096]{1,0:T(8,128)(2,1)}, bf16[96,4096]{1,0:T(8,128)(2,1)}, u32[]{:S(2)}, u32[]{:S(2)}) %collective-permute-start.16) | collective-permute-done | bytes 786464 | tf_op jit(solution)/shard_map/ppermute | solution.py:68
  453.8 2.4 collective-permute-start.21
  458.8 13.1 %collective-permute-done.21 = bf16[96,1536]{1,0:T(8,128)(2,1)S(1)} collective-permute-done((bf16[96,1536]{1,0:T(8,128)(2,1)S(1)}, bf16[96,1536]{1,0:T(8,128)(2,1)S(1)}, u32[]{:S(2)}, u32[]{:S(2)}) %collective-permute-start.21) | collective-permute-done | bytes 294944 | tf_op jit(solution)/shard_map/ppermute | solution.py:68
  471.9 2.2 collective-permute-done.22
  475.7 1.8 collective-permute-start.25
  478.4 17.7 %collective-permute-done.25 = bf16[96,768]{1,0:T(8,128)(2,1)S(1)} collective-permute-done((bf16[96,768]{1,0:T(8,128)(2,1)S(1)}, bf16[96,768]{1,0:T(8,128)(2,1)S(1)}, u32[]{:S(2)}, u32[]{:S(2)}) %collective-permute-start.25) | collective-permute-done | bytes 147488 | tf_op jit(solution)/shard_map/ppermute | solution.py:68
  497.1 1.7 slice_reduce_fusion
  501.4 2.7 copy.89
  504.1 1.7 copy.90
  (226 shorter events, 75.0 us)
Async XLA Ops:
  1.9 5.6 %copy-start.49 = (bf16[1536,768]{1,0:T(8,128)(2,1)S(1)}, bf16[1536,768]{1,0:T(8,128)(2,1)}, u32[]{:S(2)}) copy-start(bf16[1536,768]{1,0:T(8,128)(2,1)} %wg_ref.1) | copy-start | bytes 7077892
  7.5 6.6 %copy-start.7 = (bf16[1024,1536]{1,0:T(8,128)(2,1)S(1)}, bf16[1024,1536]{1,0:T(8,128)(2,1)}, u32[]{:S(2)}) copy-start(bf16[1024,1536]{1,0:T(8,128)(2,1)} %norm_gather.1) | copy-start | bytes 9437188
  7.6 6.6 %copy-start.48 = (bf16[1536,768]{1,0:T(8,128)(2,1)S(1)}, bf16[1536,768]{1,0:T(8,128)(2,1)}, u32[]{:S(2)}) copy-start(bf16[1536,768]{1,0:T(8,128)(2,1)} %wv_ref.1) | copy-start | bytes 7077892
  14.1 3.7 copy-start.47
  17.8 3.7 copy-start.46
  21.5 2.9 copy-start.43
  21.5 3.7 copy-start.40
  21.5 3.7 copy-start.44
  24.1 3.9 copy-start.6
  65.6 12.7 %copy-start.50 = (bf16[1024,1536]{1,0:T(8,128)(2,1)S(1)}, bf16[1024,1536]{1,0:T(8,128)(2,1)}, u32[]{:S(2)}) copy-start(bf16[1024,1536]{1,0:T(8,128)(2,1)} %get-tuple-element.117) | copy-start | bytes 9437188
  78.2 11.0 %copy-start.51 = (bf16[1024,1536]{1,0:T(8,128)(2,1)S(1)}, bf16[1024,1536]{1,0:T(8,128)(2,1)}, u32[]{:S(2)}) copy-start(bf16[1024,1536]{1,0:T(8,128)(2,1)} %get-tuple-element.118) | copy-start | bytes 9437188
  106.6 6.6 %copy-start.55 = (bf16[1024,2048]{1,0:T(8,128)(2,1)S(1)}, bf16[1024,2048]{1,0:T(8,128)(2,1)}, u32[]{:S(2)}) copy-start(bf16[1024,2048]{1,0:T(8,128)(2,1)} %get-tuple-element.163.hidden_ref) | copy-start | bytes 12582916
  123.5 37.7 %collective-permute-start = (bf16[2,2,2,96,1024]{4,3,2,1,0:T(8,128)(2,1)}, bf16[2,2,2,96,1024]{4,3,2,1,0:T(8,128)(2,1)S(1)}, u32[]{:S(2)}, u32[]{:S(2)}) collective-permute-start(bf16[2,2,2,96,1024]{4,3,2,1,0:T(8,128)(2,1)} %dynamic-slice_bitcast_fusion.5), channel_id=1, source_target_pairs={{0,2},{2,0},{4,6},{6,4},{8,10},{10,8},{12,14},{14,12},{16,18},{18,... | collective-permute-start | bytes 4718600 | tf_op jit(solution)/shard_map/ppermute | solution.py:68
  126.3 36.5 %collective-permute-start.1 = (bf16[2,2,2,96,1024]{4,3,2,1,0:T(8,128)(2,1)}, bf16[2,2,2,96,1024]{4,3,2,1,0:T(8,128)(2,1)}, u32[]{:S(2)}, u32[]{:S(2)}) collective-permute-start(bf16[2,2,2,96,1024]{4,3,2,1,0:T(8,128)(2,1)} %dynamic-slice_bitcast_fusion.4), channel_id=1, source_target_pairs={{0,4},{2,6},{4,0},{6,2},{8,12},{10,14},{12,8},{14,10},{16,20},{18,... | collective-permute-start | bytes 4718600 | tf_op jit(solution)/shard_map/ppermute | solution.py:68
  152.2 4.7 copy-start.14
  152.3 10.6 %copy-start.26 = (bf16[1536,1024]{1,0:T(8,128)(2,1)S(1)}, bf16[1536,1024]{1,0:T(8,128)(2,1)}, u32[]{:S(2)}) copy-start(bf16[1536,1024]{1,0:T(8,128)(2,1)} %convolution_convert_fusion.2) | copy-start | bytes 9437188
  152.3 10.6 %copy-start.27 = (bf16[1536,1024]{1,0:T(8,128)(2,1)S(1)}, bf16[1536,1024]{1,0:T(8,128)(2,1)}, u32[]{:S(2)}) copy-start(bf16[1536,1024]{1,0:T(8,128)(2,1)} %convolution_convert_fusion.3) | copy-start | bytes 9437188
  168.7 34.1 %collective-permute-start.2 = (bf16[2,2,96,1024]{3,2,1,0:T(8,128)(2,1)}, bf16[2,2,96,1024]{3,2,1,0:T(8,128)(2,1)S(1)}, u32[]{:S(2)}, u32[]{:S(2)}) collective-permute-start(bf16[2,2,96,1024]{3,2,1,0:T(8,128)(2,1)} %dynamic-slice_bitcast_fusion.16), channel_id=1, source_target_pairs={{0,4},{2,6},{4,0},{6,2},{8,12},{10,14},{12,8},{14,10},{16,20},{18,... | collective-permute-start | bytes 2359304 | tf_op jit(solution)/shard_map/ppermute | solution.py:68
  170.2 32.6 %collective-permute-start.3 = (bf16[2,2,96,1024]{3,2,1,0:T(8,128)(2,1)}, bf16[2,2,96,1024]{3,2,1,0:T(8,128)(2,1)}, u32[]{:S(2)}, u32[]{:S(2)}) collective-permute-start(bf16[2,2,96,1024]{3,2,1,0:T(8,128)(2,1)} %dynamic-slice_bitcast_fusion.15), channel_id=1, source_target_pairs={{0,2},{2,0},{4,6},{6,4},{8,10},{10,8},{12,14},{14,12},{16,18},{18,... | collective-permute-start | bytes 2359304 | tf_op jit(solution)/shard_map/ppermute | solution.py:68
  171.5 90.8 %collective-permute-start.5 = (bf16[2,2,2,96,2048]{4,3,2,1,0:T(8,128)(2,1)}, bf16[2,2,2,96,2048]{4,3,2,1,0:T(8,128)(2,1)}, u32[]{:S(2)}, u32[]{:S(2)}) collective-permute-start(bf16[2,2,2,96,2048]{4,3,2,1,0:T(8,128)(2,1)} %dynamic-slice_bitcast_fusion.1), channel_id=1, source_target_pairs={{0,2},{2,0},{4,6},{6,4},{8,10},{10,8},{12,14},{14,12},{16,18},{18,... | collective-permute-start | bytes 9437192 | tf_op jit(solution)/shard_map/ppermute | solution.py:68
  172.2 90.1 %collective-permute-start.6 = (bf16[2,2,2,96,2048]{4,3,2,1,0:T(8,128)(2,1)}, bf16[2,2,2,96,2048]{4,3,2,1,0:T(8,128)(2,1)}, u32[]{:S(2)}, u32[]{:S(2)}) collective-permute-start(bf16[2,2,2,96,2048]{4,3,2,1,0:T(8,128)(2,1)} %dynamic-slice_bitcast_fusion), channel_id=1, source_target_pairs={{0,4},{2,6},{4,0},{6,2},{8,12},{10,14},{12,8},{14,10},{16,20},{18,... | collective-permute-start | bytes 9437192 | tf_op jit(solution)/shard_map/ppermute | solution.py:68
  202.8 5.1 %copy-start.53 = (f32[1024,768]{1,0:T(8,128)S(1)}, f32[1024,768]{1,0:T(8,128)}, u32[]{:S(2)}) copy-start(f32[1024,768]{1,0:T(8,128)} %get-tuple-element.142) | copy-start | bytes 9437188
  204.4 3.5 copy-start.52
  208.0 6.0 %copy-start.3 = (bf16[1024,768]{1,0:T(8,128)(2,1)S(1)}, bf16[1024,768]{1,0:T(8,128)(2,1)}, u32[]{:S(2)}) copy-start(bf16[1024,768]{1,0:T(8,128)(2,1)} %copy-done.2) | copy-start | bytes 4718596
  208.0 6.0 %copy-start.54 = (bf16[1024,1536]{1,0:T(8,128)(2,1)S(1)}, bf16[1024,1536]{1,0:T(8,128)(2,1)}, u32[]{:S(2)}) copy-start(bf16[1024,1536]{1,0:T(8,128)(2,1)} %get-tuple-element.140) | copy-start | bytes 9437188
  214.0 3.3 copy-start.56
  223.7 38.6 %collective-permute-start.4 = (bf16[2,96,2048]{2,1,0:T(8,128)(2,1)}, bf16[2,96,2048]{2,1,0:T(8,128)(2,1)S(1)}, u32[]{:S(2)}, u32[]{:S(2)}) collective-permute-start(bf16[2,96,2048]{2,1,0:T(8,128)(2,1)} %pad_maximum_fusion.3), channel_id=1, source_target_pairs={{0,8},{2,10},{4,12},{6,14},{8,0},{10,2},{12,4},{14,6},{16,24},{18,... | collective-permute-start | bytes 2359304 | tf_op jit(solution)/shard_map/ppermute | solution.py:68
  225.2 88.1 %collective-permute-start.9 = (bf16[2,2,2,96,1536]{4,3,0,2,1:T(8,128)(2,1)}, bf16[2,2,2,96,1536]{4,3,0,2,1:T(8,128)(2,1)S(1)}, u32[]{:S(2)}, u32[]{:S(2)}) collective-permute-start(bf16[2,2,2,96,1536]{4,3,0,2,1:T(8,128)(2,1)} %pad_maximum_fusion), channel_id=1, source_target_pairs={{0,8},{2,10},{4,12},{6,14},{8,0},{10,2},{12,4},{14,6},{16,24},{18,... | collective-permute-start | bytes 7077896 | tf_op jit(solution)/shard_map/ppermute | solution.py:68
  260.0 19.2 %copy-start.5 = (bf16[1024,768]{1,0:T(8,128)(2,1)}, bf16[1024,768]{1,0:T(8,128)(2,1)S(1)}, u32[]{:S(2)}) copy-start(bf16[1024,768]{1,0:T(8,128)(2,1)S(1)} %get-tuple-element.161.key_ref) | copy-start | bytes 4718596
  260.0 29.6 %copy-start.4 = (bf16[1024,768]{1,0:T(8,128)(2,1)}, bf16[1024,768]{1,0:T(8,128)(2,1)S(1)}, u32[]{:S(2)}) copy-start(bf16[1024,768]{1,0:T(8,128)(2,1)S(1)} %get-tuple-element.173.query_ref) | copy-start | bytes 4718596
  260.0 75.3 %copy-start = (bf16[16,1024]{1,0:T(8,128)(2,1)}, bf16[16,1024]{1,0:T(8,128)(2,1)S(1)}, u32[]{:S(2)}) copy-start(bf16[16,1024]{1,0:T(8,128)(2,1)S(1)} %get-tuple-element.160.forget_ref) | copy-start | bytes 98308
  261.2 7.8 %slice-start = ((s8[6291456]{0:T(1024)(128)(4,1)}), s8[4194304]{0:T(1024)(128)(4,1)S(1)}, s32[]{:S(2)}) async-start(s8[6291456]{0:T(1024)(128)(4,1)} %bitcast.222), calls=%async_computation | async-start | bytes 8388608
  262.3 5.3 %copy-start.37 = (bf16[2,96,2048]{2,1,0:T(8,128)(2,1)}, bf16[2,96,2048]{2,1,0:T(8,128)(2,1)S(1)}, u32[]{:S(2)}) copy-start(bf16[2,96,2048]{2,1,0:T(8,128)(2,1)S(1)} %collective-permute-done.4) | copy-start | bytes 2359300
  262.3 6.7 %slice-start.1 = ((s8[6291456]{0:T(1024)(128)(4,1)}), s8[2097152]{0:T(1024)(128)(4,1)S(1)}, s32[]{:S(2)}) async-start(s8[6291456]{0:T(1024)(128)(4,1)} %bitcast.222), calls=%async_computation.1 | async-start | bytes 4194304
  267.6 4.8 copy-start.9
  274.9 4.3 copy-start.30
  282.1 5.2 %copy-start.33 = (bf16[1536,768]{1,0:T(8,128)(2,1)}, bf16[1536,768]{1,0:T(8,128)(2,1)S(1)}, u32[]{:S(2)}) copy-start(bf16[1536,768]{1,0:T(8,128)(2,1)S(1)} %convolution_convert_fusion.5) | copy-start | bytes 7077892
  282.1 36.2 %collective-permute-start.7 = (bf16[2,2,96,2048]{3,2,1,0:T(8,128)(2,1)}, bf16[2,2,96,2048]{3,2,1,0:T(8,128)(2,1)}, u32[]{:S(2)}, u32[]{:S(2)}) collective-permute-start(bf16[2,2,96,2048]{3,2,1,0:T(8,128)(2,1)} %dynamic-slice_bitcast_fusion.3), channel_id=1, source_target_pairs={{0,4},{2,6},{4,0},{6,2},{8,12},{10,14},{12,8},{14,10},{16,20},{18,... | collective-permute-start | bytes 4718600 | tf_op jit(solution)/shard_map/ppermute | solution.py:68
  283.7 35.9 %collective-permute-start.8 = (bf16[2,2,96,2048]{3,2,1,0:T(8,128)(2,1)}, bf16[2,2,96,2048]{3,2,1,0:T(8,128)(2,1)}, u32[]{:S(2)}, u32[]{:S(2)}) collective-permute-start(bf16[2,2,96,2048]{3,2,1,0:T(8,128)(2,1)} %dynamic-slice_bitcast_fusion.2), channel_id=1, source_target_pairs={{0,2},{2,0},{4,6},{6,4},{8,10},{10,8},{12,14},{14,12},{16,18},{18,... | collective-permute-start | bytes 4718600 | tf_op jit(solution)/shard_map/ppermute | solution.py:68
  295.0 41.5 %collective-permute-start.10 = (bf16[96,2048]{1,0:T(8,128)(2,1)S(1)}, bf16[96,2048]{1,0:T(8,128)(2,1)S(1)}, u32[]{:S(2)}, u32[]{:S(2)}) collective-permute-start(bf16[96,2048]{1,0:T(8,128)(2,1)S(1)} %dynamic-slice_bitcast_fusion.21), channel_id=1, source_target_pairs={{0,16},{2,18},{4,20},{6,22},{8,24},{10,26},{12,28},{14,30},{16,0},... | collective-permute-start | bytes 1179656 | tf_op jit(solution)/shard_map/ppermute | solution.py:68
  313.3 8.8 %copy-start.31 = (bf16[2,2,2,96,1536]{4,3,0,2,1:T(8,128)(2,1)}, bf16[2,2,2,96,1536]{4,3,0,2,1:T(8,128)(2,1)S(1)}, u32[]{:S(2)}) copy-start(bf16[2,2,2,96,1536]{4,3,0,2,1:T(8,128)(2,1)S(1)} %collective-permute-done.9) | copy-start | bytes 7077892
  330.4 2.8 copy-start.41
  330.4 3.5 copy-start.42
  331.5 66.7 %collective-permute-start.11 = (bf16[2,96,4096]{2,1,0:T(8,128)(2,1)}, bf16[2,96,4096]{2,1,0:T(8,128)(2,1)}, u32[]{:S(2)}, u32[]{:S(2)}) collective-permute-start(bf16[2,96,4096]{2,1,0:T(8,128)(2,1)} %pad_maximum_fusion.1), channel_id=1, source_target_pairs={{0,8},{2,10},{4,12},{6,14},{8,0},{10,2},{12,4},{14,6},{16,24},{18,... | collective-permute-start | bytes 4718600 | tf_op jit(solution)/shard_map/ppermute | solution.py:68
  333.9 64.3 %collective-permute-start.13 = (bf16[2,2,2,96,896]{4,3,2,1,0:T(8,128)(2,1)}, bf16[2,2,2,96,896]{4,3,2,1,0:T(8,128)(2,1)}, u32[]{:S(2)}, u32[]{:S(2)}) collective-permute-start(bf16[2,2,2,96,896]{4,3,2,1,0:T(8,128)(2,1)} %pad_maximum_fusion.2), channel_id=1, source_target_pairs={{0,2},{2,0},{4,6},{6,4},{8,10},{10,8},{12,14},{14,12},{16,18},{18,... | collective-permute-start | bytes 4128776 | tf_op jit(solution)/shard_map/ppermute | solution.py:68
  335.4 62.8 %collective-permute-start.14 = (bf16[2,2,2,96,768]{4,3,2,1,0:T(8,128)(2,1)}, bf16[2,2,2,96,768]{4,3,2,1,0:T(8,128)(2,1)}, u32[]{:S(2)}, u32[]{:S(2)}) collective-permute-start(bf16[2,2,2,96,768]{4,3,2,1,0:T(8,128)(2,1)} %dynamic-slice_bitcast_fusion.8), channel_id=1, source_target_pairs={{0,4},{2,6},{4,0},{6,2},{8,12},{10,14},{12,8},{14,10},{16,20},{18,... | collective-permute-start | bytes 3538952 | tf_op jit(solution)/shard_map/ppermute | solution.py:68
  336.0 62.2 %collective-permute-start.15 = (bf16[2,2,2,96,768]{4,3,0,2,1:T(8,128)(2,1)}, bf16[2,2,2,96,768]{4,3,0,2,1:T(8,128)(2,1)}, u32[]{:S(2)}, u32[]{:S(2)}) collective-permute-start(bf16[2,2,2,96,768]{4,3,0,2,1:T(8,128)(2,1)} %bitcast.239), channel_id=1, source_target_pairs={{0,8},{2,10},{4,12},{6,14},{8,0},{10,2},{12,4},{14,6},{16,24},{18,... | collective-permute-start | bytes 3538952 | tf_op jit(solution)/shard_map/ppermute | solution.py:68
  336.5 25.6 %copy-start.39 = (bf16[96,2048]{1,0:T(8,128)(2,1)}, bf16[96,2048]{1,0:T(8,128)(2,1)S(1)}, u32[]{:S(2)}) copy-start(bf16[96,2048]{1,0:T(8,128)(2,1)S(1)} %collective-permute-done.10) | copy-start | bytes 1179652
  336.6 61.7 %collective-permute-start.12 = (bf16[2,2,96,1536]{3,2,0,1:T(8,128)(2,1)}, bf16[2,2,96,1536]{3,2,0,1:T(8,128)(2,1)}, u32[]{:S(2)}, u32[]{:S(2)}) collective-permute-start(bf16[2,2,96,1536]{3,2,0,1:T(8,128)(2,1)} %dynamic-slice_bitcast_fusion.7), channel_id=1, source_target_pairs={{0,4},{2,6},{4,0},{6,2},{8,12},{10,14},{12,8},{14,10},{16,20},{18,... | collective-permute-start | bytes 3538952 | tf_op jit(solution)/shard_map/ppermute | solution.py:68
  398.3 3.0 copy-start.34
  401.3 2.9 copy-start.20
  406.9 2.7 copy-start.29
  412.5 35.8 %copy-start.16 = (bf16[2,2,2,96,896]{4,3,2,1,0:T(8,128)(2,1)S(1)}, bf16[2,2,2,96,896]{4,3,2,1,0:T(8,128)(2,1)}, u32[]{:S(2)}) copy-start(bf16[2,2,2,96,896]{4,3,2,1,0:T(8,128)(2,1)} %copy-done.15) | copy-start | bytes 4128772
  412.5 34.3 %collective-permute-start.16 = (bf16[96,4096]{1,0:T(8,128)(2,1)}, bf16[96,4096]{1,0:T(8,128)(2,1)}, u32[]{:S(2)}, u32[]{:S(2)}) collective-permute-start(bf16[96,4096]{1,0:T(8,128)(2,1)} %dynamic-slice_bitcast_fusion.10), channel_id=1, source_target_pairs={{0,16},{2,18},{4,20},{6,22},{8,24},{10,26},{12,28},{14,30},{16,0},... | collective-permute-start | bytes 2359304 | tf_op jit(solution)/shard_map/ppermute | solution.py:68
  412.9 27.4 %collective-permute-start.18 = (bf16[2,2,96,896]{3,2,1,0:T(8,128)(2,1)}, bf16[2,2,96,896]{3,2,1,0:T(8,128)(2,1)}, u32[]{:S(2)}, u32[]{:S(2)}) collective-permute-start(bf16[2,2,96,896]{3,2,1,0:T(8,128)(2,1)} %dynamic-slice_bitcast_fusion.17), channel_id=1, source_target_pairs={{0,4},{2,6},{4,0},{6,2},{8,12},{10,14},{12,8},{14,10},{16,20},{18,... | collective-permute-start | bytes 2064392 | tf_op jit(solution)/shard_map/ppermute | solution.py:68
  413.4 16.3 %collective-permute-start.17 = (bf16[2,96,1536]{2,1,0:T(8,128)(2,1)S(1)}, bf16[2,96,1536]{2,1,0:T(8,128)(2,1)}, u32[]{:S(2)}, u32[]{:S(2)}) collective-permute-start(bf16[2,96,1536]{2,1,0:T(8,128)(2,1)S(1)} %dynamic-slice_bitcast_fusion.20), channel_id=1, source_target_pairs={{0,2},{2,0},{4,6},{6,4},{8,10},{10,8},{12,14},{14,12},{16,18},{18,... | collective-permute-start | bytes 1769480 | tf_op jit(solution)/shard_map/ppermute | solution.py:68
  414.8 23.5 %collective-permute-start.19 = (bf16[2,2,96,768]{3,2,1,0:T(8,128)(2,1)}, bf16[2,2,96,768]{3,2,1,0:T(8,128)(2,1)}, u32[]{:S(2)}, u32[]{:S(2)}) collective-permute-start(bf16[2,2,96,768]{3,2,1,0:T(8,128)(2,1)} %dynamic-slice_bitcast_fusion.19), channel_id=1, source_target_pairs={{0,2},{2,0},{4,6},{6,4},{8,10},{10,8},{12,14},{14,12},{16,18},{18,... | collective-permute-start | bytes 1769480 | tf_op jit(solution)/shard_map/ppermute | solution.py:68
  415.4 24.8 %collective-permute-start.20 = (bf16[2,2,96,768]{3,2,0,1:T(8,128)(2,1)}, bf16[2,2,96,768]{3,2,0,1:T(8,128)(2,1)}, u32[]{:S(2)}, u32[]{:S(2)}) collective-permute-start(bf16[2,2,96,768]{3,2,0,1:T(8,128)(2,1)} %dynamic-slice_bitcast_fusion.18), channel_id=1, source_target_pairs={{0,4},{2,6},{4,0},{6,2},{8,12},{10,14},{12,8},{14,10},{16,20},{18,... | collective-permute-start | bytes 1769480 | tf_op jit(solution)/shard_map/ppermute | solution.py:68
  452.4 21.7 %collective-permute-start.22 = (bf16[2,96,1664]{2,1,0:T(8,128)(2,1)S(1)}, bf16[2,96,1664]{2,1,0:T(8,128)(2,1)S(1)}, u32[]{:S(2)}, u32[]{:S(2)}) collective-permute-start(bf16[2,96,1664]{2,1,0:T(8,128)(2,1)S(1)} %pad_maximum_fusion.4), channel_id=1, source_target_pairs={{0,8},{2,10},{4,12},{6,14},{8,0},{10,2},{12,4},{14,6},{16,24},{18,... | collective-permute-start | bytes 1916936 | tf_op jit(solution)/shard_map/ppermute | solution.py:68
  453.8 18.1 %collective-permute-start.21 = (bf16[96,1536]{1,0:T(8,128)(2,1)S(1)}, bf16[96,1536]{1,0:T(8,128)(2,1)S(1)}, u32[]{:S(2)}, u32[]{:S(2)}) collective-permute-start(bf16[96,1536]{1,0:T(8,128)(2,1)S(1)} %dynamic-slice_bitcast_fusion.32), channel_id=1, source_target_pairs={{0,16},{2,18},{4,20},{6,22},{8,24},{10,26},{12,28},{14,30},{16,0},... | collective-permute-start | bytes 884744 | tf_op jit(solution)/shard_map/ppermute | solution.py:68
  456.2 15.7 %collective-permute-start.23 = (bf16[2,96,768]{2,1,0:T(8,128)(2,1)S(1)}, bf16[2,96,768]{2,1,0:T(8,128)(2,1)S(1)}, u32[]{:S(2)}, u32[]{:S(2)}) collective-permute-start(bf16[2,96,768]{2,1,0:T(8,128)(2,1)S(1)} %dynamic-slice_bitcast_fusion.30), channel_id=1, source_target_pairs={{0,2},{2,0},{4,6},{6,4},{8,10},{10,8},{12,14},{14,12},{16,18},{18,... | collective-permute-start | bytes 884744 | tf_op jit(solution)/shard_map/ppermute | solution.py:68
  474.4 21.7 %collective-permute-start.24 = (bf16[96,1664]{1,0:T(8,128)(2,1)S(1)}, bf16[96,1664]{1,0:T(8,128)(2,1)S(1)}, u32[]{:S(2)}, u32[]{:S(2)}) collective-permute-start(bf16[96,1664]{1,0:T(8,128)(2,1)S(1)} %dynamic-slice_bitcast_fusion.28), channel_id=1, source_target_pairs={{0,16},{2,18},{4,20},{6,22},{8,24},{10,26},{12,28},{14,30},{16,0},... | collective-permute-start | bytes 958472 | tf_op jit(solution)/shard_map/ppermute | solution.py:68
  475.7 20.4 %collective-permute-start.25 = (bf16[96,768]{1,0:T(8,128)(2,1)S(1)}, bf16[96,768]{1,0:T(8,128)(2,1)S(1)}, u32[]{:S(2)}, u32[]{:S(2)}) collective-permute-start(bf16[96,768]{1,0:T(8,128)(2,1)S(1)} %dynamic-slice_bitcast_fusion.35), channel_id=1, source_target_pairs={{0,16},{2,18},{4,20},{6,22},{8,24},{10,26},{12,28},{14,30},{16,0},... | collective-permute-start | bytes 442376 | tf_op jit(solution)/shard_map/ppermute | solution.py:68
  496.2 7.9 %copy-start.25 = (f32[512,1536]{1,0:T(8,128)S(1)}, f32[512,1536]{1,0:T(8,128)}, u32[]{:S(2)}) copy-start(f32[512,1536]{1,0:T(8,128)} %get-tuple-element.312) | copy-start | bytes 9437188
  (22 other events, 43.4 us)
